TPU v7x, 512 devices: a whole 4x8x8 slice. The times are simulated.
512 devices in a mesh: row: 16 (over x_hi, z), col: 32 (over x_lo, y, core).
Axes of the slice: x: 4 (x_hi: 2, x_lo: 2; x = x_hi * 2 + x_lo), y: 8, z: 8, core: 2. Of those that a mesh axis runs over, the one named last changes fastest.
Arguments:
- slots: bfloat16 [3072, 128, 128], P(('row', 'col')), may hold values from -6 to 6
- block_list: int32 [3072], P(('row', 'col')), may hold values from -1 to 15, as said below
- metric: bfloat16 [8192, 4096], P('row', 'col'), may hold values from -0.125 to 0.125
Outputs:
- contracted: float32 [16384, 4096], P('row', 'col')
Inputs may be any that keep to these rules, and one draw needn't show every extreme that they name: `block_list`: the live entries of one device's 6 slots come first and name distinct blocks; -1 marks an unused slot; every device has at least 3 live slots and some device has all 6 live.
All inputs are finite; a program needn't handle non-finite values.
Results may differ from a plain program's by a relative error of at most 0.0003.
Values may be sent and summed in bfloat16 or wider, within the bound.
No kernel may reach another device: no remote copies, remote signals or barrier semaphores. Data moves between devices by JAX's collectives and lax.ppermute only.
A program may use at most 128 MiB of HBM per device.

v0:
```python
import jax
import jax.numpy as jnp
from jax import lax
from jax.sharding import PartitionSpec as P

BLK = 128
PAIR_DEV = 1024


def sent_to_all(shard, axis):
    copies = jnp.broadcast_to(shard, (lax.axis_size(axis), *shard.shape))
    return lax.all_to_all(copies, axis, split_axis=0, concat_axis=0, tiled=True)


def laid_out(tiles, dim):
    tiles = jnp.moveaxis(tiles, 0, dim)
    dims = tiles.shape
    return tiles.reshape(*dims[:dim], dims[dim] * dims[dim + 1], *dims[dim + 2 :])


def gathered_copies(shard, axis, dim):
    tiles = sent_to_all(shard, axis)
    return laid_out(tiles, dim)


def on_device(slots, block_list, metric):
    slot_count = block_list.shape[0]
    width = slots.shape[1]
    out_cols = metric.shape[1]
    metric_band = gathered_copies(metric, "row", 0)
    band_blocks = metric_band.shape[0] // width
    col_blocks = band_blocks // lax.axis_size("col")
    pair_blocks = PAIR_DEV // BLK
    metric_blocks = metric_band.reshape(band_blocks, width, out_cols)
    piece_slots = lax.all_gather(slots, "col", axis=0, tiled=True)
    piece_list = lax.all_gather(block_list, "col", axis=0, tiled=True)
    number = piece_list.shape[0]
    shard_of = jnp.arange(number, dtype=jnp.int32) // slot_count
    is_live = piece_list >= 0
    clipped = jnp.maximum(piece_list, 0)
    pair_block = clipped // col_blocks
    global_block = shard_of * col_blocks + clipped % col_blocks
    rows = metric_blocks[global_block]
    prod = jnp.einsum("sab,sbq->saq", piece_slots, rows, preferred_element_type=jnp.float32)
    placing = ((pair_block[:, None] == jnp.arange(pair_blocks)[None, :]) & is_live[:, None]).astype(
        jnp.float32
    )
    added = jnp.einsum("sp,saq->paq", placing, prod, precision=lax.Precision.HIGHEST)
    return added.reshape(pair_blocks * width, out_cols)


def solution(mesh):
    return jax.shard_map(
        on_device,
        mesh=mesh,
        in_specs=(P(("row", "col"), None, None), P(("row", "col")), P("row", "col")),
        out_specs=P("row", "col"),
        check_vma=False,
    )
```

profile of v0, /device:TPU:133, one launch (start us, length us, event | category | flops | bytes accessed | tf_op | source)
XLA Modules:
  0.0 136.9 jit_solution(17358989224031301215)
XLA Ops:
  6.5 0.0 copy-start
  6.5 0.0 all-gather.2.cloned.1.call-start
  6.5 0.7 all-gather.2.cloned.1.call-update
  7.3 2.6 %broadcast_in_dim.4 = bf16[16,512,128]{2,1,0:T(8,128)(2,1)} broadcast(bf16[512,128]{1,0:T(8,128)(2,1)} %param.5), dimensions={1,2} | broadcast | bytes 2228224 | tf_op jit(solution)/shard_map/broadcast_in_dim | solution.py:11
  9.9 10.9 %all-to-all-start = ((bf16[16,512,128]{2,1,0:T(8,128)(2,1)}), bf16[16,512,128]{2,1,0:T(8,128)(2,1)S(1)}, u32[]{:S(2)}, u32[]{:S(2)}) async-start(bf16[16,512,128]{2,1,0:T(8,128)(2,1)} %broadcast_in_dim.4), calls=%async_computation | async-start | bytes 4194304 | tf_op jit(solution)/shard_map/all_to_all | solution.py:12
  20.8 1.3 dynamic-slice
  22.7 0.0 copy-done
  22.8 0.2 dynamic-update-slice
  23.0 14.8 %all-reduce = s32[192]{0:T(256)S(1)} all-reduce(s32[192]{0:T(256)S(1)} %dynamic-update-slice), channel_id=1, replica_groups=mesh['row'=16,'col'=32] {'col'}, use_global_device_ids=true, to_apply=%add | all-reduce | flops 192 | bytes 1536
  37.8 29.6 %all-to-all-done = bf16[16,512,128]{2,1,0:T(8,128)(2,1)S(1)} async-done(((bf16[16,512,128]{2,1,0:T(8,128)(2,1)}), bf16[16,512,128]{2,1,0:T(8,128)(2,1)S(1)}, u32[]{:S(2)}, u32[]{:S(2)}) %all-to-all-start) | async-done | bytes 2097184 | tf_op jit(solution)/shard_map/all_to_all | solution.py:12
  67.5 8.1 %gather_fusion = bf16[192,128,128]{2,1,0:T(8,128)(2,1)} fusion(bf16[64,128,128]{2,1,0:T(8,128)(2,1)S(1)} %bitcast.11, s32[1024]{0:T(1024)S(1)} %pad_clamp_fusion), kind=kCustom, calls=%fused_computation | custom fusion | bytes 12583680 | tf_op jit(solution)/shard_map/gather | solution.py:43
  75.5 20.3 %all-gather.2.cloned.1.call-done = bf16[192,128,128]{2,1,0:T(8,128)(2,1)} async-done(((bf16[6,128,128]{2,1,0:T(8,128)(2,1)}), bf16[192,128,128]{2,1,0:T(8,128)(2,1)}) %all-gather.2.cloned.1.call-update) | async-done | bytes 6291472 | tf_op jit(solution)/shard_map/all_gather | solution.py:35
  95.8 13.7 %convolution_bitcast_fusion = f32[192,128,128]{1,2,0:T(8,128)} fusion(bf16[192,128,128]{2,1,0:T(8,128)(2,1)} %gather_fusion, bf16[192,128,128]{2,1,0:T(8,128)(2,1)} %all-gather.2.cloned.1.call-done), kind=kOutput, calls=%fused_computation.1 | convolution fusion | flops 805306368 | bytes 25165824 | tf_op jit(solution)/shard_map/sab,sbq->saq/dot_general | solution.py:44
  109.5 12.7 %copy.8 = f32[192,128,128]{2,0,1:T(8,128)} copy(f32[192,128,128]{1,2,0:T(8,128)} %convolution_bitcast_fusion) | data formatting | bytes 25165824 | tf_op jit(solution)/shard_map/sab,sbq->saq/dot_general | solution.py:44
  122.3 6.9 %fusion.2 = f32[8,128,128]{2,0,1:T(8,128)S(1)} fusion(f32[192,128,128]{2,0,1:T(8,128)} %copy.8, s32[192]{0:T(256)S(1)} %get-tuple-element.5, pred[192]{0:T(512)(128)(4,1)S(1)} %broadcast_compare_fusion), kind=kOutput, calls=%fused_computation.5 | convolution fusion | flops 301992960 | bytes 13108160 | tf_op jit(solution)/shard_map/sp,saq->paq/dot_general | solution.py:48
  129.2 0.9 copy.9
  (4 shorter events, 0.0 us)
Async XLA Ops:
  6.5 16.2 %copy-start = (s32[6]{0:T(128)S(1)}, s32[6]{0:T(128)}, u32[]{:S(2)}) copy-start(s32[6]{0:T(128)} %param.4) | copy-start | bytes 76
  6.5 89.3 %all-gather.2.cloned.1.call-start = ((), (), s32[]{:S(2)}) async-start(), calls=%async_computation.1 | async-start | bytes 6488064 | tf_op jit(solution)/shard_map/all_gather | solution.py:35
  9.9 57.6 %all-to-all-start = ((bf16[16,512,128]{2,1,0:T(8,128)(2,1)}), bf16[16,512,128]{2,1,0:T(8,128)(2,1)S(1)}, u32[]{:S(2)}, u32[]{:S(2)}) async-start(bf16[16,512,128]{2,1,0:T(8,128)(2,1)} %broadcast_in_dim.4), calls=%async_computation | async-start | bytes 4194304 | tf_op jit(solution)/shard_map/all_to_all | solution.py:12
Sparse Core Ops, SparseCore 0:
  9.5 86.3 all-gather.1
where the time goes:
time: 137 us
  waiting for transfers between devices  50.7 us (37%)
  local copies, waits for them, and re-layouts  25.8 us (19%)
  matrix products  20.6 us (15%)
  blocking collectives  14.8 us (11%)
  between operations  14.1 us (10%)
  starting transfers between devices  10.9 us (8%)
    all_to_all x1, waiting for transfers between devices, sent_to_all(): return lax.all_to_all(copies, axis, split_axis=0, concat_axis=0, tiled=True)  29.6 us
    all_gather x1, waiting for transfers between devices, on_device(): piece_slots = lax.all_gather(slots, 'col', axis=0, tiled=True)  20.3 us
    unnamed x1, blocking collectives  14.8 us
    dot_general x1, matrix products, on_device(): jnp.einsum('sab,sbq->saq', piece_slots, rows, preferred_element_type=jnp....  13.7 us
    dot_general x1, local copies, waits for them, and re-layouts, on_device(): jnp.einsum('sab,sbq->saq', piece_slots, rows, preferred_element_type=jnp....  12.7 us
    all_to_all x1, starting transfers between devices, sent_to_all(): return lax.all_to_all(copies, axis, split_axis=0, concat_axis=0, tiled=True)  10.9 us
    gather x1, local copies, waits for them, and re-layouts, on_device(): rows = metric_blocks[global_block]  8.05 us
    dot_general x1, matrix products, on_device(): jnp.einsum('sp,saq->paq', placing, prod, precision=lax.Precision.HIGHEST)  6.92 us
  transfers between devices with their start and end apart: 2, of which 2 were waited for; matrix products, arithmetic and copies ran while one was open for 9% of the time, Pallas kernels for 0%

commit v1 on v0

v1 whole, which is shorter than its diff:
```python
import jax
import jax.numpy as jnp
from jax import lax
from jax.experimental import pallas as pl
from jax.experimental.pallas import tpu as pltpu
from jax.sharding import PartitionSpec as P

BLK = 128
PAIR_DEV = 1024
PAIR_BLOCKS = PAIR_DEV // BLK
KMAX = 6
NY = 8
LIST_ROWS = 16
SLOT_ROWS = KMAX * BLK
P_LANE = 8


def col_of(x, y, core):
    return ((x % 2) * NY + y % NY) * 2 + core % 2


def col_perm(target):
    return [
        (col_of(x, y, c), col_of(*target(x, y, c)))
        for x in range(2)
        for y in range(NY)
        for c in range(2)
    ]


CORE = col_perm(lambda x, y, c: (x, y, c + 1))
X_PARTNER = col_perm(lambda x, y, c: (x + 1, y, c))
RING = col_perm(lambda x, y, c: (x, y + 1 if c == 0 else y - 1, c))


def sent(value, perm, axis="col"):
    return lax.ppermute(value, axis, perm)


def payload(slots, block_list, col_blocks):
    me = lax.axis_index("col")
    clipped = jnp.maximum(block_list, 0)
    band_block = me * col_blocks + clipped % col_blocks
    pair_block = jnp.where(block_list >= 0, clipped // col_blocks, PAIR_BLOCKS)
    row = jnp.concatenate(
        [
            jnp.pad(band_block, (0, P_LANE - KMAX)),
            jnp.pad(pair_block, (0, BLK - P_LANE - KMAX)),
        ]
    )
    rows = jnp.broadcast_to(row.astype(jnp.bfloat16), (LIST_ROWS, BLK))
    return jnp.concatenate([slots.reshape(SLOT_ROWS, BLK), rows])[None]


def add_products(metric_ref, piece_refs, total, metric_v, pieces_v, rows_v, list_v, list_s, sems, prepare):
    starts = [sum(ref.shape[0] for ref in piece_refs[:n]) for n in range(len(piece_refs))]
    places = [pl.ds(start, ref.shape[0]) for start, ref in zip(starts, piece_refs)]
    list_rows = [
        pltpu.make_async_copy(ref.at[:, SLOT_ROWS:, :], rows_v.at[place], sems.at[0, n])
        for n, (ref, place) in enumerate(zip(piece_refs, places))
    ]
    metric_copy = pltpu.make_async_copy(metric_ref, metric_v, sems.at[1, len(piece_refs)])
    piece_copies = [
        pltpu.make_async_copy(ref.at[:, :SLOT_ROWS, :], pieces_v.at[place], sems.at[1, n])
        for n, (ref, place) in enumerate(zip(piece_refs, places))
    ]
    for copy in (*list_rows, metric_copy, *piece_copies):
        copy.start()
    prepare()
    for copy in list_rows:
        copy.wait()
    for i in range(rows_v.shape[0]):
        rows = rows_v[i].astype(jnp.float32)
        list_v[i : i + 1, :] = rows[:1].astype(jnp.int32)
    list_copy = pltpu.make_async_copy(list_v, list_s, sems.at[0, len(piece_refs)])
    list_copy.start()
    list_copy.wait()
    metric_copy.wait()

    def one_piece(i, carry):
        for j in range(KMAX):
            band_block = list_s[i, j]
            pair_block = list_s[i, P_LANE + j]
            prod = jnp.dot(
                pieces_v[i, j * BLK : (j + 1) * BLK, :],
                metric_v[band_block],
                preferred_element_type=jnp.float32,
            )
            total[pair_block] += prod
        return carry

    for copy, start, ref in zip(piece_copies, starts, piece_refs):
        copy.wait()
        lax.fori_loop(start, start + ref.shape[0], one_piece, 0)


def early_products(metric_ref, *refs):
    *piece_refs, total, metric_v, pieces_v, rows_v, list_v, list_s, sems = refs

    def clear():
        total[...] = jnp.zeros_like(total)

    add_products(metric_ref, piece_refs, total, metric_v, pieces_v, rows_v, list_v, list_s, sems, clear)


def late_products(early_ref, metric_ref, *refs):
    *piece_refs, out_ref, total, metric_v, pieces_v, rows_v, list_v, list_s, sems = refs

    def take():
        total[...] = early_ref[...]

    add_products(metric_ref, piece_refs, total, metric_v, pieces_v, rows_v, list_v, list_s, sems, take)
    for p in range(PAIR_BLOCKS):
        out_ref[p * BLK : (p + 1) * BLK, :] = total[p]


def kernel_call(body, out_shape, taken, metric, pieces, scratch):
    vmem = pl.BlockSpec(memory_space=pltpu.VMEM)
    count = sum(piece.shape[0] for piece in pieces)
    return pl.pallas_call(
        body,
        out_shape=out_shape,
        in_specs=[vmem] * len(taken) + [pl.BlockSpec(memory_space=pltpu.HBM)] * (1 + len(pieces)),
        out_specs=vmem,
        scratch_shapes=[
            *scratch,
            pltpu.VMEM(metric.shape, metric.dtype),
            pltpu.VMEM((count, SLOT_ROWS, BLK), metric.dtype),
            pltpu.VMEM((count, LIST_ROWS, BLK), metric.dtype),
            pltpu.VMEM((count, BLK), jnp.int32),
            pltpu.SMEM((count, BLK), jnp.int32),
            pltpu.SemaphoreType.DMA((2, len(pieces) + 1)),
        ],
        compiler_params=pltpu.CompilerParams(vmem_limit_bytes=60 << 20),
    )(*taken, metric, *pieces)


def on_device(slots, block_list, metric):
    out_cols = metric.shape[1]
    rows = lax.axis_size("row")
    band_blocks = rows * metric.shape[0] // BLK
    col_blocks = band_blocks // lax.axis_size("col")
    copies = jnp.broadcast_to(metric, (rows, *metric.shape))
    band = lax.all_to_all(copies, "row", split_axis=0, concat_axis=0, tiled=True)
    band = band.reshape(band_blocks, BLK, out_cols)

    own = payload(slots, block_list, col_blocks)
    own_x = sent(own, X_PARTNER)
    near = jnp.concatenate([own, sent(own, CORE)])
    near_x = jnp.concatenate([own_x, sent(own_x, CORE)])
    a1 = sent(near, RING)
    b1 = sent(near_x, RING)
    a2 = sent(a1, RING)
    b2 = sent(b1, RING)
    a3 = sent(a2, RING)
    a4 = sent(a3[:1], RING)
    early = [a1, b1, a2, b2, a3]
    late = [sent(a3, X_PARTNER), a4, sent(a4, X_PARTNER)]
    early_other = sent(jnp.concatenate(early), CORE)
    late_other = sent(jnp.concatenate(late), CORE)
    early = [near, near_x, *early, early_other]
    late = [*late, late_other]
    total_shape = (PAIR_BLOCKS + 1, BLK, out_cols)
    total = kernel_call(
        early_products, jax.ShapeDtypeStruct(total_shape, jnp.float32), [], band, early, []
    )
    return kernel_call(
        late_products,
        jax.ShapeDtypeStruct((PAIR_DEV, out_cols), jnp.float32),
        [total],
        band,
        late,
        [pltpu.VMEM(total_shape, jnp.float32)],
    )


def solution(mesh):
    return jax.shard_map(
        on_device,
        mesh=mesh,
        in_specs=(P(("row", "col"), None, None), P(("row", "col")), P("row", "col")),
        out_specs=P("row", "col"),
        check_vma=False,
    )
```

time: 137 us -> 103 us (0.75)
  the two profiles are of different devices: /device:TPU:133 before, /device:TPU:1 now
where the time goes in v1:
time: 103 us
  starting transfers between devices  59 us (57%)
  waiting for transfers between devices  24.6 us (24%)
  Pallas kernels  13.2 us (13%)
  local copies, waits for them, and re-layouts  4.33 us (4%)
  other arithmetic  1.16 us (1%)
    ppermute x13, starting transfers between devices, sent(): return lax.ppermute(value, axis, perm)  45.4 us
    ppermute x13, waiting for transfers between devices, sent(): return lax.ppermute(value, axis, perm)  24.6 us
    all_to_all x1, starting transfers between devices, on_device(): lax.all_to_all(copies, 'row', split_axis=0, concat_axis=0, tiled=True)  13.5 us
    pallas_call x2, Pallas kernels, kernel_call(): pl.pallas_call(body, out_shape=out_shape, in_specs=[vmem] * len(taken) +...  13.2 us
    broadcast_in_dim x1, local copies, waits for them, and re-layouts, on_device(): copies = jnp.broadcast_to(metric, (rows, *metric.shape))  2.65 us
  transfers between devices with their start and end apart: 14, of which 7 were waited for; matrix products, arithmetic and copies ran while one was open for 1% of the time, Pallas kernels for 8%

profile of v1, /device:TPU:1, one launch (start us, length us, event | category | flops | bytes accessed | tf_op | source)
XLA Modules:
  0.0 102.6 jit_solution(13449861928909111944)
XLA Ops:
  0.0 2.7 %broadcast_in_dim.13 = bf16[16,512,128]{2,1,0:T(8,128)(2,1)} broadcast(bf16[512,128]{1,0:T(8,128)(2,1)} %param.5), dimensions={1,2} | broadcast | bytes 2228224 | tf_op jit(solution)/shard_map/broadcast_in_dim | solution.py:143
  2.7 13.5 %all-to-all-start = ((bf16[16,512,128]{2,1,0:T(8,128)(2,1)}), bf16[16,512,128]{2,1,0:T(8,128)(2,1)S(1)}, u32[]{:S(2)}, u32[]{:S(2)}) async-start(bf16[16,512,128]{2,1,0:T(8,128)(2,1)} %broadcast_in_dim.13), calls=%async_computation | async-start | bytes 4194304 | tf_op jit(solution)/shard_map/all_to_all | solution.py:144
  16.2 0.0 copy-done.12
  16.2 0.1 fusion.3
  16.3 0.0 copy-done.11
  16.4 2.9 %collective-permute-start = (bf16[1,784,128]{2,1,0:T(8,128)(2,1)S(1)}, bf16[1,784,128]{2,1,0:T(8,128)(2,1)S(1)}, u32[]{:S(2)}, u32[]{:S(2)}) collective-permute-start(bf16[1,784,128]{2,1,0:T(8,128)(2,1)S(1)} %maximum_bitcast_fusion), channel_id=1, source_target_pairs={{0,1},{1,0},{2,3},{3,2},{4,5},{5,4},{6,7},{7,6},{8,9},{9,8},{10,11... | collective-permute-start | bytes 602120 | tf_op jit(solution)/shard_map/ppermute | solution.py:37
  19.2 2.2 %collective-permute-start.1 = (bf16[1,784,128]{2,1,0:T(8,128)(2,1)S(1)}, bf16[1,784,128]{2,1,0:T(8,128)(2,1)S(1)}, u32[]{:S(2)}, u32[]{:S(2)}) collective-permute-start(bf16[1,784,128]{2,1,0:T(8,128)(2,1)S(1)} %maximum_bitcast_fusion), channel_id=1, source_target_pairs={{0,16},{1,17},{2,18},{3,19},{4,20},{5,21},{6,22},{7,23},{8,24},{9,... | collective-permute-start | bytes 602120 | tf_op jit(solution)/shard_map/ppermute | solution.py:37
  21.5 0.0 collective-permute-done
  21.5 0.0 copy-start.2
  21.5 5.1 %collective-permute-start.3 = (bf16[2,784,128]{2,1,0:T(8,128)(2,1)S(1)}, bf16[2,784,128]{2,1,0:T(8,128)(2,1)S(1)}, u32[]{:S(2)}, u32[]{:S(2)}) collective-permute-start(bf16[2,784,128]{2,1,0:T(8,128)(2,1)S(1)} %pad_maximum_fusion.1.refs_0_), channel_id=1, source_target_pairs={{0,2},{1,15},{2,4},{3,1},{4,6},{5,3},{6,8},{7,5},{8,10},{9,7},{10,... | collective-permute-start | bytes 1204232 | tf_op jit(solution)/shard_map/ppermute | solution.py:37
  26.6 6.2 %collective-permute-done.1 = bf16[1,784,128]{2,1,0:T(8,128)(2,1)S(1)} collective-permute-done((bf16[1,784,128]{2,1,0:T(8,128)(2,1)S(1)}, bf16[1,784,128]{2,1,0:T(8,128)(2,1)S(1)}, u32[]{:S(2)}, u32[]{:S(2)}) %collective-permute-start.1) | collective-permute-done | bytes 200736 | tf_op jit(solution)/shard_map/ppermute | solution.py:37
  32.8 2.3 %collective-permute-start.2 = (bf16[1,784,128]{2,1,0:T(8,128)(2,1)S(1)}, bf16[1,784,128]{2,1,0:T(8,128)(2,1)S(1)}, u32[]{:S(2)}, u32[]{:S(2)}) collective-permute-start(bf16[1,784,128]{2,1,0:T(8,128)(2,1)S(1)} %collective-permute-done.1), channel_id=1, source_target_pairs={{0,1},{1,0},{2,3},{3,2},{4,5},{5,4},{6,7},{7,6},{8,9},{9,8},{10,11... | collective-permute-start | bytes 602120 | tf_op jit(solution)/shard_map/ppermute | solution.py:37
  35.2 1.0 %collective-permute-done.2 = bf16[1,784,128]{2,1,0:T(8,128)(2,1)S(1)} collective-permute-done((bf16[1,784,128]{2,1,0:T(8,128)(2,1)S(1)}, bf16[1,784,128]{2,1,0:T(8,128)(2,1)S(1)}, u32[]{:S(2)}, u32[]{:S(2)}) %collective-permute-start.2) | collective-permute-done | bytes 200736 | tf_op jit(solution)/shard_map/ppermute | solution.py:37
  36.3 0.0 copy-start.8
  36.3 5.1 %collective-permute-start.4 = (bf16[2,784,128]{2,1,0:T(8,128)(2,1)S(1)}, bf16[2,784,128]{2,1,0:T(8,128)(2,1)S(1)}, u32[]{:S(2)}, u32[]{:S(2)}) collective-permute-start(bf16[2,784,128]{2,1,0:T(8,128)(2,1)S(1)} %constant_dynamic-update-slice_fusion.refs_1_), channel_id=1, source_target_pairs={{0,2},{1,15},{2,4},{3,1},{4,6},{5,3},{6,8},{7,5},{8,10},{9,7},{10,... | collective-permute-start | bytes 1204232 | tf_op jit(solution)/shard_map/ppermute | solution.py:37
  41.4 0.0 collective-permute-done.3.refs_2_
  41.4 0.0 copy-start.3
  41.4 3.0 %collective-permute-start.5 = (bf16[2,784,128]{2,1,0:T(8,128)(2,1)S(1)}, bf16[2,784,128]{2,1,0:T(8,128)(2,1)S(1)}, u32[]{:S(2)}, u32[]{:S(2)}) collective-permute-start(bf16[2,784,128]{2,1,0:T(8,128)(2,1)S(1)} %collective-permute-done.3.refs_2_), channel_id=1, source_target_pairs={{0,2},{1,15},{2,4},{3,1},{4,6},{5,3},{6,8},{7,5},{8,10},{9,7},{10,... | collective-permute-start | bytes 1204232 | tf_op jit(solution)/shard_map/ppermute | solution.py:37
  44.4 1.8 %collective-permute-done.4.refs_3_ = bf16[2,784,128]{2,1,0:T(8,128)(2,1)S(1)} collective-permute-done((bf16[2,784,128]{2,1,0:T(8,128)(2,1)S(1)}, bf16[2,784,128]{2,1,0:T(8,128)(2,1)S(1)}, u32[]{:S(2)}, u32[]{:S(2)}) %collective-permute-start.4) | collective-permute-done | bytes 401440 | tf_op jit(solution)/shard_map/ppermute | solution.py:37
  46.2 5.0 %collective-permute-start.6 = (bf16[2,784,128]{2,1,0:T(8,128)(2,1)S(1)}, bf16[2,784,128]{2,1,0:T(8,128)(2,1)S(1)}, u32[]{:S(2)}, u32[]{:S(2)}) collective-permute-start(bf16[2,784,128]{2,1,0:T(8,128)(2,1)S(1)} %collective-permute-done.4.refs_3_), channel_id=1, source_target_pairs={{0,2},{1,15},{2,4},{3,1},{4,6},{5,3},{6,8},{7,5},{8,10},{9,7},{10,... | collective-permute-start | bytes 1204232 | tf_op jit(solution)/shard_map/ppermute | solution.py:37
  51.2 0.0 collective-permute-done.5.refs_4_
  51.2 4.6 %collective-permute-start.7 = (bf16[2,784,128]{2,1,0:T(8,128)(2,1)S(1)}, bf16[2,784,128]{2,1,0:T(8,128)(2,1)S(1)}, u32[]{:S(2)}, u32[]{:S(2)}) collective-permute-start(bf16[2,784,128]{2,1,0:T(8,128)(2,1)S(1)} %collective-permute-done.5.refs_4_), channel_id=1, source_target_pairs={{0,2},{1,15},{2,4},{3,1},{4,6},{5,3},{6,8},{7,5},{8,10},{9,7},{10,... | collective-permute-start | bytes 1204232 | tf_op jit(solution)/shard_map/ppermute | solution.py:37
  55.8 0.1 constant_dynamic-update-slice_fusion.5
  55.9 0.1 constant_dynamic-update-slice_fusion.4
  55.9 0.0 collective-permute-done.6.refs_5_
  56.0 0.1 constant_dynamic-update-slice_fusion.3
  56.0 4.5 %collective-permute-done.7.refs_6_ = bf16[2,784,128]{2,1,0:T(8,128)(2,1)S(1)} collective-permute-done((bf16[2,784,128]{2,1,0:T(8,128)(2,1)S(1)}, bf16[2,784,128]{2,1,0:T(8,128)(2,1)S(1)}, u32[]{:S(2)}, u32[]{:S(2)}) %collective-permute-start.7) | collective-permute-done | bytes 401440 | tf_op jit(solution)/shard_map/ppermute | solution.py:37
  60.6 0.1 constant_dynamic-update-slice_fusion.2
  60.6 4.5 %collective-permute-start.8 = (bf16[10,784,128]{2,1,0:T(8,128)(2,1)S(1)}, bf16[10,784,128]{2,1,0:T(8,128)(2,1)}, u32[]{:S(2)}, u32[]{:S(2)}) collective-permute-start(bf16[10,784,128]{2,1,0:T(8,128)(2,1)S(1)} %constant_dynamic-update-slice_fusion.2), channel_id=1, source_target_pairs={{0,1},{1,0},{2,3},{3,2},{4,5},{5,4},{6,7},{7,6},{8,9},{9,8},{10,11... | collective-permute-start | bytes 6021128 | tf_op jit(solution)/shard_map/ppermute | solution.py:37
  65.1 2.8 %collective-permute-start.10 = (bf16[1,784,128]{2,1,0:T(8,128)(2,1)S(1)}, bf16[1,784,128]{2,1,0:T(8,128)(2,1)S(1)}, u32[]{:S(2)}, u32[]{:S(2)}) collective-permute-start(bf16[1,784,128]{2,1,0:T(8,128)(2,1)S(1)} %slice.4), channel_id=1, source_target_pairs={{0,2},{1,15},{2,4},{3,1},{4,6},{5,3},{6,8},{7,5},{8,10},{9,7},{10,... | collective-permute-start | bytes 602120 | tf_op jit(solution)/shard_map/ppermute | solution.py:37
  67.9 2.9 %collective-permute-start.9 = (bf16[2,784,128]{2,1,0:T(8,128)(2,1)S(1)}, bf16[2,784,128]{2,1,0:T(8,128)(2,1)S(1)}, u32[]{:S(2)}, u32[]{:S(2)}) collective-permute-start(bf16[2,784,128]{2,1,0:T(8,128)(2,1)S(1)} %collective-permute-done.7.refs_6_), channel_id=1, source_target_pairs={{0,16},{1,17},{2,18},{3,19},{4,20},{5,21},{6,22},{7,23},{8,24},{9,... | collective-permute-start | bytes 1204232 | tf_op jit(solution)/shard_map/ppermute | solution.py:37
  70.8 1.0 %collective-permute-done.10.refs_1_ = bf16[1,784,128]{2,1,0:T(8,128)(2,1)S(1)} collective-permute-done((bf16[1,784,128]{2,1,0:T(8,128)(2,1)S(1)}, bf16[1,784,128]{2,1,0:T(8,128)(2,1)S(1)}, u32[]{:S(2)}, u32[]{:S(2)}) %collective-permute-start.10) | collective-permute-done | bytes 200736 | tf_op jit(solution)/shard_map/ppermute | solution.py:37
  71.9 2.9 %collective-permute-start.11 = (bf16[1,784,128]{2,1,0:T(8,128)(2,1)S(1)}, bf16[1,784,128]{2,1,0:T(8,128)(2,1)S(1)}, u32[]{:S(2)}, u32[]{:S(2)}) collective-permute-start(bf16[1,784,128]{2,1,0:T(8,128)(2,1)S(1)} %collective-permute-done.10.refs_1_), channel_id=1, source_target_pairs={{0,16},{1,17},{2,18},{3,19},{4,20},{5,21},{6,22},{7,23},{8,24},{9,... | collective-permute-start | bytes 602120 | tf_op jit(solution)/shard_map/ppermute | solution.py:37
  74.8 6.3 %collective-permute-done.9.refs_0_ = bf16[2,784,128]{2,1,0:T(8,128)(2,1)S(1)} collective-permute-done((bf16[2,784,128]{2,1,0:T(8,128)(2,1)S(1)}, bf16[2,784,128]{2,1,0:T(8,128)(2,1)S(1)}, u32[]{:S(2)}, u32[]{:S(2)}) %collective-permute-start.9) | collective-permute-done | bytes 401440 | tf_op jit(solution)/shard_map/ppermute | solution.py:37
  81.1 3.6 %collective-permute-done.11.refs_2_ = bf16[1,784,128]{2,1,0:T(8,128)(2,1)S(1)} collective-permute-done((bf16[1,784,128]{2,1,0:T(8,128)(2,1)S(1)}, bf16[1,784,128]{2,1,0:T(8,128)(2,1)S(1)}, u32[]{:S(2)}, u32[]{:S(2)}) %collective-permute-start.11) | collective-permute-done | bytes 200736 | tf_op jit(solution)/shard_map/ppermute | solution.py:37
  84.8 1.0 pad_maximum_fusion
  85.8 2.2 %collective-permute-start.12 = (bf16[4,784,128]{2,1,0:T(8,128)(2,1)}, bf16[4,784,128]{2,1,0:T(8,128)(2,1)}, u32[]{:S(2)}, u32[]{:S(2)}) collective-permute-start(bf16[4,784,128]{2,1,0:T(8,128)(2,1)} %pad_maximum_fusion), channel_id=1, source_target_pairs={{0,1},{1,0},{2,3},{3,2},{4,5},{5,4},{6,7},{7,6},{8,9},{9,8},{10,11... | collective-permute-start | bytes 2408456 | tf_op jit(solution)/shard_map/ppermute | solution.py:37
  88.0 0.0 collective-permute-done.8.refs_7_
  88.0 0.0 all-to-all-done
  88.0 0.0 copy-start
  88.0 0.0 copy-done.1
  88.0 1.3 %copy-done = bf16[16,512,128]{2,1,0:T(8,128)(2,1)} copy-done((bf16[16,512,128]{2,1,0:T(8,128)(2,1)}, bf16[16,512,128]{2,1,0:T(8,128)(2,1)S(1)}, u32[]{:S(2)}) %copy-start) | copy-done | bytes 2097176
  89.3 7.9 %shard_map.37.early_ref = f32[9,128,128]{2,1,0:T(8,128)} custom-call(bf16[64,128,128]{2,1,0:T(8,128)(2,1)} %bitcast.4, bf16[2,784,128]{2,1,0:T(8,128)(2,1)} %copy-done.2, bf16[2,784,128]{2,1,0:T(8,128)(2,1)} %copy-done.8, bf16[2,784,128]{2,1,0:T(8,128)(2,1)} %copy-done.3, bf16[2,784,128]{2,1,0:T(8,128)(2,1)} %copy-done.4, bf16[2,784,128]{2,1,0:T(8,128)(2,1)} %copy-done.5, ...), custom_call_target="tpu_custom_call" | custom-call | tf_op jit(solution)/shard_map/pallas_call | solution.py:120
  97.2 0.0 copy-done.9
  97.2 0.0 copy-done.7
  97.2 0.0 copy-done.10
  97.3 0.0 collective-permute-done.12.refs_3_
  97.3 5.3 %shard_map.38 = f32[1024,128]{1,0:T(8,128)} custom-call(f32[9,128,128]{2,1,0:T(8,128)} %shard_map.37.early_ref, bf16[64,128,128]{2,1,0:T(8,128)(2,1)} %bitcast.5, bf16[2,784,128]{2,1,0:T(8,128)(2,1)} %copy-done.7, bf16[1,784,128]{2,1,0:T(8,128)(2,1)} %copy-done.9, bf16[1,784,128]{2,1,0:T(8,128)(2,1)} %copy-done.10, ...), custom_call_target="tpu_custom_call" | custom-call | tf_op jit(solution)/shard_map/pallas_call | solution.py:120
  (23 shorter events, 0.2 us)
Async XLA Ops:
  2.7 13.6 %copy-start.12 = (s32[6]{0:T(128)S(1)}, s32[6]{0:T(128)}, u32[]{:S(2)}) copy-start(s32[6]{0:T(128)} %param.4) | copy-start | bytes 76
  2.7 13.7 %copy-start.11 = (bf16[6,128,128]{2,1,0:T(8,128)(2,1)S(1)}, bf16[6,128,128]{2,1,0:T(8,128)(2,1)}, u32[]{:S(2)}) copy-start(bf16[6,128,128]{2,1,0:T(8,128)(2,1)} %param.3) | copy-start | bytes 589828
  2.7 85.3 %all-to-all-start = ((bf16[16,512,128]{2,1,0:T(8,128)(2,1)}), bf16[16,512,128]{2,1,0:T(8,128)(2,1)S(1)}, u32[]{:S(2)}, u32[]{:S(2)}) async-start(bf16[16,512,128]{2,1,0:T(8,128)(2,1)} %broadcast_in_dim.13), calls=%async_computation | async-start | bytes 4194304 | tf_op jit(solution)/shard_map/all_to_all | solution.py:144
  16.4 5.1 %collective-permute-start = (bf16[1,784,128]{2,1,0:T(8,128)(2,1)S(1)}, bf16[1,784,128]{2,1,0:T(8,128)(2,1)S(1)}, u32[]{:S(2)}, u32[]{:S(2)}) collective-permute-start(bf16[1,784,128]{2,1,0:T(8,128)(2,1)S(1)} %maximum_bitcast_fusion), channel_id=1, source_target_pairs={{0,1},{1,0},{2,3},{3,2},{4,5},{5,4},{6,7},{7,6},{8,9},{9,8},{10,11... | collective-permute-start | bytes 602120 | tf_op jit(solution)/shard_map/ppermute | solution.py:37
  19.2 13.6 %collective-permute-start.1 = (bf16[1,784,128]{2,1,0:T(8,128)(2,1)S(1)}, bf16[1,784,128]{2,1,0:T(8,128)(2,1)S(1)}, u32[]{:S(2)}, u32[]{:S(2)}) collective-permute-start(bf16[1,784,128]{2,1,0:T(8,128)(2,1)S(1)} %maximum_bitcast_fusion), channel_id=1, source_target_pairs={{0,16},{1,17},{2,18},{3,19},{4,20},{5,21},{6,22},{7,23},{8,24},{9,... | collective-permute-start | bytes 602120 | tf_op jit(solution)/shard_map/ppermute | solution.py:37
  21.5 34.5 %copy-start.2 = (bf16[2,784,128]{2,1,0:T(8,128)(2,1)}, bf16[2,784,128]{2,1,0:T(8,128)(2,1)S(1)}, u32[]{:S(2)}) copy-start(bf16[2,784,128]{2,1,0:T(8,128)(2,1)S(1)} %pad_maximum_fusion.1.refs_0_) | copy-start | bytes 1204228
  21.5 19.8 %collective-permute-start.3 = (bf16[2,784,128]{2,1,0:T(8,128)(2,1)S(1)}, bf16[2,784,128]{2,1,0:T(8,128)(2,1)S(1)}, u32[]{:S(2)}, u32[]{:S(2)}) collective-permute-start(bf16[2,784,128]{2,1,0:T(8,128)(2,1)S(1)} %pad_maximum_fusion.1.refs_0_), channel_id=1, source_target_pairs={{0,2},{1,15},{2,4},{3,1},{4,6},{5,3},{6,8},{7,5},{8,10},{9,7},{10,... | collective-permute-start | bytes 1204232 | tf_op jit(solution)/shard_map/ppermute | solution.py:37
  32.8 3.4 %collective-permute-start.2 = (bf16[1,784,128]{2,1,0:T(8,128)(2,1)S(1)}, bf16[1,784,128]{2,1,0:T(8,128)(2,1)S(1)}, u32[]{:S(2)}, u32[]{:S(2)}) collective-permute-start(bf16[1,784,128]{2,1,0:T(8,128)(2,1)S(1)} %collective-permute-done.1), channel_id=1, source_target_pairs={{0,1},{1,0},{2,3},{3,2},{4,5},{5,4},{6,7},{7,6},{8,9},{9,8},{10,11... | collective-permute-start | bytes 602120 | tf_op jit(solution)/shard_map/ppermute | solution.py:37
  36.3 14.9 %copy-start.8 = (bf16[2,784,128]{2,1,0:T(8,128)(2,1)}, bf16[2,784,128]{2,1,0:T(8,128)(2,1)S(1)}, u32[]{:S(2)}) copy-start(bf16[2,784,128]{2,1,0:T(8,128)(2,1)S(1)} %constant_dynamic-update-slice_fusion.refs_1_) | copy-start | bytes 1204228
  36.3 9.9 %collective-permute-start.4 = (bf16[2,784,128]{2,1,0:T(8,128)(2,1)S(1)}, bf16[2,784,128]{2,1,0:T(8,128)(2,1)S(1)}, u32[]{:S(2)}, u32[]{:S(2)}) collective-permute-start(bf16[2,784,128]{2,1,0:T(8,128)(2,1)S(1)} %constant_dynamic-update-slice_fusion.refs_1_), channel_id=1, source_target_pairs={{0,2},{1,15},{2,4},{3,1},{4,6},{5,3},{6,8},{7,5},{8,10},{9,7},{10,... | collective-permute-start | bytes 1204232 | tf_op jit(solution)/shard_map/ppermute | solution.py:37
  41.4 19.2 %copy-start.3 = (bf16[2,784,128]{2,1,0:T(8,128)(2,1)}, bf16[2,784,128]{2,1,0:T(8,128)(2,1)S(1)}, u32[]{:S(2)}) copy-start(bf16[2,784,128]{2,1,0:T(8,128)(2,1)S(1)} %collective-permute-done.3.refs_2_) | copy-start | bytes 1204228
  41.4 9.8 %collective-permute-start.5 = (bf16[2,784,128]{2,1,0:T(8,128)(2,1)S(1)}, bf16[2,784,128]{2,1,0:T(8,128)(2,1)S(1)}, u32[]{:S(2)}, u32[]{:S(2)}) collective-permute-start(bf16[2,784,128]{2,1,0:T(8,128)(2,1)S(1)} %collective-permute-done.3.refs_2_), channel_id=1, source_target_pairs={{0,2},{1,15},{2,4},{3,1},{4,6},{5,3},{6,8},{7,5},{8,10},{9,7},{10,... | collective-permute-start | bytes 1204232 | tf_op jit(solution)/shard_map/ppermute | solution.py:37
  46.2 14.5 %copy-start.4 = (bf16[2,784,128]{2,1,0:T(8,128)(2,1)}, bf16[2,784,128]{2,1,0:T(8,128)(2,1)S(1)}, u32[]{:S(2)}) copy-start(bf16[2,784,128]{2,1,0:T(8,128)(2,1)S(1)} %collective-permute-done.4.refs_3_) | copy-start | bytes 1204228
  46.2 9.8 %collective-permute-start.6 = (bf16[2,784,128]{2,1,0:T(8,128)(2,1)S(1)}, bf16[2,784,128]{2,1,0:T(8,128)(2,1)S(1)}, u32[]{:S(2)}, u32[]{:S(2)}) collective-permute-start(bf16[2,784,128]{2,1,0:T(8,128)(2,1)S(1)} %collective-permute-done.4.refs_3_), channel_id=1, source_target_pairs={{0,2},{1,15},{2,4},{3,1},{4,6},{5,3},{6,8},{7,5},{8,10},{9,7},{10,... | collective-permute-start | bytes 1204232 | tf_op jit(solution)/shard_map/ppermute | solution.py:37
  51.2 9.4 %copy-start.5 = (bf16[2,784,128]{2,1,0:T(8,128)(2,1)}, bf16[2,784,128]{2,1,0:T(8,128)(2,1)S(1)}, u32[]{:S(2)}) copy-start(bf16[2,784,128]{2,1,0:T(8,128)(2,1)S(1)} %collective-permute-done.5.refs_4_) | copy-start | bytes 1204228
  51.2 9.4 %collective-permute-start.7 = (bf16[2,784,128]{2,1,0:T(8,128)(2,1)S(1)}, bf16[2,784,128]{2,1,0:T(8,128)(2,1)S(1)}, u32[]{:S(2)}, u32[]{:S(2)}) collective-permute-start(bf16[2,784,128]{2,1,0:T(8,128)(2,1)S(1)} %collective-permute-done.5.refs_4_), channel_id=1, source_target_pairs={{0,2},{1,15},{2,4},{3,1},{4,6},{5,3},{6,8},{7,5},{8,10},{9,7},{10,... | collective-permute-start | bytes 1204232 | tf_op jit(solution)/shard_map/ppermute | solution.py:37
  56.0 25.2 %copy-start.6 = (bf16[2,784,128]{2,1,0:T(8,128)(2,1)}, bf16[2,784,128]{2,1,0:T(8,128)(2,1)S(1)}, u32[]{:S(2)}) copy-start(bf16[2,784,128]{2,1,0:T(8,128)(2,1)S(1)} %collective-permute-done.6.refs_5_) | copy-start | bytes 1204228
  60.6 27.4 %copy-start.1 = (bf16[2,784,128]{2,1,0:T(8,128)(2,1)}, bf16[2,784,128]{2,1,0:T(8,128)(2,1)S(1)}, u32[]{:S(2)}) copy-start(bf16[2,784,128]{2,1,0:T(8,128)(2,1)S(1)} %collective-permute-done.7.refs_6_) | copy-start | bytes 1204228
  60.6 27.3 %collective-permute-start.8 = (bf16[10,784,128]{2,1,0:T(8,128)(2,1)S(1)}, bf16[10,784,128]{2,1,0:T(8,128)(2,1)}, u32[]{:S(2)}, u32[]{:S(2)}) collective-permute-start(bf16[10,784,128]{2,1,0:T(8,128)(2,1)S(1)} %constant_dynamic-update-slice_fusion.2), channel_id=1, source_target_pairs={{0,1},{1,0},{2,3},{3,2},{4,5},{5,4},{6,7},{7,6},{8,9},{9,8},{10,11... | collective-permute-start | bytes 6021128 | tf_op jit(solution)/shard_map/ppermute | solution.py:37
  65.1 6.8 %collective-permute-start.10 = (bf16[1,784,128]{2,1,0:T(8,128)(2,1)S(1)}, bf16[1,784,128]{2,1,0:T(8,128)(2,1)S(1)}, u32[]{:S(2)}, u32[]{:S(2)}) collective-permute-start(bf16[1,784,128]{2,1,0:T(8,128)(2,1)S(1)} %slice.4), channel_id=1, source_target_pairs={{0,2},{1,15},{2,4},{3,1},{4,6},{5,3},{6,8},{7,5},{8,10},{9,7},{10,... | collective-permute-start | bytes 602120 | tf_op jit(solution)/shard_map/ppermute | solution.py:37
  67.9 13.2 %collective-permute-start.9 = (bf16[2,784,128]{2,1,0:T(8,128)(2,1)S(1)}, bf16[2,784,128]{2,1,0:T(8,128)(2,1)S(1)}, u32[]{:S(2)}, u32[]{:S(2)}) collective-permute-start(bf16[2,784,128]{2,1,0:T(8,128)(2,1)S(1)} %collective-permute-done.7.refs_6_), channel_id=1, source_target_pairs={{0,16},{1,17},{2,18},{3,19},{4,20},{5,21},{6,22},{7,23},{8,24},{9,... | collective-permute-start | bytes 1204232 | tf_op jit(solution)/shard_map/ppermute | solution.py:37
  71.9 25.3 %copy-start.9 = (bf16[1,784,128]{2,1,0:T(8,128)(2,1)}, bf16[1,784,128]{2,1,0:T(8,128)(2,1)S(1)}, u32[]{:S(2)}) copy-start(bf16[1,784,128]{2,1,0:T(8,128)(2,1)S(1)} %collective-permute-done.10.refs_1_) | copy-start | bytes 602116
  71.9 12.9 %collective-permute-start.11 = (bf16[1,784,128]{2,1,0:T(8,128)(2,1)S(1)}, bf16[1,784,128]{2,1,0:T(8,128)(2,1)S(1)}, u32[]{:S(2)}, u32[]{:S(2)}) collective-permute-start(bf16[1,784,128]{2,1,0:T(8,128)(2,1)S(1)} %collective-permute-done.10.refs_1_), channel_id=1, source_target_pairs={{0,16},{1,17},{2,18},{3,19},{4,20},{5,21},{6,22},{7,23},{8,24},{9,... | collective-permute-start | bytes 602120 | tf_op jit(solution)/shard_map/ppermute | solution.py:37
  81.1 16.1 %copy-start.7 = (bf16[2,784,128]{2,1,0:T(8,128)(2,1)}, bf16[2,784,128]{2,1,0:T(8,128)(2,1)S(1)}, u32[]{:S(2)}) copy-start(bf16[2,784,128]{2,1,0:T(8,128)(2,1)S(1)} %collective-permute-done.9.refs_0_) | copy-start | bytes 1204228
  84.8 12.5 %copy-start.10 = (bf16[1,784,128]{2,1,0:T(8,128)(2,1)}, bf16[1,784,128]{2,1,0:T(8,128)(2,1)S(1)}, u32[]{:S(2)}) copy-start(bf16[1,784,128]{2,1,0:T(8,128)(2,1)S(1)} %collective-permute-done.11.refs_2_) | copy-start | bytes 602116
  85.8 11.5 %collective-permute-start.12 = (bf16[4,784,128]{2,1,0:T(8,128)(2,1)}, bf16[4,784,128]{2,1,0:T(8,128)(2,1)}, u32[]{:S(2)}, u32[]{:S(2)}) collective-permute-start(bf16[4,784,128]{2,1,0:T(8,128)(2,1)} %pad_maximum_fusion), channel_id=1, source_target_pairs={{0,1},{1,0},{2,3},{3,2},{4,5},{5,4},{6,7},{7,6},{8,9},{9,8},{10,11... | collective-permute-start | bytes 2408456 | tf_op jit(solution)/shard_map/ppermute | solution.py:37
  88.0 1.3 %copy-start = (bf16[16,512,128]{2,1,0:T(8,128)(2,1)}, bf16[16,512,128]{2,1,0:T(8,128)(2,1)S(1)}, u32[]{:S(2)}) copy-start(bf16[16,512,128]{2,1,0:T(8,128)(2,1)S(1)} %all-to-all-done) | copy-start | bytes 6291460

commit v2 on v1

v2 whole, which is shorter than its diff:
```python
import functools

import jax
import jax.numpy as jnp
from jax import lax
from jax.experimental import pallas as pl
from jax.experimental.pallas import tpu as pltpu
from jax.sharding import PartitionSpec as P

BLK = 128
PAIR_DEV = 1024
PAIR_BLOCKS = PAIR_DEV // BLK
KMAX = 6
NY = 8
NZ = 8
LIST_ROWS = 16
SLOT_ROWS = KMAX * BLK
P_LANE = 8


def col_of(x, y, core):
    return ((x % 2) * NY + y % NY) * 2 + core % 2


def col_perm(target):
    return [
        (col_of(x, y, c), col_of(*target(x, y, c)))
        for x in range(2)
        for y in range(NY)
        for c in range(2)
    ]


CORE = col_perm(lambda x, y, c: (x, y, c + 1))
X_PARTNER = col_perm(lambda x, y, c: (x + 1, y, c))
RING = col_perm(lambda x, y, c: (x, y + 1 if c == 0 else y - 1, c))


def row_of(x, z):
    return (x % 2) * NZ + z % NZ


def row_perm(step):
    return [(row_of(x, z), row_of(x, z + step)) for x in range(2) for z in range(NZ)]


BAND_GROUPS = [[row_of(x, z) for x in range(2) for z in range(first, NZ, 2)] for first in range(2)]


def sent(value, perm, axis="col"):
    return lax.ppermute(value, axis, perm)


def payload(slots, block_list, col_blocks, shard_blocks):
    me = lax.axis_index("col")
    clipped = jnp.maximum(block_list, 0)
    shard = me * col_blocks // shard_blocks
    x, z = shard // NZ, shard % NZ
    place = (z % 2) * NZ + x * (NZ // 2) + z // 2
    band_block = place * shard_blocks + me * col_blocks % shard_blocks + clipped % col_blocks
    pair_block = jnp.where(block_list >= 0, clipped // col_blocks, PAIR_BLOCKS)
    row = jnp.concatenate(
        [
            jnp.pad(band_block, (0, P_LANE - KMAX)),
            jnp.pad(pair_block, (0, BLK - P_LANE - KMAX)),
        ]
    )
    rows = jnp.broadcast_to(row.astype(jnp.bfloat16), (LIST_ROWS, BLK))
    return jnp.concatenate([slots.reshape(SLOT_ROWS, BLK), rows])[None]


def add_products(pieces_refs, band_refs, total, band_v, pieces_v, rows_v, list_v, list_s, sems, prepare):
    def copies(refs, target, row, take):
        start, made = 0, []
        for n, ref in enumerate(refs):
            count = ref.shape[0]
            made.append(pltpu.make_async_copy(take(ref), target.at[pl.ds(start, count)], sems.at[row, n]))
            start += count
        return made

    list_rows = copies(pieces_refs, rows_v, 0, lambda ref: ref.at[:, SLOT_ROWS:, :])
    band_copies = copies(band_refs, band_v, 1, lambda ref: ref)
    piece_copies = copies(pieces_refs, pieces_v, 2, lambda ref: ref.at[:, :SLOT_ROWS, :])
    for copy in (*list_rows, *band_copies, *piece_copies):
        copy.start()
    prepare()
    for copy in list_rows:
        copy.wait()
    odd = lax.axis_index("row") % 2
    half = band_v.shape[0] // 2
    lanes = lax.broadcasted_iota(jnp.int32, (1, BLK), 1)
    flip = jnp.where(lanes < P_LANE, odd * half, 0)
    for i in range(rows_v.shape[0]):
        rows = rows_v[i].astype(jnp.float32)
        list_v[i : i + 1, :] = jnp.bitwise_xor(rows[:1].astype(jnp.int32), flip)
    list_copy = pltpu.make_async_copy(list_v, list_s, sems.at[3, 0])
    list_copy.start()
    list_copy.wait()
    for copy in band_copies:
        copy.wait()

    def one_piece(i, carry):
        for j in range(KMAX):
            band_block = list_s[i, j]
            pair_block = list_s[i, P_LANE + j]
            prod = jnp.dot(
                pieces_v[i, j * BLK : (j + 1) * BLK, :],
                band_v[band_block],
                preferred_element_type=jnp.float32,
            )
            total[pair_block] += prod
        return carry

    start = 0
    for copy, ref in zip(piece_copies, pieces_refs):
        copy.wait()
        lax.fori_loop(start, start + ref.shape[0], one_piece, 0)
        start += ref.shape[0]


def early_products(count, *refs):
    total, *scratch = refs[-7:]

    def clear():
        total[...] = jnp.zeros_like(total)

    add_products(refs[:count], refs[count:-7], total, *scratch, clear)


def late_products(count, early_ref, *refs):
    out_ref, total, *scratch = refs[-8:]

    def take():
        total[...] = early_ref[...]

    add_products(refs[:count], refs[count:-8], total, *scratch, take)
    for p in range(PAIR_BLOCKS):
        out_ref[p * BLK : (p + 1) * BLK, :] = total[p]


def kernel_call(body, out_shape, taken, pieces, band, scratch):
    vmem = pl.BlockSpec(memory_space=pltpu.VMEM)
    count = sum(piece.shape[0] for piece in pieces)
    blocks = sum(part.shape[0] for part in band)
    dtype = pieces[0].dtype
    return pl.pallas_call(
        functools.partial(body, len(pieces)),
        out_shape=out_shape,
        in_specs=[vmem] * len(taken)
        + [pl.BlockSpec(memory_space=pltpu.HBM)] * (len(pieces) + len(band)),
        out_specs=vmem,
        scratch_shapes=[
            *scratch,
            pltpu.VMEM((blocks, BLK, BLK), dtype),
            pltpu.VMEM((count, SLOT_ROWS, BLK), dtype),
            pltpu.VMEM((count, LIST_ROWS, BLK), dtype),
            pltpu.VMEM((count, BLK), jnp.int32),
            pltpu.SMEM((count, BLK), jnp.int32),
            pltpu.SemaphoreType.DMA((4, max(len(pieces), len(band)))),
        ],
        compiler_params=pltpu.CompilerParams(vmem_limit_bytes=60 << 20),
    )(*taken, *pieces, *band)


def gathered_band(metric):
    copies = jnp.broadcast_to(metric, (NZ, *metric.shape))
    same = lax.all_to_all(
        copies, "row", split_axis=0, concat_axis=0, tiled=True, axis_index_groups=BAND_GROUPS
    )
    upper, lower = same[: NZ // 2], same[NZ // 2 :]
    parts = [same, sent(upper, row_perm(1), "row"), sent(lower, row_perm(-1), "row")]
    return [part.reshape(-1, BLK, metric.shape[1]) for part in parts]


def on_device(slots, block_list, metric):
    out_cols = metric.shape[1]
    rows = lax.axis_size("row")
    band_blocks = rows * metric.shape[0] // BLK
    col_blocks = band_blocks // lax.axis_size("col")
    band = gathered_band(metric)
    own = payload(slots, block_list, col_blocks, metric.shape[0] // BLK)
    own_x = sent(own, X_PARTNER)
    near = jnp.concatenate([own, sent(own, CORE)])
    near_x = jnp.concatenate([own_x, sent(own_x, CORE)])
    a1 = sent(near, RING)
    b1 = sent(near_x, RING)
    a2 = sent(a1, RING)
    b2 = sent(b1, RING)
    a3 = sent(a2, RING)
    b3 = sent(b2, RING)
    a4 = sent(a3[:1], RING)
    b4 = sent(b3[:1], RING)
    early = [a1, b1, a2, b2, a3]
    late = [b3, a4, b4]
    early_other = sent(jnp.concatenate(early), CORE)
    late_other = sent(jnp.concatenate(late), CORE)
    early = [near, near_x, *early, early_other]
    late = [*late, late_other]
    total_shape = (PAIR_BLOCKS + 1, BLK, out_cols)
    total = kernel_call(
        early_products, jax.ShapeDtypeStruct(total_shape, jnp.float32), [], early, band, []
    )
    return kernel_call(
        late_products,
        jax.ShapeDtypeStruct((PAIR_DEV, out_cols), jnp.float32),
        [total],
        late,
        band,
        [pltpu.VMEM(total_shape, jnp.float32)],
    )


def solution(mesh):
    return jax.shard_map(
        on_device,
        mesh=mesh,
        in_specs=(P(("row", "col"), None, None), P(("row", "col")), P("row", "col")),
        out_specs=P("row", "col"),
        check_vma=False,
    )
```

time: 103 us -> 115 us (1.12)
  waiting for transfers between devices: 24.6 us -> 31 us
  starting transfers between devices: 59 us -> 61.1 us
  local copies, waits for them, and re-layouts: 4.33 us -> 6.08 us
  other arithmetic: 1.16 us -> 2.76 us
    ppermute x13 -> x15, waiting for transfers between devices: 24.6 us -> 31 us  [sent(): return lax.ppermute(value, axis, perm)]
    ppermute x13 -> x15, starting transfers between devices: 45.4 us -> 50.8 us  [sent(): return lax.ppermute(value, axis, perm)]
    all_to_all x1, starting transfers between devices: 13.5 us -> 10.3 us  [gathered_band(): lax.all_to_all(copies, 'row', split_axis=0, concat_axis=0, tiled=True, ax...]
    unnamed x31 -> x33, local copies, waits for them, and re-layouts: 1.58 us -> 4.02 us
    broadcast_in_dim x1, local copies, waits for them, and re-layouts: 2.65 us -> 1.12 us  [gathered_band(): copies = jnp.broadcast_to(metric, (NZ, *metric.shape))]
  transfers between devices with their start and end apart: 14 -> 16, of which waited for: 7 -> 8; matrix products, arithmetic and copies ran while one was open for 1% -> 5% of each run, Pallas kernels for 8% -> 7%
where the time goes in v2:
time: 115 us
  starting transfers between devices  61.1 us (53%)
  waiting for transfers between devices  31 us (27%)
  Pallas kernels  13.4 us (12%)
  local copies, waits for them, and re-layouts  6.08 us (5%)
  other arithmetic  2.76 us (2%)
    ppermute x15, starting transfers between devices, sent(): return lax.ppermute(value, axis, perm)  50.8 us
    ppermute x15, waiting for transfers between devices, sent(): return lax.ppermute(value, axis, perm)  31 us
    pallas_call x2, Pallas kernels, kernel_call(): pl.pallas_call(functools.partial(body, len(pieces)), out_shape=out_shape,...  13.4 us
    all_to_all x1, starting transfers between devices, gathered_band(): lax.all_to_all(copies, 'row', split_axis=0, concat_axis=0, tiled=True, ax...  10.3 us
    unnamed x33, local copies, waits for them, and re-layouts  4.02 us
  transfers between devices with their start and end apart: 16, of which 8 were waited for; matrix products, arithmetic and copies ran while one was open for 5% of the time, Pallas kernels for 7%

profile of v2, /device:TPU:1, one launch (start us, length us, event | category | flops | bytes accessed | tf_op | source)
XLA Modules:
  0.0 114.7 jit_solution(10943815067777913698)
XLA Ops:
  0.0 0.7 fusion.1
  0.7 0.1 fusion.3
  0.8 0.9 maximum_bitcast_fusion
  1.7 8.7 %collective-permute-start = (bf16[1,784,128]{2,1,0:T(8,128)(2,1)S(1)}, bf16[1,784,128]{2,1,0:T(8,128)(2,1)S(1)}, u32[]{:S(2)}, u32[]{:S(2)}) collective-permute-start(bf16[1,784,128]{2,1,0:T(8,128)(2,1)S(1)} %maximum_bitcast_fusion), channel_id=1, source_target_pairs={{0,1},{1,0},{2,3},{3,2},{4,5},{5,4},{6,7},{7,6},{8,9},{9,8},{10,11... | collective-permute-start | bytes 602120 | tf_op jit(solution)/shard_map/ppermute | solution.py:51
  10.5 1.9 %collective-permute-start.1 = (bf16[1,784,128]{2,1,0:T(8,128)(2,1)S(1)}, bf16[1,784,128]{2,1,0:T(8,128)(2,1)S(1)}, u32[]{:S(2)}, u32[]{:S(2)}) collective-permute-start(bf16[1,784,128]{2,1,0:T(8,128)(2,1)S(1)} %maximum_bitcast_fusion), channel_id=1, source_target_pairs={{0,16},{1,17},{2,18},{3,19},{4,20},{5,21},{6,22},{7,23},{8,24},{9,... | collective-permute-start | bytes 602120 | tf_op jit(solution)/shard_map/ppermute | solution.py:51
  12.4 0.0 collective-permute-done
  12.5 0.0 copy-start.5
  12.5 1.9 %collective-permute-start.3 = (bf16[2,784,128]{2,1,0:T(8,128)(2,1)S(1)}, bf16[2,784,128]{2,1,0:T(8,128)(2,1)S(1)}, u32[]{:S(2)}, u32[]{:S(2)}) collective-permute-start(bf16[2,784,128]{2,1,0:T(8,128)(2,1)S(1)} %pad_maximum_fusion.1.refs_0_), channel_id=1, source_target_pairs={{0,2},{1,15},{2,4},{3,1},{4,6},{5,3},{6,8},{7,5},{8,10},{9,7},{10,... | collective-permute-start | bytes 1204232 | tf_op jit(solution)/shard_map/ppermute | solution.py:51
  14.4 4.5 %collective-permute-done.1 = bf16[1,784,128]{2,1,0:T(8,128)(2,1)S(1)} collective-permute-done((bf16[1,784,128]{2,1,0:T(8,128)(2,1)S(1)}, bf16[1,784,128]{2,1,0:T(8,128)(2,1)S(1)}, u32[]{:S(2)}, u32[]{:S(2)}) %collective-permute-start.1) | collective-permute-done | bytes 200736 | tf_op jit(solution)/shard_map/ppermute | solution.py:51
  18.9 2.8 %collective-permute-start.2 = (bf16[1,784,128]{2,1,0:T(8,128)(2,1)S(1)}, bf16[1,784,128]{2,1,0:T(8,128)(2,1)S(1)}, u32[]{:S(2)}, u32[]{:S(2)}) collective-permute-start(bf16[1,784,128]{2,1,0:T(8,128)(2,1)S(1)} %collective-permute-done.1), channel_id=1, source_target_pairs={{0,1},{1,0},{2,3},{3,2},{4,5},{5,4},{6,7},{7,6},{8,9},{9,8},{10,11... | collective-permute-start | bytes 602120 | tf_op jit(solution)/shard_map/ppermute | solution.py:51
  21.7 1.0 collective-permute-done.2
  22.8 0.0 copy-start.10
  22.8 1.9 %collective-permute-start.4 = (bf16[2,784,128]{2,1,0:T(8,128)(2,1)S(1)}, bf16[2,784,128]{2,1,0:T(8,128)(2,1)S(1)}, u32[]{:S(2)}, u32[]{:S(2)}) collective-permute-start(bf16[2,784,128]{2,1,0:T(8,128)(2,1)S(1)} %constant_dynamic-update-slice_fusion.refs_1_), channel_id=1, source_target_pairs={{0,2},{1,15},{2,4},{3,1},{4,6},{5,3},{6,8},{7,5},{8,10},{9,7},{10,... | collective-permute-start | bytes 1204232 | tf_op jit(solution)/shard_map/ppermute | solution.py:51
  24.7 0.0 collective-permute-done.3.refs_2_
  24.7 1.9 %collective-permute-start.5 = (bf16[2,784,128]{2,1,0:T(8,128)(2,1)S(1)}, bf16[2,784,128]{2,1,0:T(8,128)(2,1)S(1)}, u32[]{:S(2)}, u32[]{:S(2)}) collective-permute-start(bf16[2,784,128]{2,1,0:T(8,128)(2,1)S(1)} %collective-permute-done.3.refs_2_), channel_id=1, source_target_pairs={{0,2},{1,15},{2,4},{3,1},{4,6},{5,3},{6,8},{7,5},{8,10},{9,7},{10,... | collective-permute-start | bytes 1204232 | tf_op jit(solution)/shard_map/ppermute | solution.py:51
  26.7 5.0 %collective-permute-done.4.refs_3_ = bf16[2,784,128]{2,1,0:T(8,128)(2,1)S(1)} collective-permute-done((bf16[2,784,128]{2,1,0:T(8,128)(2,1)S(1)}, bf16[2,784,128]{2,1,0:T(8,128)(2,1)S(1)}, u32[]{:S(2)}, u32[]{:S(2)}) %collective-permute-start.4) | collective-permute-done | bytes 401440 | tf_op jit(solution)/shard_map/ppermute | solution.py:51
  31.7 2.8 %collective-permute-start.6 = (bf16[2,784,128]{2,1,0:T(8,128)(2,1)S(1)}, bf16[2,784,128]{2,1,0:T(8,128)(2,1)S(1)}, u32[]{:S(2)}, u32[]{:S(2)}) collective-permute-start(bf16[2,784,128]{2,1,0:T(8,128)(2,1)S(1)} %collective-permute-done.4.refs_3_), channel_id=1, source_target_pairs={{0,2},{1,15},{2,4},{3,1},{4,6},{5,3},{6,8},{7,5},{8,10},{9,7},{10,... | collective-permute-start | bytes 1204232 | tf_op jit(solution)/shard_map/ppermute | solution.py:51
  34.5 1.1 broadcast_in_dim.16
  35.7 10.3 %all-to-all-start = ((bf16[8,512,128]{2,1,0:T(8,128)(2,1)}), bf16[8,512,128]{2,1,0:T(8,128)(2,1)S(1)}, u32[]{:S(2)}, u32[]{:S(2)}) async-start(bf16[8,512,128]{2,1,0:T(8,128)(2,1)} %broadcast_in_dim.16), calls=%async_computation | async-start | bytes 2097152 | tf_op jit(solution)/shard_map/all_to_all | solution.py:167
  46.0 0.0 collective-permute-done.5.refs_4_
  46.0 2.1 %collective-permute-start.7 = (bf16[2,784,128]{2,1,0:T(8,128)(2,1)S(1)}, bf16[2,784,128]{2,1,0:T(8,128)(2,1)S(1)}, u32[]{:S(2)}, u32[]{:S(2)}) collective-permute-start(bf16[2,784,128]{2,1,0:T(8,128)(2,1)S(1)} %collective-permute-done.5.refs_4_), channel_id=1, source_target_pairs={{0,2},{1,15},{2,4},{3,1},{4,6},{5,3},{6,8},{7,5},{8,10},{9,7},{10,... | collective-permute-start | bytes 1204232 | tf_op jit(solution)/shard_map/ppermute | solution.py:51
  48.1 0.8 constant_dynamic-update-slice_fusion.6
  48.8 0.8 constant_dynamic-update-slice_fusion.5
  49.6 0.8 constant_dynamic-update-slice_fusion.4
  50.4 0.0 collective-permute-done.6.refs_5_
  50.4 0.8 constant_dynamic-update-slice_fusion.3
  51.3 3.6 %collective-permute-done.7.refs_6_ = bf16[2,784,128]{2,1,0:T(8,128)(2,1)S(1)} collective-permute-done((bf16[2,784,128]{2,1,0:T(8,128)(2,1)S(1)}, bf16[2,784,128]{2,1,0:T(8,128)(2,1)S(1)}, u32[]{:S(2)}, u32[]{:S(2)}) %collective-permute-start.7) | collective-permute-done | bytes 401440 | tf_op jit(solution)/shard_map/ppermute | solution.py:51
  54.9 0.8 constant_dynamic-update-slice_fusion.2
  55.7 2.9 %collective-permute-start.8 = (bf16[10,784,128]{2,1,0:T(8,128)(2,1)}, bf16[10,784,128]{2,1,0:T(8,128)(2,1)}, u32[]{:S(2)}, u32[]{:S(2)}) collective-permute-start(bf16[10,784,128]{2,1,0:T(8,128)(2,1)} %constant_dynamic-update-slice_fusion.2), channel_id=1, source_target_pairs={{0,1},{1,0},{2,3},{3,2},{4,5},{5,4},{6,7},{7,6},{8,9},{9,8},{10,11... | collective-permute-start | bytes 6021128 | tf_op jit(solution)/shard_map/ppermute | solution.py:51
  58.7 3.5 %collective-permute-start.11 = (bf16[2,784,128]{2,1,0:T(8,128)(2,1)S(1)}, bf16[2,784,128]{2,1,0:T(8,128)(2,1)S(1)}, u32[]{:S(2)}, u32[]{:S(2)}) collective-permute-start(bf16[2,784,128]{2,1,0:T(8,128)(2,1)S(1)} %collective-permute-done.6.refs_5_), channel_id=1, source_target_pairs={{0,2},{1,15},{2,4},{3,1},{4,6},{5,3},{6,8},{7,5},{8,10},{9,7},{10,... | collective-permute-start | bytes 1204232 | tf_op jit(solution)/shard_map/ppermute | solution.py:51
  62.2 2.4 %collective-permute-start.12 = (bf16[1,784,128]{2,1,0:T(8,128)(2,1)S(1)}, bf16[1,784,128]{2,1,0:T(8,128)(2,1)S(1)}, u32[]{:S(2)}, u32[]{:S(2)}) collective-permute-start(bf16[1,784,128]{2,1,0:T(8,128)(2,1)S(1)} %slice.18), channel_id=1, source_target_pairs={{0,2},{1,15},{2,4},{3,1},{4,6},{5,3},{6,8},{7,5},{8,10},{9,7},{10,... | collective-permute-start | bytes 602120 | tf_op jit(solution)/shard_map/ppermute | solution.py:51
  64.7 2.9 %collective-permute-done.11.refs_0_ = bf16[2,784,128]{2,1,0:T(8,128)(2,1)S(1)} collective-permute-done((bf16[2,784,128]{2,1,0:T(8,128)(2,1)S(1)}, bf16[2,784,128]{2,1,0:T(8,128)(2,1)S(1)}, u32[]{:S(2)}, u32[]{:S(2)}) %collective-permute-start.11) | collective-permute-done | bytes 401440 | tf_op jit(solution)/shard_map/ppermute | solution.py:51
  67.6 4.7 %collective-permute-start.13 = (bf16[1,784,128]{2,1,0:T(8,128)(2,1)S(1)}, bf16[1,784,128]{2,1,0:T(8,128)(2,1)S(1)}, u32[]{:S(2)}, u32[]{:S(2)}) collective-permute-start(bf16[1,784,128]{2,1,0:T(8,128)(2,1)S(1)} %slice.19), channel_id=1, source_target_pairs={{0,2},{1,15},{2,4},{3,1},{4,6},{5,3},{6,8},{7,5},{8,10},{9,7},{10,... | collective-permute-start | bytes 602120 | tf_op jit(solution)/shard_map/ppermute | solution.py:51
  72.3 0.0 collective-permute-done.12.refs_1_
  72.4 2.6 %collective-permute-done.13.refs_2_ = bf16[1,784,128]{2,1,0:T(8,128)(2,1)S(1)} collective-permute-done((bf16[1,784,128]{2,1,0:T(8,128)(2,1)S(1)}, bf16[1,784,128]{2,1,0:T(8,128)(2,1)S(1)}, u32[]{:S(2)}, u32[]{:S(2)}) %collective-permute-start.13) | collective-permute-done | bytes 200736 | tf_op jit(solution)/shard_map/ppermute | solution.py:51
  75.0 1.0 pad_maximum_fusion
  76.0 5.4 %collective-permute-start.14 = (bf16[4,784,128]{2,1,0:T(8,128)(2,1)}, bf16[4,784,128]{2,1,0:T(8,128)(2,1)}, u32[]{:S(2)}, u32[]{:S(2)}) collective-permute-start(bf16[4,784,128]{2,1,0:T(8,128)(2,1)} %pad_maximum_fusion), channel_id=1, source_target_pairs={{0,1},{1,0},{2,3},{3,2},{4,5},{5,4},{6,7},{7,6},{8,9},{9,8},{10,11... | collective-permute-start | bytes 2408456 | tf_op jit(solution)/shard_map/ppermute | solution.py:51
  81.4 0.0 all-to-all-done
  81.4 0.1 fusion.4
  81.5 3.1 %collective-permute-start.9 = (bf16[4,512,128]{2,1,0:T(8,128)(2,1)S(1)}, bf16[4,512,128]{2,1,0:T(8,128)(2,1)S(1)}, u32[]{:S(2)}, u32[]{:S(2)}) collective-permute-start(bf16[4,512,128]{2,1,0:T(8,128)(2,1)S(1)} %get-tuple-element.6), channel_id=1, source_target_pairs={{0,32},{32,64},{64,96},{96,128},{128,160},{160,192},{192,224},{224... | collective-permute-start | bytes 1572872 | tf_op jit(solution)/shard_map/ppermute | solution.py:51
  84.6 4.6 %collective-permute-start.10 = (bf16[4,512,128]{2,1,0:T(8,128)(2,1)S(1)}, bf16[4,512,128]{2,1,0:T(8,128)(2,1)S(1)}, u32[]{:S(2)}, u32[]{:S(2)}) collective-permute-start(bf16[4,512,128]{2,1,0:T(8,128)(2,1)S(1)} %get-tuple-element.5), channel_id=1, source_target_pairs={{0,224},{32,0},{64,32},{96,64},{128,96},{160,128},{192,160},{224,1... | collective-permute-start | bytes 1572872 | tf_op jit(solution)/shard_map/ppermute | solution.py:51
  89.2 10.3 %collective-permute-done.9 = bf16[4,512,128]{2,1,0:T(8,128)(2,1)S(1)} collective-permute-done((bf16[4,512,128]{2,1,0:T(8,128)(2,1)S(1)}, bf16[4,512,128]{2,1,0:T(8,128)(2,1)S(1)}, u32[]{:S(2)}, u32[]{:S(2)}) %collective-permute-start.9) | collective-permute-done | bytes 524320 | tf_op jit(solution)/shard_map/ppermute | solution.py:51
  99.6 0.9 collective-permute-done.10
  100.5 0.0 collective-permute-done.8.refs_7_
  100.5 0.8 copy-done.4
  101.2 8.0 %shard_map.37.early_ref = f32[9,128,128]{2,1,0:T(8,128)} custom-call(bf16[2,784,128]{2,1,0:T(8,128)(2,1)} %copy-done.5, bf16[2,784,128]{2,1,0:T(8,128)(2,1)} %copy-done.10, bf16[2,784,128]{2,1,0:T(8,128)(2,1)} %copy-done.6, bf16[2,784,128]{2,1,0:T(8,128)(2,1)} %copy-done.7, bf16[2,784,128]{2,1,0:T(8,128)(2,1)} %copy-done.8, bf16[2,784,128]{2,1,0:T(8,128)(2,1)} %copy-done.9, ...), custom_call_target="tpu_custom_call" | custom-call | tf_op jit(solution)/shard_map/pallas_call | solution.py:146
  109.3 0.0 collective-permute-done.14.refs_3_
  109.3 5.4 %shard_map.38 = f32[1024,128]{1,0:T(8,128)} custom-call(f32[9,128,128]{2,1,0:T(8,128)} %shard_map.37.early_ref, bf16[2,784,128]{2,1,0:T(8,128)(2,1)} %copy-done.2, bf16[1,784,128]{2,1,0:T(8,128)(2,1)} %copy-done.11, bf16[1,784,128]{2,1,0:T(8,128)(2,1)} %copy-done.12, bf16[4,784,128]{2,1,0:T(8,128)(2,1)} %collective-permute-done.14.refs_3_, ...), custom_call_target="tpu_custom_call" | custom-call | tf_op jit(solution)/shard_map/pallas_call | solution.py:146
  (31 shorter events, 0.2 us)
Async XLA Ops:
  0.0 34.5 %copy-start.13 = (bf16[512,128]{1,0:T(8,128)(2,1)S(1)}, bf16[512,128]{1,0:T(8,128)(2,1)}, u32[]{:S(2)}) copy-start(bf16[512,128]{1,0:T(8,128)(2,1)} %param.5) | copy-start | bytes 393220
  1.7 10.7 %collective-permute-start = (bf16[1,784,128]{2,1,0:T(8,128)(2,1)S(1)}, bf16[1,784,128]{2,1,0:T(8,128)(2,1)S(1)}, u32[]{:S(2)}, u32[]{:S(2)}) collective-permute-start(bf16[1,784,128]{2,1,0:T(8,128)(2,1)S(1)} %maximum_bitcast_fusion), channel_id=1, source_target_pairs={{0,1},{1,0},{2,3},{3,2},{4,5},{5,4},{6,7},{7,6},{8,9},{9,8},{10,11... | collective-permute-start | bytes 602120 | tf_op jit(solution)/shard_map/ppermute | solution.py:51
  10.5 8.4 %collective-permute-start.1 = (bf16[1,784,128]{2,1,0:T(8,128)(2,1)S(1)}, bf16[1,784,128]{2,1,0:T(8,128)(2,1)S(1)}, u32[]{:S(2)}, u32[]{:S(2)}) collective-permute-start(bf16[1,784,128]{2,1,0:T(8,128)(2,1)S(1)} %maximum_bitcast_fusion), channel_id=1, source_target_pairs={{0,16},{1,17},{2,18},{3,19},{4,20},{5,21},{6,22},{7,23},{8,24},{9,... | collective-permute-start | bytes 602120 | tf_op jit(solution)/shard_map/ppermute | solution.py:51
  12.5 23.2 %copy-start.5 = (bf16[2,784,128]{2,1,0:T(8,128)(2,1)}, bf16[2,784,128]{2,1,0:T(8,128)(2,1)S(1)}, u32[]{:S(2)}) copy-start(bf16[2,784,128]{2,1,0:T(8,128)(2,1)S(1)} %pad_maximum_fusion.1.refs_0_) | copy-start | bytes 1204228
  12.5 12.2 %collective-permute-start.3 = (bf16[2,784,128]{2,1,0:T(8,128)(2,1)S(1)}, bf16[2,784,128]{2,1,0:T(8,128)(2,1)S(1)}, u32[]{:S(2)}, u32[]{:S(2)}) collective-permute-start(bf16[2,784,128]{2,1,0:T(8,128)(2,1)S(1)} %pad_maximum_fusion.1.refs_0_), channel_id=1, source_target_pairs={{0,2},{1,15},{2,4},{3,1},{4,6},{5,3},{6,8},{7,5},{8,10},{9,7},{10,... | collective-permute-start | bytes 1204232 | tf_op jit(solution)/shard_map/ppermute | solution.py:51
  18.9 3.8 %collective-permute-start.2 = (bf16[1,784,128]{2,1,0:T(8,128)(2,1)S(1)}, bf16[1,784,128]{2,1,0:T(8,128)(2,1)S(1)}, u32[]{:S(2)}, u32[]{:S(2)}) collective-permute-start(bf16[1,784,128]{2,1,0:T(8,128)(2,1)S(1)} %collective-permute-done.1), channel_id=1, source_target_pairs={{0,1},{1,0},{2,3},{3,2},{4,5},{5,4},{6,7},{7,6},{8,9},{9,8},{10,11... | collective-permute-start | bytes 602120 | tf_op jit(solution)/shard_map/ppermute | solution.py:51
  22.8 26.1 %copy-start.10 = (bf16[2,784,128]{2,1,0:T(8,128)(2,1)}, bf16[2,784,128]{2,1,0:T(8,128)(2,1)S(1)}, u32[]{:S(2)}) copy-start(bf16[2,784,128]{2,1,0:T(8,128)(2,1)S(1)} %constant_dynamic-update-slice_fusion.refs_1_) | copy-start | bytes 1204228
  22.8 8.9 %collective-permute-start.4 = (bf16[2,784,128]{2,1,0:T(8,128)(2,1)S(1)}, bf16[2,784,128]{2,1,0:T(8,128)(2,1)S(1)}, u32[]{:S(2)}, u32[]{:S(2)}) collective-permute-start(bf16[2,784,128]{2,1,0:T(8,128)(2,1)S(1)} %constant_dynamic-update-slice_fusion.refs_1_), channel_id=1, source_target_pairs={{0,2},{1,15},{2,4},{3,1},{4,6},{5,3},{6,8},{7,5},{8,10},{9,7},{10,... | collective-permute-start | bytes 1204232 | tf_op jit(solution)/shard_map/ppermute | solution.py:51
  24.7 24.1 %copy-start.6 = (bf16[2,784,128]{2,1,0:T(8,128)(2,1)}, bf16[2,784,128]{2,1,0:T(8,128)(2,1)S(1)}, u32[]{:S(2)}) copy-start(bf16[2,784,128]{2,1,0:T(8,128)(2,1)S(1)} %collective-permute-done.3.refs_2_) | copy-start | bytes 1204228
  24.7 21.2 %collective-permute-start.5 = (bf16[2,784,128]{2,1,0:T(8,128)(2,1)S(1)}, bf16[2,784,128]{2,1,0:T(8,128)(2,1)S(1)}, u32[]{:S(2)}, u32[]{:S(2)}) collective-permute-start(bf16[2,784,128]{2,1,0:T(8,128)(2,1)S(1)} %collective-permute-done.3.refs_2_), channel_id=1, source_target_pairs={{0,2},{1,15},{2,4},{3,1},{4,6},{5,3},{6,8},{7,5},{8,10},{9,7},{10,... | collective-permute-start | bytes 1204232 | tf_op jit(solution)/shard_map/ppermute | solution.py:51
  31.7 17.2 %copy-start.7 = (bf16[2,784,128]{2,1,0:T(8,128)(2,1)}, bf16[2,784,128]{2,1,0:T(8,128)(2,1)S(1)}, u32[]{:S(2)}) copy-start(bf16[2,784,128]{2,1,0:T(8,128)(2,1)S(1)} %collective-permute-done.4.refs_3_) | copy-start | bytes 1204228
  31.7 18.7 %collective-permute-start.6 = (bf16[2,784,128]{2,1,0:T(8,128)(2,1)S(1)}, bf16[2,784,128]{2,1,0:T(8,128)(2,1)S(1)}, u32[]{:S(2)}, u32[]{:S(2)}) collective-permute-start(bf16[2,784,128]{2,1,0:T(8,128)(2,1)S(1)} %collective-permute-done.4.refs_3_), channel_id=1, source_target_pairs={{0,2},{1,15},{2,4},{3,1},{4,6},{5,3},{6,8},{7,5},{8,10},{9,7},{10,... | collective-permute-start | bytes 1204232 | tf_op jit(solution)/shard_map/ppermute | solution.py:51
  35.7 45.7 %all-to-all-start = ((bf16[8,512,128]{2,1,0:T(8,128)(2,1)}), bf16[8,512,128]{2,1,0:T(8,128)(2,1)S(1)}, u32[]{:S(2)}, u32[]{:S(2)}) async-start(bf16[8,512,128]{2,1,0:T(8,128)(2,1)} %broadcast_in_dim.16), calls=%async_computation | async-start | bytes 2097152 | tf_op jit(solution)/shard_map/all_to_all | solution.py:167
  46.0 9.7 %copy-start.8 = (bf16[2,784,128]{2,1,0:T(8,128)(2,1)}, bf16[2,784,128]{2,1,0:T(8,128)(2,1)S(1)}, u32[]{:S(2)}) copy-start(bf16[2,784,128]{2,1,0:T(8,128)(2,1)S(1)} %collective-permute-done.5.refs_4_) | copy-start | bytes 1204228
  46.0 8.9 %collective-permute-start.7 = (bf16[2,784,128]{2,1,0:T(8,128)(2,1)S(1)}, bf16[2,784,128]{2,1,0:T(8,128)(2,1)S(1)}, u32[]{:S(2)}, u32[]{:S(2)}) collective-permute-start(bf16[2,784,128]{2,1,0:T(8,128)(2,1)S(1)} %collective-permute-done.5.refs_4_), channel_id=1, source_target_pairs={{0,2},{1,15},{2,4},{3,1},{4,6},{5,3},{6,8},{7,5},{8,10},{9,7},{10,... | collective-permute-start | bytes 1204232 | tf_op jit(solution)/shard_map/ppermute | solution.py:51
  50.4 31.1 %copy-start.9 = (bf16[2,784,128]{2,1,0:T(8,128)(2,1)}, bf16[2,784,128]{2,1,0:T(8,128)(2,1)S(1)}, u32[]{:S(2)}) copy-start(bf16[2,784,128]{2,1,0:T(8,128)(2,1)S(1)} %collective-permute-done.6.refs_5_) | copy-start | bytes 1204228
  54.9 26.6 %copy-start.1 = (bf16[2,784,128]{2,1,0:T(8,128)(2,1)}, bf16[2,784,128]{2,1,0:T(8,128)(2,1)S(1)}, u32[]{:S(2)}) copy-start(bf16[2,784,128]{2,1,0:T(8,128)(2,1)S(1)} %collective-permute-done.7.refs_6_) | copy-start | bytes 1204228
  55.7 44.8 %collective-permute-start.8 = (bf16[10,784,128]{2,1,0:T(8,128)(2,1)}, bf16[10,784,128]{2,1,0:T(8,128)(2,1)}, u32[]{:S(2)}, u32[]{:S(2)}) collective-permute-start(bf16[10,784,128]{2,1,0:T(8,128)(2,1)} %constant_dynamic-update-slice_fusion.2), channel_id=1, source_target_pairs={{0,1},{1,0},{2,3},{3,2},{4,5},{5,4},{6,7},{7,6},{8,9},{9,8},{10,11... | collective-permute-start | bytes 6021128 | tf_op jit(solution)/shard_map/ppermute | solution.py:51
  58.7 8.9 %collective-permute-start.11 = (bf16[2,784,128]{2,1,0:T(8,128)(2,1)S(1)}, bf16[2,784,128]{2,1,0:T(8,128)(2,1)S(1)}, u32[]{:S(2)}, u32[]{:S(2)}) collective-permute-start(bf16[2,784,128]{2,1,0:T(8,128)(2,1)S(1)} %collective-permute-done.6.refs_5_), channel_id=1, source_target_pairs={{0,2},{1,15},{2,4},{3,1},{4,6},{5,3},{6,8},{7,5},{8,10},{9,7},{10,... | collective-permute-start | bytes 1204232 | tf_op jit(solution)/shard_map/ppermute | solution.py:51
  62.2 10.1 %collective-permute-start.12 = (bf16[1,784,128]{2,1,0:T(8,128)(2,1)S(1)}, bf16[1,784,128]{2,1,0:T(8,128)(2,1)S(1)}, u32[]{:S(2)}, u32[]{:S(2)}) collective-permute-start(bf16[1,784,128]{2,1,0:T(8,128)(2,1)S(1)} %slice.18), channel_id=1, source_target_pairs={{0,2},{1,15},{2,4},{3,1},{4,6},{5,3},{6,8},{7,5},{8,10},{9,7},{10,... | collective-permute-start | bytes 602120 | tf_op jit(solution)/shard_map/ppermute | solution.py:51
  67.6 13.9 %copy-start.2 = (bf16[2,784,128]{2,1,0:T(8,128)(2,1)}, bf16[2,784,128]{2,1,0:T(8,128)(2,1)S(1)}, u32[]{:S(2)}) copy-start(bf16[2,784,128]{2,1,0:T(8,128)(2,1)S(1)} %collective-permute-done.11.refs_0_) | copy-start | bytes 1204228
  67.6 7.4 %collective-permute-start.13 = (bf16[1,784,128]{2,1,0:T(8,128)(2,1)S(1)}, bf16[1,784,128]{2,1,0:T(8,128)(2,1)S(1)}, u32[]{:S(2)}, u32[]{:S(2)}) collective-permute-start(bf16[1,784,128]{2,1,0:T(8,128)(2,1)S(1)} %slice.19), channel_id=1, source_target_pairs={{0,2},{1,15},{2,4},{3,1},{4,6},{5,3},{6,8},{7,5},{8,10},{9,7},{10,... | collective-permute-start | bytes 602120 | tf_op jit(solution)/shard_map/ppermute | solution.py:51
  72.3 36.9 %copy-start.11 = (bf16[1,784,128]{2,1,0:T(8,128)(2,1)}, bf16[1,784,128]{2,1,0:T(8,128)(2,1)S(1)}, u32[]{:S(2)}) copy-start(bf16[1,784,128]{2,1,0:T(8,128)(2,1)S(1)} %collective-permute-done.12.refs_1_) | copy-start | bytes 602116
  75.0 34.3 %copy-start.12 = (bf16[1,784,128]{2,1,0:T(8,128)(2,1)}, bf16[1,784,128]{2,1,0:T(8,128)(2,1)S(1)}, u32[]{:S(2)}) copy-start(bf16[1,784,128]{2,1,0:T(8,128)(2,1)S(1)} %collective-permute-done.13.refs_2_) | copy-start | bytes 602116
  76.0 33.3 %collective-permute-start.14 = (bf16[4,784,128]{2,1,0:T(8,128)(2,1)}, bf16[4,784,128]{2,1,0:T(8,128)(2,1)}, u32[]{:S(2)}, u32[]{:S(2)}) collective-permute-start(bf16[4,784,128]{2,1,0:T(8,128)(2,1)} %pad_maximum_fusion), channel_id=1, source_target_pairs={{0,1},{1,0},{2,3},{3,2},{4,5},{5,4},{6,7},{7,6},{8,9},{9,8},{10,11... | collective-permute-start | bytes 2408456 | tf_op jit(solution)/shard_map/ppermute | solution.py:51
  81.4 19.1 %copy-start = (bf16[8,512,128]{2,1,0:T(8,128)(2,1)}, bf16[8,512,128]{2,1,0:T(8,128)(2,1)S(1)}, u32[]{:S(2)}) copy-start(bf16[8,512,128]{2,1,0:T(8,128)(2,1)S(1)} %all-to-all-done) | copy-start | bytes 3145732
  81.5 18.0 %collective-permute-start.9 = (bf16[4,512,128]{2,1,0:T(8,128)(2,1)S(1)}, bf16[4,512,128]{2,1,0:T(8,128)(2,1)S(1)}, u32[]{:S(2)}, u32[]{:S(2)}) collective-permute-start(bf16[4,512,128]{2,1,0:T(8,128)(2,1)S(1)} %get-tuple-element.6), channel_id=1, source_target_pairs={{0,32},{32,64},{64,96},{96,128},{128,160},{160,192},{192,224},{224... | collective-permute-start | bytes 1572872 | tf_op jit(solution)/shard_map/ppermute | solution.py:51
  84.6 15.8 %collective-permute-start.10 = (bf16[4,512,128]{2,1,0:T(8,128)(2,1)S(1)}, bf16[4,512,128]{2,1,0:T(8,128)(2,1)S(1)}, u32[]{:S(2)}, u32[]{:S(2)}) collective-permute-start(bf16[4,512,128]{2,1,0:T(8,128)(2,1)S(1)} %get-tuple-element.5), channel_id=1, source_target_pairs={{0,224},{32,0},{64,32},{96,64},{128,96},{160,128},{192,160},{224,1... | collective-permute-start | bytes 1572872 | tf_op jit(solution)/shard_map/ppermute | solution.py:51
  99.6 0.9 copy-start.3
  100.5 0.8 copy-start.4

commit v3 on v1

--- a/solution.py
+++ b/solution.py
@@ -66,7 +66,6 @@
     ]
     for copy in (*list_rows, metric_copy, *piece_copies):
         copy.start()
-    prepare()
     for copy in list_rows:
         copy.wait()
     for i in range(rows_v.shape[0]):
@@ -74,6 +73,7 @@
         list_v[i : i + 1, :] = rows[:1].astype(jnp.int32)
     list_copy = pltpu.make_async_copy(list_v, list_s, sems.at[0, len(piece_refs)])
     list_copy.start()
+    prepare()
     list_copy.wait()
     metric_copy.wait()
 
@@ -91,7 +91,7 @@
 
     for copy, start, ref in zip(piece_copies, starts, piece_refs):
         copy.wait()
-        lax.fori_loop(start, start + ref.shape[0], one_piece, 0)
+        lax.fori_loop(start, start + ref.shape[0], one_piece, 0, unroll=min(2, ref.shape[0]))
 
 
 def early_products(metric_ref, *refs):
@@ -104,24 +104,24 @@
 
 
 def late_products(early_ref, metric_ref, *refs):
-    *piece_refs, out_ref, total, metric_v, pieces_v, rows_v, list_v, list_s, sems = refs
-
-    def take():
-        total[...] = early_ref[...]
-
-    add_products(metric_ref, piece_refs, total, metric_v, pieces_v, rows_v, list_v, list_s, sems, take)
-    for p in range(PAIR_BLOCKS):
-        out_ref[p * BLK : (p + 1) * BLK, :] = total[p]
-
-
-def kernel_call(body, out_shape, taken, metric, pieces, scratch):
-    vmem = pl.BlockSpec(memory_space=pltpu.VMEM)
+    *piece_refs, out_ref, total, total_sem, metric_v, pieces_v, rows_v, list_v, list_s, sems = refs
+    taken = pltpu.make_async_copy(early_ref, total, total_sem)
+    taken.start()
+    add_products(
+        metric_ref, piece_refs, total, metric_v, pieces_v, rows_v, list_v, list_s, sems, taken.wait
+    )
+    given = pltpu.make_async_copy(total.at[:PAIR_BLOCKS], out_ref, total_sem)
+    given.start()
+    given.wait()
+
+
+def kernel_call(body, out_shape, out_space, taken, metric, pieces, scratch):
     count = sum(piece.shape[0] for piece in pieces)
     return pl.pallas_call(
         body,
         out_shape=out_shape,
-        in_specs=[vmem] * len(taken) + [pl.BlockSpec(memory_space=pltpu.HBM)] * (1 + len(pieces)),
-        out_specs=vmem,
+        in_specs=[pl.BlockSpec(memory_space=pltpu.HBM)] * (len(taken) + 1 + len(pieces)),
+        out_specs=pl.BlockSpec(memory_space=out_space),
         scratch_shapes=[
             *scratch,
             pltpu.VMEM(metric.shape, metric.dtype),
@@ -135,12 +135,30 @@
     )(*taken, metric, *pieces)
 
 
+def copy_to_each(source_ref, copies_ref, source_v, sems):
+    count = copies_ref.shape[0]
+    taken = pltpu.make_async_copy(source_ref, source_v, sems.at[count])
+    taken.start()
+    taken.wait()
+    copies = [pltpu.make_async_copy(source_v, copies_ref.at[i], sems.at[i]) for i in range(count)]
+    for copy in copies:
+        copy.start()
+    for copy in copies:
+        copy.wait()
+
+
 def on_device(slots, block_list, metric):
     out_cols = metric.shape[1]
     rows = lax.axis_size("row")
     band_blocks = rows * metric.shape[0] // BLK
     col_blocks = band_blocks // lax.axis_size("col")
-    copies = jnp.broadcast_to(metric, (rows, *metric.shape))
+    copies = pl.pallas_call(
+        copy_to_each,
+        out_shape=jax.ShapeDtypeStruct((rows, *metric.shape), metric.dtype),
+        in_specs=[pl.BlockSpec(memory_space=pltpu.HBM)],
+        out_specs=pl.BlockSpec(memory_space=pltpu.HBM),
+        scratch_shapes=[pltpu.VMEM(metric.shape, metric.dtype), pltpu.SemaphoreType.DMA((rows + 1,))],
+    )(metric)
     band = lax.all_to_all(copies, "row", split_axis=0, concat_axis=0, tiled=True)
     band = band.reshape(band_blocks, BLK, out_cols)
 
@@ -162,16 +180,24 @@
     late = [*late, late_other]
     total_shape = (PAIR_BLOCKS + 1, BLK, out_cols)
     total = kernel_call(
-        early_products, jax.ShapeDtypeStruct(total_shape, jnp.float32), [], band, early, []
-    )
-    return kernel_call(
+        early_products,
+        jax.ShapeDtypeStruct(total_shape, jnp.float32),
+        pltpu.VMEM,
+        [],
+        band,
+        early,
+        [],
+    )
+    blocks = kernel_call(
         late_products,
-        jax.ShapeDtypeStruct((PAIR_DEV, out_cols), jnp.float32),
+        jax.ShapeDtypeStruct((PAIR_BLOCKS, BLK, out_cols), jnp.float32),
+        pltpu.HBM,
         [total],
         band,
         late,
-        [pltpu.VMEM(total_shape, jnp.float32)],
-    )
+        [pltpu.VMEM(total_shape, jnp.float32), pltpu.SemaphoreType.DMA],
+    )
+    return blocks.reshape(PAIR_DEV, out_cols)
 
 
 def solution(mesh):

time: 103 us -> 99.9 us (0.970)
  local copies, waits for them, and re-layouts: 4.33 us -> 1.69 us
    broadcast_in_dim x1 -> x0, local copies, waits for them, and re-layouts: 2.65 us -> none  [on_device(): copies = jnp.broadcast_to(metric, (rows, *metric.shape))]
    pallas_call x2 -> x3, Pallas kernels: 13.2 us -> 12.6 us  [the longest x2 10.2 us: kernel_call(): pl.pallas_call(body, out_shape=out_shape, in_specs=[pl.BlockSpec(memory_s...]
  transfers between devices with their start and end apart: 14 -> 14, of which waited for: 7 -> 7; matrix products, arithmetic and copies ran while one was open for 1% -> 1% of each run, Pallas kernels for 8% -> 6%
where the time goes in v3:
time: 99.9 us; the launch traced here: 99.3 us
  starting transfers between devices  59 us (59%)
  waiting for transfers between devices  24.6 us (25%)
  Pallas kernels  12.6 us (13%)
  local copies, waits for them, and re-layouts  1.69 us (2%)
  other arithmetic  1.16 us (1%)
    ppermute x13, starting transfers between devices, sent(): return lax.ppermute(value, axis, perm)  45.4 us
    ppermute x13, waiting for transfers between devices, sent(): return lax.ppermute(value, axis, perm)  24.6 us
    all_to_all x1, starting transfers between devices, on_device(): lax.all_to_all(copies, 'row', split_axis=0, concat_axis=0, tiled=True)  13.6 us
    pallas_call x2, Pallas kernels, kernel_call(): pl.pallas_call(body, out_shape=out_shape, in_specs=[pl.BlockSpec(memory_s...  10.2 us
    pallas_call x1, Pallas kernels, on_device(): pl.pallas_call(copy_to_each, out_shape=jax.ShapeDtypeStruct((rows, *metri...  2.4 us
  transfers between devices with their start and end apart: 14, of which 7 were waited for; matrix products, arithmetic and copies ran while one was open for 1% of the time, Pallas kernels for 6%

profile of v3, /device:TPU:1, one launch (start us, length us, event | category | flops | bytes accessed | tf_op | source)
XLA Modules:
  0.0 99.3 jit_solution(11647727469501734224)
XLA Ops:
  0.0 2.4 %shard_map.37 = bf16[16,512,128]{2,1,0:T(8,128)(2,1)} custom-call(bf16[512,128]{1,0:T(8,128)(2,1)} %source_ref.1), custom_call_target="tpu_custom_call" | custom-call | tf_op jit(solution)/shard_map/pallas_call | solution.py:155
  2.4 0.0 copy-start.12
  2.4 0.0 copy-start.11
  2.4 13.6 %all-to-all-start = ((bf16[16,512,128]{2,1,0:T(8,128)(2,1)}), bf16[16,512,128]{2,1,0:T(8,128)(2,1)S(1)}, u32[]{:S(2)}, u32[]{:S(2)}) async-start(bf16[16,512,128]{2,1,0:T(8,128)(2,1)} %shard_map.37), calls=%async_computation | async-start | bytes 4194304 | tf_op jit(solution)/shard_map/all_to_all | solution.py:162
  16.0 0.0 copy-done.12
  16.0 0.1 fusion.3
  16.1 0.0 copy-done.11
  16.1 2.9 %collective-permute-start = (bf16[1,784,128]{2,1,0:T(8,128)(2,1)S(1)}, bf16[1,784,128]{2,1,0:T(8,128)(2,1)S(1)}, u32[]{:S(2)}, u32[]{:S(2)}) collective-permute-start(bf16[1,784,128]{2,1,0:T(8,128)(2,1)S(1)} %maximum_bitcast_fusion), channel_id=1, source_target_pairs={{0,1},{1,0},{2,3},{3,2},{4,5},{5,4},{6,7},{7,6},{8,9},{9,8},{10,11... | collective-permute-start | bytes 602120 | tf_op jit(solution)/shard_map/ppermute | solution.py:37
  19.0 2.2 %collective-permute-start.1 = (bf16[1,784,128]{2,1,0:T(8,128)(2,1)S(1)}, bf16[1,784,128]{2,1,0:T(8,128)(2,1)S(1)}, u32[]{:S(2)}, u32[]{:S(2)}) collective-permute-start(bf16[1,784,128]{2,1,0:T(8,128)(2,1)S(1)} %maximum_bitcast_fusion), channel_id=1, source_target_pairs={{0,16},{1,17},{2,18},{3,19},{4,20},{5,21},{6,22},{7,23},{8,24},{9,... | collective-permute-start | bytes 602120 | tf_op jit(solution)/shard_map/ppermute | solution.py:37
  21.2 0.0 collective-permute-done
  21.3 0.0 copy-start.2
  21.3 5.1 %collective-permute-start.3 = (bf16[2,784,128]{2,1,0:T(8,128)(2,1)S(1)}, bf16[2,784,128]{2,1,0:T(8,128)(2,1)S(1)}, u32[]{:S(2)}, u32[]{:S(2)}) collective-permute-start(bf16[2,784,128]{2,1,0:T(8,128)(2,1)S(1)} %pad_maximum_fusion.1.refs_0_), channel_id=1, source_target_pairs={{0,2},{1,15},{2,4},{3,1},{4,6},{5,3},{6,8},{7,5},{8,10},{9,7},{10,... | collective-permute-start | bytes 1204232 | tf_op jit(solution)/shard_map/ppermute | solution.py:37
  26.4 6.2 %collective-permute-done.1 = bf16[1,784,128]{2,1,0:T(8,128)(2,1)S(1)} collective-permute-done((bf16[1,784,128]{2,1,0:T(8,128)(2,1)S(1)}, bf16[1,784,128]{2,1,0:T(8,128)(2,1)S(1)}, u32[]{:S(2)}, u32[]{:S(2)}) %collective-permute-start.1) | collective-permute-done | bytes 200736 | tf_op jit(solution)/shard_map/ppermute | solution.py:37
  32.6 2.3 %collective-permute-start.2 = (bf16[1,784,128]{2,1,0:T(8,128)(2,1)S(1)}, bf16[1,784,128]{2,1,0:T(8,128)(2,1)S(1)}, u32[]{:S(2)}, u32[]{:S(2)}) collective-permute-start(bf16[1,784,128]{2,1,0:T(8,128)(2,1)S(1)} %collective-permute-done.1), channel_id=1, source_target_pairs={{0,1},{1,0},{2,3},{3,2},{4,5},{5,4},{6,7},{7,6},{8,9},{9,8},{10,11... | collective-permute-start | bytes 602120 | tf_op jit(solution)/shard_map/ppermute | solution.py:37
  35.0 1.0 %collective-permute-done.2 = bf16[1,784,128]{2,1,0:T(8,128)(2,1)S(1)} collective-permute-done((bf16[1,784,128]{2,1,0:T(8,128)(2,1)S(1)}, bf16[1,784,128]{2,1,0:T(8,128)(2,1)S(1)}, u32[]{:S(2)}, u32[]{:S(2)}) %collective-permute-start.2) | collective-permute-done | bytes 200736 | tf_op jit(solution)/shard_map/ppermute | solution.py:37
  36.0 0.0 copy-start.8
  36.0 5.1 %collective-permute-start.4 = (bf16[2,784,128]{2,1,0:T(8,128)(2,1)S(1)}, bf16[2,784,128]{2,1,0:T(8,128)(2,1)S(1)}, u32[]{:S(2)}, u32[]{:S(2)}) collective-permute-start(bf16[2,784,128]{2,1,0:T(8,128)(2,1)S(1)} %constant_dynamic-update-slice_fusion.refs_1_), channel_id=1, source_target_pairs={{0,2},{1,15},{2,4},{3,1},{4,6},{5,3},{6,8},{7,5},{8,10},{9,7},{10,... | collective-permute-start | bytes 1204232 | tf_op jit(solution)/shard_map/ppermute | solution.py:37
  41.1 0.0 collective-permute-done.3.refs_2_
  41.2 0.0 copy-start.3
  41.2 3.0 %collective-permute-start.5 = (bf16[2,784,128]{2,1,0:T(8,128)(2,1)S(1)}, bf16[2,784,128]{2,1,0:T(8,128)(2,1)S(1)}, u32[]{:S(2)}, u32[]{:S(2)}) collective-permute-start(bf16[2,784,128]{2,1,0:T(8,128)(2,1)S(1)} %collective-permute-done.3.refs_2_), channel_id=1, source_target_pairs={{0,2},{1,15},{2,4},{3,1},{4,6},{5,3},{6,8},{7,5},{8,10},{9,7},{10,... | collective-permute-start | bytes 1204232 | tf_op jit(solution)/shard_map/ppermute | solution.py:37
  44.2 1.8 %collective-permute-done.4.refs_3_ = bf16[2,784,128]{2,1,0:T(8,128)(2,1)S(1)} collective-permute-done((bf16[2,784,128]{2,1,0:T(8,128)(2,1)S(1)}, bf16[2,784,128]{2,1,0:T(8,128)(2,1)S(1)}, u32[]{:S(2)}, u32[]{:S(2)}) %collective-permute-start.4) | collective-permute-done | bytes 401440 | tf_op jit(solution)/shard_map/ppermute | solution.py:37
  45.9 5.0 %collective-permute-start.6 = (bf16[2,784,128]{2,1,0:T(8,128)(2,1)S(1)}, bf16[2,784,128]{2,1,0:T(8,128)(2,1)S(1)}, u32[]{:S(2)}, u32[]{:S(2)}) collective-permute-start(bf16[2,784,128]{2,1,0:T(8,128)(2,1)S(1)} %collective-permute-done.4.refs_3_), channel_id=1, source_target_pairs={{0,2},{1,15},{2,4},{3,1},{4,6},{5,3},{6,8},{7,5},{8,10},{9,7},{10,... | collective-permute-start | bytes 1204232 | tf_op jit(solution)/shard_map/ppermute | solution.py:37
  51.0 0.0 collective-permute-done.5.refs_4_
  51.0 4.6 %collective-permute-start.7 = (bf16[2,784,128]{2,1,0:T(8,128)(2,1)S(1)}, bf16[2,784,128]{2,1,0:T(8,128)(2,1)S(1)}, u32[]{:S(2)}, u32[]{:S(2)}) collective-permute-start(bf16[2,784,128]{2,1,0:T(8,128)(2,1)S(1)} %collective-permute-done.5.refs_4_), channel_id=1, source_target_pairs={{0,2},{1,15},{2,4},{3,1},{4,6},{5,3},{6,8},{7,5},{8,10},{9,7},{10,... | collective-permute-start | bytes 1204232 | tf_op jit(solution)/shard_map/ppermute | solution.py:37
  55.6 0.1 constant_dynamic-update-slice_fusion.5
  55.7 0.1 constant_dynamic-update-slice_fusion.4
  55.7 0.0 collective-permute-done.6.refs_5_
  55.7 0.1 constant_dynamic-update-slice_fusion.3
  55.8 4.5 %collective-permute-done.7.refs_6_ = bf16[2,784,128]{2,1,0:T(8,128)(2,1)S(1)} collective-permute-done((bf16[2,784,128]{2,1,0:T(8,128)(2,1)S(1)}, bf16[2,784,128]{2,1,0:T(8,128)(2,1)S(1)}, u32[]{:S(2)}, u32[]{:S(2)}) %collective-permute-start.7) | collective-permute-done | bytes 401440 | tf_op jit(solution)/shard_map/ppermute | solution.py:37
  60.3 0.1 constant_dynamic-update-slice_fusion.2
  60.4 0.0 copy-done.3
  60.4 0.0 copy-done.4
  60.4 0.0 copy-done.5
  60.4 4.5 %collective-permute-start.8 = (bf16[10,784,128]{2,1,0:T(8,128)(2,1)S(1)}, bf16[10,784,128]{2,1,0:T(8,128)(2,1)}, u32[]{:S(2)}, u32[]{:S(2)}) collective-permute-start(bf16[10,784,128]{2,1,0:T(8,128)(2,1)S(1)} %constant_dynamic-update-slice_fusion.2), channel_id=1, source_target_pairs={{0,1},{1,0},{2,3},{3,2},{4,5},{5,4},{6,7},{7,6},{8,9},{9,8},{10,11... | collective-permute-start | bytes 6021128 | tf_op jit(solution)/shard_map/ppermute | solution.py:37
  64.9 2.8 %collective-permute-start.10 = (bf16[1,784,128]{2,1,0:T(8,128)(2,1)S(1)}, bf16[1,784,128]{2,1,0:T(8,128)(2,1)S(1)}, u32[]{:S(2)}, u32[]{:S(2)}) collective-permute-start(bf16[1,784,128]{2,1,0:T(8,128)(2,1)S(1)} %slice.4), channel_id=1, source_target_pairs={{0,2},{1,15},{2,4},{3,1},{4,6},{5,3},{6,8},{7,5},{8,10},{9,7},{10,... | collective-permute-start | bytes 602120 | tf_op jit(solution)/shard_map/ppermute | solution.py:37
  67.7 2.9 %collective-permute-start.9 = (bf16[2,784,128]{2,1,0:T(8,128)(2,1)S(1)}, bf16[2,784,128]{2,1,0:T(8,128)(2,1)S(1)}, u32[]{:S(2)}, u32[]{:S(2)}) collective-permute-start(bf16[2,784,128]{2,1,0:T(8,128)(2,1)S(1)} %collective-permute-done.7.refs_6_), channel_id=1, source_target_pairs={{0,16},{1,17},{2,18},{3,19},{4,20},{5,21},{6,22},{7,23},{8,24},{9,... | collective-permute-start | bytes 1204232 | tf_op jit(solution)/shard_map/ppermute | solution.py:37
  70.6 1.0 %collective-permute-done.10.refs_1_ = bf16[1,784,128]{2,1,0:T(8,128)(2,1)S(1)} collective-permute-done((bf16[1,784,128]{2,1,0:T(8,128)(2,1)S(1)}, bf16[1,784,128]{2,1,0:T(8,128)(2,1)S(1)}, u32[]{:S(2)}, u32[]{:S(2)}) %collective-permute-start.10) | collective-permute-done | bytes 200736 | tf_op jit(solution)/shard_map/ppermute | solution.py:37
  71.7 2.9 %collective-permute-start.11 = (bf16[1,784,128]{2,1,0:T(8,128)(2,1)S(1)}, bf16[1,784,128]{2,1,0:T(8,128)(2,1)S(1)}, u32[]{:S(2)}, u32[]{:S(2)}) collective-permute-start(bf16[1,784,128]{2,1,0:T(8,128)(2,1)S(1)} %collective-permute-done.10.refs_1_), channel_id=1, source_target_pairs={{0,16},{1,17},{2,18},{3,19},{4,20},{5,21},{6,22},{7,23},{8,24},{9,... | collective-permute-start | bytes 602120 | tf_op jit(solution)/shard_map/ppermute | solution.py:37
  74.6 6.3 %collective-permute-done.9.refs_0_ = bf16[2,784,128]{2,1,0:T(8,128)(2,1)S(1)} collective-permute-done((bf16[2,784,128]{2,1,0:T(8,128)(2,1)S(1)}, bf16[2,784,128]{2,1,0:T(8,128)(2,1)S(1)}, u32[]{:S(2)}, u32[]{:S(2)}) %collective-permute-start.9) | collective-permute-done | bytes 401440 | tf_op jit(solution)/shard_map/ppermute | solution.py:37
  80.9 3.6 %collective-permute-done.11.refs_2_ = bf16[1,784,128]{2,1,0:T(8,128)(2,1)S(1)} collective-permute-done((bf16[1,784,128]{2,1,0:T(8,128)(2,1)S(1)}, bf16[1,784,128]{2,1,0:T(8,128)(2,1)S(1)}, u32[]{:S(2)}, u32[]{:S(2)}) %collective-permute-start.11) | collective-permute-done | bytes 200736 | tf_op jit(solution)/shard_map/ppermute | solution.py:37
  84.5 1.0 %pad_maximum_fusion = bf16[4,784,128]{2,1,0:T(8,128)(2,1)} fusion(bf16[1,784,128]{2,1,0:T(8,128)(2,1)S(1)} %collective-permute-done.11.refs_2_, bf16[1,784,128]{2,1,0:T(8,128)(2,1)S(1)} %collective-permute-done.10.refs_1_, bf16[2,784,128]{2,1,0:T(8,128)(2,1)S(1)} %collective-permute-done.9.refs_0_), kind=kLoop, calls=%fused_computation | loop fusion | flops 802816 | bytes 1605632 | tf_op jit(solution)/shard_map/concatenate | solution.py:178
  85.5 2.2 %collective-permute-start.12 = (bf16[4,784,128]{2,1,0:T(8,128)(2,1)}, bf16[4,784,128]{2,1,0:T(8,128)(2,1)}, u32[]{:S(2)}, u32[]{:S(2)}) collective-permute-start(bf16[4,784,128]{2,1,0:T(8,128)(2,1)} %pad_maximum_fusion), channel_id=1, source_target_pairs={{0,1},{1,0},{2,3},{3,2},{4,5},{5,4},{6,7},{7,6},{8,9},{9,8},{10,11... | collective-permute-start | bytes 2408456 | tf_op jit(solution)/shard_map/ppermute | solution.py:37
  87.7 0.0 collective-permute-done.8.refs_7_
  87.8 0.0 all-to-all-done
  87.8 1.3 %copy-done = bf16[16,512,128]{2,1,0:T(8,128)(2,1)} copy-done((bf16[16,512,128]{2,1,0:T(8,128)(2,1)}, bf16[16,512,128]{2,1,0:T(8,128)(2,1)S(1)}, u32[]{:S(2)}) %copy-start) | copy-done | bytes 2097176
  89.1 6.1 %shard_map.38.early_ref = f32[9,128,128]{2,1,0:T(8,128)} custom-call(bf16[64,128,128]{2,1,0:T(8,128)(2,1)} %bitcast.5, bf16[2,784,128]{2,1,0:T(8,128)(2,1)} %copy-done.2, bf16[2,784,128]{2,1,0:T(8,128)(2,1)} %copy-done.8, bf16[2,784,128]{2,1,0:T(8,128)(2,1)} %copy-done.3, bf16[2,784,128]{2,1,0:T(8,128)(2,1)} %copy-done.4, bf16[2,784,128]{2,1,0:T(8,128)(2,1)} %copy-done.5, ...), custom_call_target="tpu_custom_call" | custom-call | tf_op jit(solution)/shard_map/pallas_call | solution.py:120
  95.2 0.0 collective-permute-done.12.refs_3_
  95.2 4.1 %shard_map.39 = f32[8,128,128]{2,1,0:T(8,128)} custom-call(f32[9,128,128]{2,1,0:T(8,128)} %shard_map.38.early_ref, bf16[64,128,128]{2,1,0:T(8,128)(2,1)} %bitcast.6, bf16[2,784,128]{2,1,0:T(8,128)(2,1)} %copy-done.7, bf16[1,784,128]{2,1,0:T(8,128)(2,1)} %copy-done.9, bf16[1,784,128]{2,1,0:T(8,128)(2,1)} %copy-done.10, ...), custom_call_target="tpu_custom_call" | custom-call | tf_op jit(solution)/shard_map/pallas_call | solution.py:120
  (23 shorter events, 0.2 us)
Async XLA Ops:
  2.4 13.6 %copy-start.12 = (s32[6]{0:T(128)S(1)}, s32[6]{0:T(128)}, u32[]{:S(2)}) copy-start(s32[6]{0:T(128)} %param.4) | copy-start | bytes 76
  2.4 13.7 %copy-start.11 = (bf16[6,128,128]{2,1,0:T(8,128)(2,1)S(1)}, bf16[6,128,128]{2,1,0:T(8,128)(2,1)}, u32[]{:S(2)}) copy-start(bf16[6,128,128]{2,1,0:T(8,128)(2,1)} %param.3) | copy-start | bytes 589828
  2.4 85.3 %all-to-all-start = ((bf16[16,512,128]{2,1,0:T(8,128)(2,1)}), bf16[16,512,128]{2,1,0:T(8,128)(2,1)S(1)}, u32[]{:S(2)}, u32[]{:S(2)}) async-start(bf16[16,512,128]{2,1,0:T(8,128)(2,1)} %shard_map.37), calls=%async_computation | async-start | bytes 4194304 | tf_op jit(solution)/shard_map/all_to_all | solution.py:162
  16.1 5.1 %collective-permute-start = (bf16[1,784,128]{2,1,0:T(8,128)(2,1)S(1)}, bf16[1,784,128]{2,1,0:T(8,128)(2,1)S(1)}, u32[]{:S(2)}, u32[]{:S(2)}) collective-permute-start(bf16[1,784,128]{2,1,0:T(8,128)(2,1)S(1)} %maximum_bitcast_fusion), channel_id=1, source_target_pairs={{0,1},{1,0},{2,3},{3,2},{4,5},{5,4},{6,7},{7,6},{8,9},{9,8},{10,11... | collective-permute-start | bytes 602120 | tf_op jit(solution)/shard_map/ppermute | solution.py:37
  19.0 13.6 %collective-permute-start.1 = (bf16[1,784,128]{2,1,0:T(8,128)(2,1)S(1)}, bf16[1,784,128]{2,1,0:T(8,128)(2,1)S(1)}, u32[]{:S(2)}, u32[]{:S(2)}) collective-permute-start(bf16[1,784,128]{2,1,0:T(8,128)(2,1)S(1)} %maximum_bitcast_fusion), channel_id=1, source_target_pairs={{0,16},{1,17},{2,18},{3,19},{4,20},{5,21},{6,22},{7,23},{8,24},{9,... | collective-permute-start | bytes 602120 | tf_op jit(solution)/shard_map/ppermute | solution.py:37
  21.3 34.5 %copy-start.2 = (bf16[2,784,128]{2,1,0:T(8,128)(2,1)}, bf16[2,784,128]{2,1,0:T(8,128)(2,1)S(1)}, u32[]{:S(2)}) copy-start(bf16[2,784,128]{2,1,0:T(8,128)(2,1)S(1)} %pad_maximum_fusion.1.refs_0_) | copy-start | bytes 1204228
  21.3 19.8 %collective-permute-start.3 = (bf16[2,784,128]{2,1,0:T(8,128)(2,1)S(1)}, bf16[2,784,128]{2,1,0:T(8,128)(2,1)S(1)}, u32[]{:S(2)}, u32[]{:S(2)}) collective-permute-start(bf16[2,784,128]{2,1,0:T(8,128)(2,1)S(1)} %pad_maximum_fusion.1.refs_0_), channel_id=1, source_target_pairs={{0,2},{1,15},{2,4},{3,1},{4,6},{5,3},{6,8},{7,5},{8,10},{9,7},{10,... | collective-permute-start | bytes 1204232 | tf_op jit(solution)/shard_map/ppermute | solution.py:37
  32.6 3.4 %collective-permute-start.2 = (bf16[1,784,128]{2,1,0:T(8,128)(2,1)S(1)}, bf16[1,784,128]{2,1,0:T(8,128)(2,1)S(1)}, u32[]{:S(2)}, u32[]{:S(2)}) collective-permute-start(bf16[1,784,128]{2,1,0:T(8,128)(2,1)S(1)} %collective-permute-done.1), channel_id=1, source_target_pairs={{0,1},{1,0},{2,3},{3,2},{4,5},{5,4},{6,7},{7,6},{8,9},{9,8},{10,11... | collective-permute-start | bytes 602120 | tf_op jit(solution)/shard_map/ppermute | solution.py:37
  36.0 14.9 %copy-start.8 = (bf16[2,784,128]{2,1,0:T(8,128)(2,1)}, bf16[2,784,128]{2,1,0:T(8,128)(2,1)S(1)}, u32[]{:S(2)}) copy-start(bf16[2,784,128]{2,1,0:T(8,128)(2,1)S(1)} %constant_dynamic-update-slice_fusion.refs_1_) | copy-start | bytes 1204228
  36.0 9.9 %collective-permute-start.4 = (bf16[2,784,128]{2,1,0:T(8,128)(2,1)S(1)}, bf16[2,784,128]{2,1,0:T(8,128)(2,1)S(1)}, u32[]{:S(2)}, u32[]{:S(2)}) collective-permute-start(bf16[2,784,128]{2,1,0:T(8,128)(2,1)S(1)} %constant_dynamic-update-slice_fusion.refs_1_), channel_id=1, source_target_pairs={{0,2},{1,15},{2,4},{3,1},{4,6},{5,3},{6,8},{7,5},{8,10},{9,7},{10,... | collective-permute-start | bytes 1204232 | tf_op jit(solution)/shard_map/ppermute | solution.py:37
  41.2 19.2 %copy-start.3 = (bf16[2,784,128]{2,1,0:T(8,128)(2,1)}, bf16[2,784,128]{2,1,0:T(8,128)(2,1)S(1)}, u32[]{:S(2)}) copy-start(bf16[2,784,128]{2,1,0:T(8,128)(2,1)S(1)} %collective-permute-done.3.refs_2_) | copy-start | bytes 1204228
  41.2 9.8 %collective-permute-start.5 = (bf16[2,784,128]{2,1,0:T(8,128)(2,1)S(1)}, bf16[2,784,128]{2,1,0:T(8,128)(2,1)S(1)}, u32[]{:S(2)}, u32[]{:S(2)}) collective-permute-start(bf16[2,784,128]{2,1,0:T(8,128)(2,1)S(1)} %collective-permute-done.3.refs_2_), channel_id=1, source_target_pairs={{0,2},{1,15},{2,4},{3,1},{4,6},{5,3},{6,8},{7,5},{8,10},{9,7},{10,... | collective-permute-start | bytes 1204232 | tf_op jit(solution)/shard_map/ppermute | solution.py:37
  45.9 14.5 %copy-start.4 = (bf16[2,784,128]{2,1,0:T(8,128)(2,1)}, bf16[2,784,128]{2,1,0:T(8,128)(2,1)S(1)}, u32[]{:S(2)}) copy-start(bf16[2,784,128]{2,1,0:T(8,128)(2,1)S(1)} %collective-permute-done.4.refs_3_) | copy-start | bytes 1204228
  45.9 9.8 %collective-permute-start.6 = (bf16[2,784,128]{2,1,0:T(8,128)(2,1)S(1)}, bf16[2,784,128]{2,1,0:T(8,128)(2,1)S(1)}, u32[]{:S(2)}, u32[]{:S(2)}) collective-permute-start(bf16[2,784,128]{2,1,0:T(8,128)(2,1)S(1)} %collective-permute-done.4.refs_3_), channel_id=1, source_target_pairs={{0,2},{1,15},{2,4},{3,1},{4,6},{5,3},{6,8},{7,5},{8,10},{9,7},{10,... | collective-permute-start | bytes 1204232 | tf_op jit(solution)/shard_map/ppermute | solution.py:37
  51.0 9.4 %copy-start.5 = (bf16[2,784,128]{2,1,0:T(8,128)(2,1)}, bf16[2,784,128]{2,1,0:T(8,128)(2,1)S(1)}, u32[]{:S(2)}) copy-start(bf16[2,784,128]{2,1,0:T(8,128)(2,1)S(1)} %collective-permute-done.5.refs_4_) | copy-start | bytes 1204228
  51.0 9.4 %collective-permute-start.7 = (bf16[2,784,128]{2,1,0:T(8,128)(2,1)S(1)}, bf16[2,784,128]{2,1,0:T(8,128)(2,1)S(1)}, u32[]{:S(2)}, u32[]{:S(2)}) collective-permute-start(bf16[2,784,128]{2,1,0:T(8,128)(2,1)S(1)} %collective-permute-done.5.refs_4_), channel_id=1, source_target_pairs={{0,2},{1,15},{2,4},{3,1},{4,6},{5,3},{6,8},{7,5},{8,10},{9,7},{10,... | collective-permute-start | bytes 1204232 | tf_op jit(solution)/shard_map/ppermute | solution.py:37
  55.7 25.2 %copy-start.6 = (bf16[2,784,128]{2,1,0:T(8,128)(2,1)}, bf16[2,784,128]{2,1,0:T(8,128)(2,1)S(1)}, u32[]{:S(2)}) copy-start(bf16[2,784,128]{2,1,0:T(8,128)(2,1)S(1)} %collective-permute-done.6.refs_5_) | copy-start | bytes 1204228
  60.3 27.4 %copy-start.1 = (bf16[2,784,128]{2,1,0:T(8,128)(2,1)}, bf16[2,784,128]{2,1,0:T(8,128)(2,1)S(1)}, u32[]{:S(2)}) copy-start(bf16[2,784,128]{2,1,0:T(8,128)(2,1)S(1)} %collective-permute-done.7.refs_6_) | copy-start | bytes 1204228
  60.4 27.3 %collective-permute-start.8 = (bf16[10,784,128]{2,1,0:T(8,128)(2,1)S(1)}, bf16[10,784,128]{2,1,0:T(8,128)(2,1)}, u32[]{:S(2)}, u32[]{:S(2)}) collective-permute-start(bf16[10,784,128]{2,1,0:T(8,128)(2,1)S(1)} %constant_dynamic-update-slice_fusion.2), channel_id=1, source_target_pairs={{0,1},{1,0},{2,3},{3,2},{4,5},{5,4},{6,7},{7,6},{8,9},{9,8},{10,11... | collective-permute-start | bytes 6021128 | tf_op jit(solution)/shard_map/ppermute | solution.py:37
  64.9 6.8 %collective-permute-start.10 = (bf16[1,784,128]{2,1,0:T(8,128)(2,1)S(1)}, bf16[1,784,128]{2,1,0:T(8,128)(2,1)S(1)}, u32[]{:S(2)}, u32[]{:S(2)}) collective-permute-start(bf16[1,784,128]{2,1,0:T(8,128)(2,1)S(1)} %slice.4), channel_id=1, source_target_pairs={{0,2},{1,15},{2,4},{3,1},{4,6},{5,3},{6,8},{7,5},{8,10},{9,7},{10,... | collective-permute-start | bytes 602120 | tf_op jit(solution)/shard_map/ppermute | solution.py:37
  67.7 13.2 %collective-permute-start.9 = (bf16[2,784,128]{2,1,0:T(8,128)(2,1)S(1)}, bf16[2,784,128]{2,1,0:T(8,128)(2,1)S(1)}, u32[]{:S(2)}, u32[]{:S(2)}) collective-permute-start(bf16[2,784,128]{2,1,0:T(8,128)(2,1)S(1)} %collective-permute-done.7.refs_6_), channel_id=1, source_target_pairs={{0,16},{1,17},{2,18},{3,19},{4,20},{5,21},{6,22},{7,23},{8,24},{9,... | collective-permute-start | bytes 1204232 | tf_op jit(solution)/shard_map/ppermute | solution.py:37
  71.7 23.5 %copy-start.9 = (bf16[1,784,128]{2,1,0:T(8,128)(2,1)}, bf16[1,784,128]{2,1,0:T(8,128)(2,1)S(1)}, u32[]{:S(2)}) copy-start(bf16[1,784,128]{2,1,0:T(8,128)(2,1)S(1)} %collective-permute-done.10.refs_1_) | copy-start | bytes 602116
  71.7 12.9 %collective-permute-start.11 = (bf16[1,784,128]{2,1,0:T(8,128)(2,1)S(1)}, bf16[1,784,128]{2,1,0:T(8,128)(2,1)S(1)}, u32[]{:S(2)}, u32[]{:S(2)}) collective-permute-start(bf16[1,784,128]{2,1,0:T(8,128)(2,1)S(1)} %collective-permute-done.10.refs_1_), channel_id=1, source_target_pairs={{0,16},{1,17},{2,18},{3,19},{4,20},{5,21},{6,22},{7,23},{8,24},{9,... | collective-permute-start | bytes 602120 | tf_op jit(solution)/shard_map/ppermute | solution.py:37
  80.9 14.3 %copy-start.7 = (bf16[2,784,128]{2,1,0:T(8,128)(2,1)}, bf16[2,784,128]{2,1,0:T(8,128)(2,1)S(1)}, u32[]{:S(2)}) copy-start(bf16[2,784,128]{2,1,0:T(8,128)(2,1)S(1)} %collective-permute-done.9.refs_0_) | copy-start | bytes 1204228
  84.5 10.7 %copy-start.10 = (bf16[1,784,128]{2,1,0:T(8,128)(2,1)}, bf16[1,784,128]{2,1,0:T(8,128)(2,1)S(1)}, u32[]{:S(2)}) copy-start(bf16[1,784,128]{2,1,0:T(8,128)(2,1)S(1)} %collective-permute-done.11.refs_2_) | copy-start | bytes 602116
  85.5 9.7 %collective-permute-start.12 = (bf16[4,784,128]{2,1,0:T(8,128)(2,1)}, bf16[4,784,128]{2,1,0:T(8,128)(2,1)}, u32[]{:S(2)}, u32[]{:S(2)}) collective-permute-start(bf16[4,784,128]{2,1,0:T(8,128)(2,1)} %pad_maximum_fusion), channel_id=1, source_target_pairs={{0,1},{1,0},{2,3},{3,2},{4,5},{5,4},{6,7},{7,6},{8,9},{9,8},{10,11... | collective-permute-start | bytes 2408456 | tf_op jit(solution)/shard_map/ppermute | solution.py:37
  87.8 1.3 %copy-start = (bf16[16,512,128]{2,1,0:T(8,128)(2,1)}, bf16[16,512,128]{2,1,0:T(8,128)(2,1)S(1)}, u32[]{:S(2)}) copy-start(bf16[16,512,128]{2,1,0:T(8,128)(2,1)S(1)} %all-to-all-done) | copy-start | bytes 6291460

commit v4 on v3

--- a/solution.py
+++ b/solution.py
@@ -59,12 +59,15 @@
         pltpu.make_async_copy(ref.at[:, SLOT_ROWS:, :], rows_v.at[place], sems.at[0, n])
         for n, (ref, place) in enumerate(zip(piece_refs, places))
     ]
-    metric_copy = pltpu.make_async_copy(metric_ref, metric_v, sems.at[1, len(piece_refs)])
+    metric_copies = []
+    if metric_v is not None:
+        metric_copies = [pltpu.make_async_copy(metric_ref, metric_v, sems.at[1, len(piece_refs)])]
+    band = metric_ref if metric_v is None else metric_v
     piece_copies = [
         pltpu.make_async_copy(ref.at[:, :SLOT_ROWS, :], pieces_v.at[place], sems.at[1, n])
         for n, (ref, place) in enumerate(zip(piece_refs, places))
     ]
-    for copy in (*list_rows, metric_copy, *piece_copies):
+    for copy in (*list_rows, *metric_copies, *piece_copies):
         copy.start()
     for copy in list_rows:
         copy.wait()
@@ -75,7 +78,8 @@
     list_copy.start()
     prepare()
     list_copy.wait()
-    metric_copy.wait()
+    for copy in metric_copies:
+        copy.wait()
 
     def one_piece(i, carry):
         for j in range(KMAX):
@@ -83,24 +87,24 @@
             pair_block = list_s[i, P_LANE + j]
             prod = jnp.dot(
                 pieces_v[i, j * BLK : (j + 1) * BLK, :],
-                metric_v[band_block],
+                band[band_block],
                 preferred_element_type=jnp.float32,
             )
             total[pair_block] += prod
         return carry
 
-    for copy, start, ref in zip(piece_copies, starts, piece_refs):
-        copy.wait()
-        lax.fori_loop(start, start + ref.shape[0], one_piece, 0, unroll=min(2, ref.shape[0]))
+    for copy in piece_copies:
+        copy.wait()
+    lax.fori_loop(0, rows_v.shape[0], one_piece, 0, unroll=2)
 
 
 def early_products(metric_ref, *refs):
-    *piece_refs, total, metric_v, pieces_v, rows_v, list_v, list_s, sems = refs
+    *piece_refs, total, pieces_v, rows_v, list_v, list_s, sems = refs
 
     def clear():
         total[...] = jnp.zeros_like(total)
 
-    add_products(metric_ref, piece_refs, total, metric_v, pieces_v, rows_v, list_v, list_s, sems, clear)
+    add_products(metric_ref, piece_refs, total, None, pieces_v, rows_v, list_v, list_s, sems, clear)
 
 
 def late_products(early_ref, metric_ref, *refs):
@@ -115,32 +119,30 @@
     given.wait()
 
 
-def kernel_call(body, out_shape, out_space, taken, metric, pieces, scratch):
+def kernel_call(body, limit, out_shape, out_space, band_space, taken, metric, pieces, scratch):
     count = sum(piece.shape[0] for piece in pieces)
     return pl.pallas_call(
         body,
         out_shape=out_shape,
-        in_specs=[pl.BlockSpec(memory_space=pltpu.HBM)] * (len(taken) + 1 + len(pieces)),
+        in_specs=[pl.BlockSpec(memory_space=pltpu.HBM)] * len(taken)
+        + [pl.BlockSpec(memory_space=band_space)]
+        + [pl.BlockSpec(memory_space=pltpu.HBM)] * len(pieces),
         out_specs=pl.BlockSpec(memory_space=out_space),
         scratch_shapes=[
             *scratch,
-            pltpu.VMEM(metric.shape, metric.dtype),
             pltpu.VMEM((count, SLOT_ROWS, BLK), metric.dtype),
             pltpu.VMEM((count, LIST_ROWS, BLK), metric.dtype),
             pltpu.VMEM((count, BLK), jnp.int32),
             pltpu.SMEM((count, BLK), jnp.int32),
             pltpu.SemaphoreType.DMA((2, len(pieces) + 1)),
         ],
-        compiler_params=pltpu.CompilerParams(vmem_limit_bytes=60 << 20),
+        compiler_params=pltpu.CompilerParams(vmem_limit_bytes=limit << 20),
     )(*taken, metric, *pieces)
 
 
-def copy_to_each(source_ref, copies_ref, source_v, sems):
+def copy_to_each(source_ref, copies_ref, sems):
     count = copies_ref.shape[0]
-    taken = pltpu.make_async_copy(source_ref, source_v, sems.at[count])
-    taken.start()
-    taken.wait()
-    copies = [pltpu.make_async_copy(source_v, copies_ref.at[i], sems.at[i]) for i in range(count)]
+    copies = [pltpu.make_async_copy(source_ref, copies_ref.at[i], sems.at[i]) for i in range(count)]
     for copy in copies:
         copy.start()
     for copy in copies:
@@ -157,7 +159,7 @@
         out_shape=jax.ShapeDtypeStruct((rows, *metric.shape), metric.dtype),
         in_specs=[pl.BlockSpec(memory_space=pltpu.HBM)],
         out_specs=pl.BlockSpec(memory_space=pltpu.HBM),
-        scratch_shapes=[pltpu.VMEM(metric.shape, metric.dtype), pltpu.SemaphoreType.DMA((rows + 1,))],
+        scratch_shapes=[pltpu.SemaphoreType.DMA((rows,))],
     )(metric)
     band = lax.all_to_all(copies, "row", split_axis=0, concat_axis=0, tiled=True)
     band = band.reshape(band_blocks, BLK, out_cols)
@@ -181,21 +183,29 @@
     total_shape = (PAIR_BLOCKS + 1, BLK, out_cols)
     total = kernel_call(
         early_products,
+        52,
         jax.ShapeDtypeStruct(total_shape, jnp.float32),
         pltpu.VMEM,
+        pltpu.VMEM,
         [],
-        band,
+        pltpu.with_memory_space_constraint(band, pltpu.VMEM),
         early,
         [],
     )
     blocks = kernel_call(
         late_products,
+        40,
         jax.ShapeDtypeStruct((PAIR_BLOCKS, BLK, out_cols), jnp.float32),
+        pltpu.HBM,
         pltpu.HBM,
         [total],
         band,
         late,
-        [pltpu.VMEM(total_shape, jnp.float32), pltpu.SemaphoreType.DMA],
+        [
+            pltpu.VMEM(total_shape, jnp.float32),
+            pltpu.SemaphoreType.DMA,
+            pltpu.VMEM(band.shape, band.dtype),
+        ],
     )
     return blocks.reshape(PAIR_DEV, out_cols)
 

time: 99.9 us -> 163 us (1.63)
  Pallas kernels: 12.6 us -> 75.6 us
    pallas_call x1, Pallas kernels: 2.4 us -> 64.8 us  [on_device(): pl.pallas_call(copy_to_each, out_shape=jax.ShapeDtypeStruct((rows, *metri...]
  transfers between devices with their start and end apart: 14 -> 14, of which waited for: 7 -> 7; matrix products, arithmetic and copies ran while one was open for 1% -> 1% of each run, Pallas kernels for 6% -> 4%
where the time goes in v4:
time: 163 us; the launch traced here: 162 us
  Pallas kernels  75.6 us (46%)
  starting transfers between devices  59 us (36%)
  waiting for transfers between devices  24.6 us (15%)
    pallas_call x1, Pallas kernels, on_device(): pl.pallas_call(copy_to_each, out_shape=jax.ShapeDtypeStruct((rows, *metri...  64.8 us
    ppermute x13, starting transfers between devices, sent(): return lax.ppermute(value, axis, perm)  45.4 us
    ppermute x13, waiting for transfers between devices, sent(): return lax.ppermute(value, axis, perm)  24.6 us
    all_to_all x1, starting transfers between devices, on_device(): lax.all_to_all(copies, 'row', split_axis=0, concat_axis=0, tiled=True)  13.6 us
    pallas_call x2, Pallas kernels, kernel_call(): pl.pallas_call(body, out_shape=out_shape, in_specs=[pl.BlockSpec(memory_s...  10.8 us
  transfers between devices with their start and end apart: 14, of which 7 were waited for; matrix products, arithmetic and copies ran while one was open for 1% of the time, Pallas kernels for 4%

profile of v4, /device:TPU:1, one launch (start us, length us, event | category | flops | bytes accessed | tf_op | source)
XLA Modules:
  0.0 162.0 jit_solution(10007491854858169313)
XLA Ops:
  0.0 64.8 %shard_map.37 = bf16[16,512,128]{2,1,0:T(8,128)(2,1)} custom-call(bf16[512,128]{1,0:T(8,128)(2,1)} %source_ref.1), custom_call_target="tpu_custom_call" | custom-call | tf_op jit(solution)/shard_map/pallas_call | solution.py:157
  64.8 0.0 copy-start.9
  64.8 0.0 copy-start.8
  64.8 13.6 %all-to-all-start = ((bf16[16,512,128]{2,1,0:T(8,128)(2,1)}), bf16[16,512,128]{2,1,0:T(8,128)(2,1)S(1)}, u32[]{:S(2)}, u32[]{:S(2)}) async-start(bf16[16,512,128]{2,1,0:T(8,128)(2,1)} %shard_map.37), calls=%async_computation | async-start | bytes 4194304 | tf_op jit(solution)/shard_map/all_to_all | solution.py:164
  78.4 0.0 copy-done.9
  78.4 0.1 fusion.3
  78.5 0.0 copy-done.8
  78.5 2.9 %collective-permute-start = (bf16[1,784,128]{2,1,0:T(8,128)(2,1)S(1)}, bf16[1,784,128]{2,1,0:T(8,128)(2,1)S(1)}, u32[]{:S(2)}, u32[]{:S(2)}) collective-permute-start(bf16[1,784,128]{2,1,0:T(8,128)(2,1)S(1)} %maximum_bitcast_fusion), channel_id=1, source_target_pairs={{0,1},{1,0},{2,3},{3,2},{4,5},{5,4},{6,7},{7,6},{8,9},{9,8},{10,11... | collective-permute-start | bytes 602120 | tf_op jit(solution)/shard_map/ppermute | solution.py:37
  81.4 2.2 %collective-permute-start.1 = (bf16[1,784,128]{2,1,0:T(8,128)(2,1)S(1)}, bf16[1,784,128]{2,1,0:T(8,128)(2,1)S(1)}, u32[]{:S(2)}, u32[]{:S(2)}) collective-permute-start(bf16[1,784,128]{2,1,0:T(8,128)(2,1)S(1)} %maximum_bitcast_fusion), channel_id=1, source_target_pairs={{0,16},{1,17},{2,18},{3,19},{4,20},{5,21},{6,22},{7,23},{8,24},{9,... | collective-permute-start | bytes 602120 | tf_op jit(solution)/shard_map/ppermute | solution.py:37
  83.6 0.0 collective-permute-done
  83.7 0.0 copy-start.2
  83.7 5.1 %collective-permute-start.3 = (bf16[2,784,128]{2,1,0:T(8,128)(2,1)S(1)}, bf16[2,784,128]{2,1,0:T(8,128)(2,1)S(1)}, u32[]{:S(2)}, u32[]{:S(2)}) collective-permute-start(bf16[2,784,128]{2,1,0:T(8,128)(2,1)S(1)} %pad_maximum_fusion.1.refs_0_), channel_id=1, source_target_pairs={{0,2},{1,15},{2,4},{3,1},{4,6},{5,3},{6,8},{7,5},{8,10},{9,7},{10,... | collective-permute-start | bytes 1204232 | tf_op jit(solution)/shard_map/ppermute | solution.py:37
  88.8 6.2 %collective-permute-done.1 = bf16[1,784,128]{2,1,0:T(8,128)(2,1)S(1)} collective-permute-done((bf16[1,784,128]{2,1,0:T(8,128)(2,1)S(1)}, bf16[1,784,128]{2,1,0:T(8,128)(2,1)S(1)}, u32[]{:S(2)}, u32[]{:S(2)}) %collective-permute-start.1) | collective-permute-done | bytes 200736 | tf_op jit(solution)/shard_map/ppermute | solution.py:37
  95.0 2.3 %collective-permute-start.2 = (bf16[1,784,128]{2,1,0:T(8,128)(2,1)S(1)}, bf16[1,784,128]{2,1,0:T(8,128)(2,1)S(1)}, u32[]{:S(2)}, u32[]{:S(2)}) collective-permute-start(bf16[1,784,128]{2,1,0:T(8,128)(2,1)S(1)} %collective-permute-done.1), channel_id=1, source_target_pairs={{0,1},{1,0},{2,3},{3,2},{4,5},{5,4},{6,7},{7,6},{8,9},{9,8},{10,11... | collective-permute-start | bytes 602120 | tf_op jit(solution)/shard_map/ppermute | solution.py:37
  97.3 1.0 collective-permute-done.2
  98.4 0.0 copy-start.7
  98.4 5.1 %collective-permute-start.4 = (bf16[2,784,128]{2,1,0:T(8,128)(2,1)S(1)}, bf16[2,784,128]{2,1,0:T(8,128)(2,1)S(1)}, u32[]{:S(2)}, u32[]{:S(2)}) collective-permute-start(bf16[2,784,128]{2,1,0:T(8,128)(2,1)S(1)} %constant_dynamic-update-slice_fusion.refs_1_), channel_id=1, source_target_pairs={{0,2},{1,15},{2,4},{3,1},{4,6},{5,3},{6,8},{7,5},{8,10},{9,7},{10,... | collective-permute-start | bytes 1204232 | tf_op jit(solution)/shard_map/ppermute | solution.py:37
  103.5 0.0 collective-permute-done.3.refs_2_
  103.5 0.0 copy-start.3
  103.5 3.0 %collective-permute-start.5 = (bf16[2,784,128]{2,1,0:T(8,128)(2,1)S(1)}, bf16[2,784,128]{2,1,0:T(8,128)(2,1)S(1)}, u32[]{:S(2)}, u32[]{:S(2)}) collective-permute-start(bf16[2,784,128]{2,1,0:T(8,128)(2,1)S(1)} %collective-permute-done.3.refs_2_), channel_id=1, source_target_pairs={{0,2},{1,15},{2,4},{3,1},{4,6},{5,3},{6,8},{7,5},{8,10},{9,7},{10,... | collective-permute-start | bytes 1204232 | tf_op jit(solution)/shard_map/ppermute | solution.py:37
  106.5 1.8 %collective-permute-done.4.refs_3_ = bf16[2,784,128]{2,1,0:T(8,128)(2,1)S(1)} collective-permute-done((bf16[2,784,128]{2,1,0:T(8,128)(2,1)S(1)}, bf16[2,784,128]{2,1,0:T(8,128)(2,1)S(1)}, u32[]{:S(2)}, u32[]{:S(2)}) %collective-permute-start.4) | collective-permute-done | bytes 401440 | tf_op jit(solution)/shard_map/ppermute | solution.py:37
  108.3 5.0 %collective-permute-start.6 = (bf16[2,784,128]{2,1,0:T(8,128)(2,1)S(1)}, bf16[2,784,128]{2,1,0:T(8,128)(2,1)S(1)}, u32[]{:S(2)}, u32[]{:S(2)}) collective-permute-start(bf16[2,784,128]{2,1,0:T(8,128)(2,1)S(1)} %collective-permute-done.4.refs_3_), channel_id=1, source_target_pairs={{0,2},{1,15},{2,4},{3,1},{4,6},{5,3},{6,8},{7,5},{8,10},{9,7},{10,... | collective-permute-start | bytes 1204232 | tf_op jit(solution)/shard_map/ppermute | solution.py:37
  113.3 0.0 collective-permute-done.5.refs_4_
  113.4 4.6 %collective-permute-start.7 = (bf16[2,784,128]{2,1,0:T(8,128)(2,1)S(1)}, bf16[2,784,128]{2,1,0:T(8,128)(2,1)S(1)}, u32[]{:S(2)}, u32[]{:S(2)}) collective-permute-start(bf16[2,784,128]{2,1,0:T(8,128)(2,1)S(1)} %collective-permute-done.5.refs_4_), channel_id=1, source_target_pairs={{0,2},{1,15},{2,4},{3,1},{4,6},{5,3},{6,8},{7,5},{8,10},{9,7},{10,... | collective-permute-start | bytes 1204232 | tf_op jit(solution)/shard_map/ppermute | solution.py:37
  118.0 0.1 constant_dynamic-update-slice_fusion.5
  118.0 0.1 constant_dynamic-update-slice_fusion.4
  118.1 0.0 collective-permute-done.6.refs_5_
  118.1 0.1 constant_dynamic-update-slice_fusion.3
  118.2 4.5 %collective-permute-done.7.refs_6_ = bf16[2,784,128]{2,1,0:T(8,128)(2,1)S(1)} collective-permute-done((bf16[2,784,128]{2,1,0:T(8,128)(2,1)S(1)}, bf16[2,784,128]{2,1,0:T(8,128)(2,1)S(1)}, u32[]{:S(2)}, u32[]{:S(2)}) %collective-permute-start.7) | collective-permute-done | bytes 401440 | tf_op jit(solution)/shard_map/ppermute | solution.py:37
  122.7 0.1 constant_dynamic-update-slice_fusion.2
  122.8 0.0 copy-done.3
  122.8 0.0 copy-done.4
  122.8 0.0 copy-done.5
  122.8 4.5 %collective-permute-start.8 = (bf16[10,784,128]{2,1,0:T(8,128)(2,1)S(1)}, bf16[10,784,128]{2,1,0:T(8,128)(2,1)}, u32[]{:S(2)}, u32[]{:S(2)}) collective-permute-start(bf16[10,784,128]{2,1,0:T(8,128)(2,1)S(1)} %constant_dynamic-update-slice_fusion.2), channel_id=1, source_target_pairs={{0,1},{1,0},{2,3},{3,2},{4,5},{5,4},{6,7},{7,6},{8,9},{9,8},{10,11... | collective-permute-start | bytes 6021128 | tf_op jit(solution)/shard_map/ppermute | solution.py:37
  127.3 2.8 %collective-permute-start.10 = (bf16[1,784,128]{2,1,0:T(8,128)(2,1)S(1)}, bf16[1,784,128]{2,1,0:T(8,128)(2,1)S(1)}, u32[]{:S(2)}, u32[]{:S(2)}) collective-permute-start(bf16[1,784,128]{2,1,0:T(8,128)(2,1)S(1)} %slice.4), channel_id=1, source_target_pairs={{0,2},{1,15},{2,4},{3,1},{4,6},{5,3},{6,8},{7,5},{8,10},{9,7},{10,... | collective-permute-start | bytes 602120 | tf_op jit(solution)/shard_map/ppermute | solution.py:37
  130.1 2.9 %collective-permute-start.9 = (bf16[2,784,128]{2,1,0:T(8,128)(2,1)S(1)}, bf16[2,784,128]{2,1,0:T(8,128)(2,1)S(1)}, u32[]{:S(2)}, u32[]{:S(2)}) collective-permute-start(bf16[2,784,128]{2,1,0:T(8,128)(2,1)S(1)} %collective-permute-done.7.refs_6_), channel_id=1, source_target_pairs={{0,16},{1,17},{2,18},{3,19},{4,20},{5,21},{6,22},{7,23},{8,24},{9,... | collective-permute-start | bytes 1204232 | tf_op jit(solution)/shard_map/ppermute | solution.py:37
  133.0 1.0 collective-permute-done.10.refs_1_
  134.0 2.9 %collective-permute-start.11 = (bf16[1,784,128]{2,1,0:T(8,128)(2,1)S(1)}, bf16[1,784,128]{2,1,0:T(8,128)(2,1)S(1)}, u32[]{:S(2)}, u32[]{:S(2)}) collective-permute-start(bf16[1,784,128]{2,1,0:T(8,128)(2,1)S(1)} %collective-permute-done.10.refs_1_), channel_id=1, source_target_pairs={{0,16},{1,17},{2,18},{3,19},{4,20},{5,21},{6,22},{7,23},{8,24},{9,... | collective-permute-start | bytes 602120 | tf_op jit(solution)/shard_map/ppermute | solution.py:37
  137.0 6.3 %collective-permute-done.9.refs_0_ = bf16[2,784,128]{2,1,0:T(8,128)(2,1)S(1)} collective-permute-done((bf16[2,784,128]{2,1,0:T(8,128)(2,1)S(1)}, bf16[2,784,128]{2,1,0:T(8,128)(2,1)S(1)}, u32[]{:S(2)}, u32[]{:S(2)}) %collective-permute-start.9) | collective-permute-done | bytes 401440 | tf_op jit(solution)/shard_map/ppermute | solution.py:37
  143.3 3.6 %collective-permute-done.11.refs_2_ = bf16[1,784,128]{2,1,0:T(8,128)(2,1)S(1)} collective-permute-done((bf16[1,784,128]{2,1,0:T(8,128)(2,1)S(1)}, bf16[1,784,128]{2,1,0:T(8,128)(2,1)S(1)}, u32[]{:S(2)}, u32[]{:S(2)}) %collective-permute-start.11) | collective-permute-done | bytes 200736 | tf_op jit(solution)/shard_map/ppermute | solution.py:37
  146.9 1.0 pad_maximum_fusion
  147.9 2.2 %collective-permute-start.12 = (bf16[4,784,128]{2,1,0:T(8,128)(2,1)}, bf16[4,784,128]{2,1,0:T(8,128)(2,1)}, u32[]{:S(2)}, u32[]{:S(2)}) collective-permute-start(bf16[4,784,128]{2,1,0:T(8,128)(2,1)} %pad_maximum_fusion), channel_id=1, source_target_pairs={{0,1},{1,0},{2,3},{3,2},{4,5},{5,4},{6,7},{7,6},{8,9},{9,8},{10,11... | collective-permute-start | bytes 2408456 | tf_op jit(solution)/shard_map/ppermute | solution.py:37
  150.1 0.0 collective-permute-done.8.refs_7_
  150.1 0.0 all-to-all-done
  150.2 6.8 %shard_map.38.early_ref = f32[9,128,128]{2,1,0:T(8,128)} custom-call(bf16[64,128,128]{2,1,0:T(8,128)(2,1)S(1)} %bitcast.5, bf16[2,784,128]{2,1,0:T(8,128)(2,1)} %copy-done.2, bf16[2,784,128]{2,1,0:T(8,128)(2,1)} %copy-done.7, bf16[2,784,128]{2,1,0:T(8,128)(2,1)} %copy-done.3, bf16[2,784,128]{2,1,0:T(8,128)(2,1)} %copy-done.4, ...), custom_call_target="tpu_custom_call" | custom-call | tf_op jit(solution)/shard_map/pallas_call | solution.py:124
  157.0 0.0 collective-permute-done.12.refs_3_
  157.0 1.1 copy-done
  158.0 4.0 %shard_map.39 = f32[8,128,128]{2,1,0:T(8,128)} custom-call(f32[9,128,128]{2,1,0:T(8,128)S(1)} %copy-done, bf16[64,128,128]{2,1,0:T(8,128)(2,1)S(1)} %bitcast.6, bf16[2,784,128]{2,1,0:T(8,128)(2,1)S(1)} %collective-permute-done.9.refs_0_, bf16[1,784,128]{2,1,0:T(8,128)(2,1)S(1)} %collective-permute-done.10.refs_1_, ...), custom_call_target="tpu_custom_call" | custom-call | tf_op jit(solution)/shard_map/pallas_call | solution.py:124
  (17 shorter events, 0.2 us)
Async XLA Ops:
  64.8 13.6 %copy-start.9 = (s32[6]{0:T(128)S(1)}, s32[6]{0:T(128)}, u32[]{:S(2)}) copy-start(s32[6]{0:T(128)} %param.4) | copy-start | bytes 76
  64.8 13.7 %copy-start.8 = (bf16[6,128,128]{2,1,0:T(8,128)(2,1)S(1)}, bf16[6,128,128]{2,1,0:T(8,128)(2,1)}, u32[]{:S(2)}) copy-start(bf16[6,128,128]{2,1,0:T(8,128)(2,1)} %param.3) | copy-start | bytes 589828
  64.8 85.3 %all-to-all-start = ((bf16[16,512,128]{2,1,0:T(8,128)(2,1)}), bf16[16,512,128]{2,1,0:T(8,128)(2,1)S(1)}, u32[]{:S(2)}, u32[]{:S(2)}) async-start(bf16[16,512,128]{2,1,0:T(8,128)(2,1)} %shard_map.37), calls=%async_computation | async-start | bytes 4194304 | tf_op jit(solution)/shard_map/all_to_all | solution.py:164
  78.5 5.1 %collective-permute-start = (bf16[1,784,128]{2,1,0:T(8,128)(2,1)S(1)}, bf16[1,784,128]{2,1,0:T(8,128)(2,1)S(1)}, u32[]{:S(2)}, u32[]{:S(2)}) collective-permute-start(bf16[1,784,128]{2,1,0:T(8,128)(2,1)S(1)} %maximum_bitcast_fusion), channel_id=1, source_target_pairs={{0,1},{1,0},{2,3},{3,2},{4,5},{5,4},{6,7},{7,6},{8,9},{9,8},{10,11... | collective-permute-start | bytes 602120 | tf_op jit(solution)/shard_map/ppermute | solution.py:37
  81.4 13.6 %collective-permute-start.1 = (bf16[1,784,128]{2,1,0:T(8,128)(2,1)S(1)}, bf16[1,784,128]{2,1,0:T(8,128)(2,1)S(1)}, u32[]{:S(2)}, u32[]{:S(2)}) collective-permute-start(bf16[1,784,128]{2,1,0:T(8,128)(2,1)S(1)} %maximum_bitcast_fusion), channel_id=1, source_target_pairs={{0,16},{1,17},{2,18},{3,19},{4,20},{5,21},{6,22},{7,23},{8,24},{9,... | collective-permute-start | bytes 602120 | tf_op jit(solution)/shard_map/ppermute | solution.py:37
  83.7 34.5 %copy-start.2 = (bf16[2,784,128]{2,1,0:T(8,128)(2,1)}, bf16[2,784,128]{2,1,0:T(8,128)(2,1)S(1)}, u32[]{:S(2)}) copy-start(bf16[2,784,128]{2,1,0:T(8,128)(2,1)S(1)} %pad_maximum_fusion.1.refs_0_) | copy-start | bytes 1204228
  83.7 19.8 %collective-permute-start.3 = (bf16[2,784,128]{2,1,0:T(8,128)(2,1)S(1)}, bf16[2,784,128]{2,1,0:T(8,128)(2,1)S(1)}, u32[]{:S(2)}, u32[]{:S(2)}) collective-permute-start(bf16[2,784,128]{2,1,0:T(8,128)(2,1)S(1)} %pad_maximum_fusion.1.refs_0_), channel_id=1, source_target_pairs={{0,2},{1,15},{2,4},{3,1},{4,6},{5,3},{6,8},{7,5},{8,10},{9,7},{10,... | collective-permute-start | bytes 1204232 | tf_op jit(solution)/shard_map/ppermute | solution.py:37
  95.0 3.4 %collective-permute-start.2 = (bf16[1,784,128]{2,1,0:T(8,128)(2,1)S(1)}, bf16[1,784,128]{2,1,0:T(8,128)(2,1)S(1)}, u32[]{:S(2)}, u32[]{:S(2)}) collective-permute-start(bf16[1,784,128]{2,1,0:T(8,128)(2,1)S(1)} %collective-permute-done.1), channel_id=1, source_target_pairs={{0,1},{1,0},{2,3},{3,2},{4,5},{5,4},{6,7},{7,6},{8,9},{9,8},{10,11... | collective-permute-start | bytes 602120 | tf_op jit(solution)/shard_map/ppermute | solution.py:37
  98.4 14.9 %copy-start.7 = (bf16[2,784,128]{2,1,0:T(8,128)(2,1)}, bf16[2,784,128]{2,1,0:T(8,128)(2,1)S(1)}, u32[]{:S(2)}) copy-start(bf16[2,784,128]{2,1,0:T(8,128)(2,1)S(1)} %constant_dynamic-update-slice_fusion.refs_1_) | copy-start | bytes 1204228
  98.4 9.9 %collective-permute-start.4 = (bf16[2,784,128]{2,1,0:T(8,128)(2,1)S(1)}, bf16[2,784,128]{2,1,0:T(8,128)(2,1)S(1)}, u32[]{:S(2)}, u32[]{:S(2)}) collective-permute-start(bf16[2,784,128]{2,1,0:T(8,128)(2,1)S(1)} %constant_dynamic-update-slice_fusion.refs_1_), channel_id=1, source_target_pairs={{0,2},{1,15},{2,4},{3,1},{4,6},{5,3},{6,8},{7,5},{8,10},{9,7},{10,... | collective-permute-start | bytes 1204232 | tf_op jit(solution)/shard_map/ppermute | solution.py:37
  103.5 19.2 %copy-start.3 = (bf16[2,784,128]{2,1,0:T(8,128)(2,1)}, bf16[2,784,128]{2,1,0:T(8,128)(2,1)S(1)}, u32[]{:S(2)}) copy-start(bf16[2,784,128]{2,1,0:T(8,128)(2,1)S(1)} %collective-permute-done.3.refs_2_) | copy-start | bytes 1204228
  103.5 9.8 %collective-permute-start.5 = (bf16[2,784,128]{2,1,0:T(8,128)(2,1)S(1)}, bf16[2,784,128]{2,1,0:T(8,128)(2,1)S(1)}, u32[]{:S(2)}, u32[]{:S(2)}) collective-permute-start(bf16[2,784,128]{2,1,0:T(8,128)(2,1)S(1)} %collective-permute-done.3.refs_2_), channel_id=1, source_target_pairs={{0,2},{1,15},{2,4},{3,1},{4,6},{5,3},{6,8},{7,5},{8,10},{9,7},{10,... | collective-permute-start | bytes 1204232 | tf_op jit(solution)/shard_map/ppermute | solution.py:37
  108.3 14.5 %copy-start.4 = (bf16[2,784,128]{2,1,0:T(8,128)(2,1)}, bf16[2,784,128]{2,1,0:T(8,128)(2,1)S(1)}, u32[]{:S(2)}) copy-start(bf16[2,784,128]{2,1,0:T(8,128)(2,1)S(1)} %collective-permute-done.4.refs_3_) | copy-start | bytes 1204228
  108.3 9.8 %collective-permute-start.6 = (bf16[2,784,128]{2,1,0:T(8,128)(2,1)S(1)}, bf16[2,784,128]{2,1,0:T(8,128)(2,1)S(1)}, u32[]{:S(2)}, u32[]{:S(2)}) collective-permute-start(bf16[2,784,128]{2,1,0:T(8,128)(2,1)S(1)} %collective-permute-done.4.refs_3_), channel_id=1, source_target_pairs={{0,2},{1,15},{2,4},{3,1},{4,6},{5,3},{6,8},{7,5},{8,10},{9,7},{10,... | collective-permute-start | bytes 1204232 | tf_op jit(solution)/shard_map/ppermute | solution.py:37
  113.4 9.4 %copy-start.5 = (bf16[2,784,128]{2,1,0:T(8,128)(2,1)}, bf16[2,784,128]{2,1,0:T(8,128)(2,1)S(1)}, u32[]{:S(2)}) copy-start(bf16[2,784,128]{2,1,0:T(8,128)(2,1)S(1)} %collective-permute-done.5.refs_4_) | copy-start | bytes 1204228
  113.4 9.4 %collective-permute-start.7 = (bf16[2,784,128]{2,1,0:T(8,128)(2,1)S(1)}, bf16[2,784,128]{2,1,0:T(8,128)(2,1)S(1)}, u32[]{:S(2)}, u32[]{:S(2)}) collective-permute-start(bf16[2,784,128]{2,1,0:T(8,128)(2,1)S(1)} %collective-permute-done.5.refs_4_), channel_id=1, source_target_pairs={{0,2},{1,15},{2,4},{3,1},{4,6},{5,3},{6,8},{7,5},{8,10},{9,7},{10,... | collective-permute-start | bytes 1204232 | tf_op jit(solution)/shard_map/ppermute | solution.py:37
  118.1 25.2 %copy-start.6 = (bf16[2,784,128]{2,1,0:T(8,128)(2,1)}, bf16[2,784,128]{2,1,0:T(8,128)(2,1)S(1)}, u32[]{:S(2)}) copy-start(bf16[2,784,128]{2,1,0:T(8,128)(2,1)S(1)} %collective-permute-done.6.refs_5_) | copy-start | bytes 1204228
  122.7 27.4 %copy-start.1 = (bf16[2,784,128]{2,1,0:T(8,128)(2,1)}, bf16[2,784,128]{2,1,0:T(8,128)(2,1)S(1)}, u32[]{:S(2)}) copy-start(bf16[2,784,128]{2,1,0:T(8,128)(2,1)S(1)} %collective-permute-done.7.refs_6_) | copy-start | bytes 1204228
  122.8 27.3 %collective-permute-start.8 = (bf16[10,784,128]{2,1,0:T(8,128)(2,1)S(1)}, bf16[10,784,128]{2,1,0:T(8,128)(2,1)}, u32[]{:S(2)}, u32[]{:S(2)}) collective-permute-start(bf16[10,784,128]{2,1,0:T(8,128)(2,1)S(1)} %constant_dynamic-update-slice_fusion.2), channel_id=1, source_target_pairs={{0,1},{1,0},{2,3},{3,2},{4,5},{5,4},{6,7},{7,6},{8,9},{9,8},{10,11... | collective-permute-start | bytes 6021128 | tf_op jit(solution)/shard_map/ppermute | solution.py:37
  127.3 6.8 %collective-permute-start.10 = (bf16[1,784,128]{2,1,0:T(8,128)(2,1)S(1)}, bf16[1,784,128]{2,1,0:T(8,128)(2,1)S(1)}, u32[]{:S(2)}, u32[]{:S(2)}) collective-permute-start(bf16[1,784,128]{2,1,0:T(8,128)(2,1)S(1)} %slice.4), channel_id=1, source_target_pairs={{0,2},{1,15},{2,4},{3,1},{4,6},{5,3},{6,8},{7,5},{8,10},{9,7},{10,... | collective-permute-start | bytes 602120 | tf_op jit(solution)/shard_map/ppermute | solution.py:37
  130.1 13.2 %collective-permute-start.9 = (bf16[2,784,128]{2,1,0:T(8,128)(2,1)S(1)}, bf16[2,784,128]{2,1,0:T(8,128)(2,1)S(1)}, u32[]{:S(2)}, u32[]{:S(2)}) collective-permute-start(bf16[2,784,128]{2,1,0:T(8,128)(2,1)S(1)} %collective-permute-done.7.refs_6_), channel_id=1, source_target_pairs={{0,16},{1,17},{2,18},{3,19},{4,20},{5,21},{6,22},{7,23},{8,24},{9,... | collective-permute-start | bytes 1204232 | tf_op jit(solution)/shard_map/ppermute | solution.py:37
  134.0 12.9 %collective-permute-start.11 = (bf16[1,784,128]{2,1,0:T(8,128)(2,1)S(1)}, bf16[1,784,128]{2,1,0:T(8,128)(2,1)S(1)}, u32[]{:S(2)}, u32[]{:S(2)}) collective-permute-start(bf16[1,784,128]{2,1,0:T(8,128)(2,1)S(1)} %collective-permute-done.10.refs_1_), channel_id=1, source_target_pairs={{0,16},{1,17},{2,18},{3,19},{4,20},{5,21},{6,22},{7,23},{8,24},{9,... | collective-permute-start | bytes 602120 | tf_op jit(solution)/shard_map/ppermute | solution.py:37
  147.9 9.0 %collective-permute-start.12 = (bf16[4,784,128]{2,1,0:T(8,128)(2,1)}, bf16[4,784,128]{2,1,0:T(8,128)(2,1)}, u32[]{:S(2)}, u32[]{:S(2)}) collective-permute-start(bf16[4,784,128]{2,1,0:T(8,128)(2,1)} %pad_maximum_fusion), channel_id=1, source_target_pairs={{0,1},{1,0},{2,3},{3,2},{4,5},{5,4},{6,7},{7,6},{8,9},{9,8},{10,11... | collective-permute-start | bytes 2408456 | tf_op jit(solution)/shard_map/ppermute | solution.py:37
  157.0 1.1 copy-start

commit v5 on v4

--- a/solution.py
+++ b/solution.py
@@ -12,6 +12,7 @@
 NY = 8
 LIST_ROWS = 16
 SLOT_ROWS = KMAX * BLK
+UNIT = SLOT_ROWS + LIST_ROWS
 P_LANE = 8
 
 
@@ -35,21 +36,6 @@
 
 def sent(value, perm, axis="col"):
     return lax.ppermute(value, axis, perm)
-
-
-def payload(slots, block_list, col_blocks):
-    me = lax.axis_index("col")
-    clipped = jnp.maximum(block_list, 0)
-    band_block = me * col_blocks + clipped % col_blocks
-    pair_block = jnp.where(block_list >= 0, clipped // col_blocks, PAIR_BLOCKS)
-    row = jnp.concatenate(
-        [
-            jnp.pad(band_block, (0, P_LANE - KMAX)),
-            jnp.pad(pair_block, (0, BLK - P_LANE - KMAX)),
-        ]
-    )
-    rows = jnp.broadcast_to(row.astype(jnp.bfloat16), (LIST_ROWS, BLK))
-    return jnp.concatenate([slots.reshape(SLOT_ROWS, BLK), rows])[None]
 
 
 def add_products(metric_ref, piece_refs, total, metric_v, pieces_v, rows_v, list_v, list_s, sems, prepare):
@@ -93,9 +79,13 @@
             total[pair_block] += prod
         return carry
 
-    for copy in piece_copies:
-        copy.wait()
-    lax.fori_loop(0, rows_v.shape[0], one_piece, 0, unroll=2)
+    start, end = 0, 0
+    for copy, ref in zip(piece_copies, piece_refs):
+        copy.wait()
+        end += ref.shape[0]
+        if (end - start) % 2 == 0:
+            lax.fori_loop(start, end, one_piece, 0, unroll=2)
+            start = end
 
 
 def early_products(metric_ref, *refs):
@@ -140,31 +130,67 @@
     )(*taken, metric, *pieces)
 
 
-def copy_to_each(source_ref, copies_ref, sems):
+def prepare_sends(list_ref, metric_ref, slots_ref, copies_ref, payload_ref, metric_v, payload_v, sems):
     count = copies_ref.shape[0]
-    copies = [pltpu.make_async_copy(source_ref, copies_ref.at[i], sems.at[i]) for i in range(count)]
+    metric_in = pltpu.make_async_copy(metric_ref, metric_v, sems.at[count])
+    metric_in.start()
+    slots_in = [
+        pltpu.make_async_copy(
+            slots_ref.at[j], payload_v.at[0, j * BLK : (j + 1) * BLK, :], sems.at[count + 1 + j]
+        )
+        for j in range(KMAX)
+    ]
+    for copy in slots_in:
+        copy.start()
+    band_blocks = count * metric_ref.shape[0] // BLK
+    col_blocks = band_blocks // lax.axis_size("col")
+    first_block = lax.axis_index("col") * col_blocks
+    lanes = lax.broadcasted_iota(jnp.int32, (LIST_ROWS, BLK), 1)
+    rows = jnp.zeros((LIST_ROWS, BLK), jnp.int32)
+    for j in range(KMAX):
+        entry = list_ref[j]
+        used = jnp.maximum(entry, 0)
+        pair_block = jnp.where(entry >= 0, used // col_blocks, PAIR_BLOCKS)
+        rows = jnp.where(lanes == j, first_block + used % col_blocks, rows)
+        rows = jnp.where(lanes == P_LANE + j, pair_block, rows)
+    payload_v[0, SLOT_ROWS:, :] = rows.astype(jnp.float32).astype(payload_v.dtype)
+    metric_in.wait()
+    copies = [pltpu.make_async_copy(metric_v, copies_ref.at[i], sems.at[i]) for i in range(count)]
     for copy in copies:
         copy.start()
+    for copy in slots_in:
+        copy.wait()
+    payload_out = pltpu.make_async_copy(payload_v, payload_ref, sems.at[count])
+    payload_out.start()
     for copy in copies:
         copy.wait()
+    payload_out.wait()
 
 
 def on_device(slots, block_list, metric):
     out_cols = metric.shape[1]
     rows = lax.axis_size("row")
     band_blocks = rows * metric.shape[0] // BLK
-    col_blocks = band_blocks // lax.axis_size("col")
-    copies = pl.pallas_call(
-        copy_to_each,
-        out_shape=jax.ShapeDtypeStruct((rows, *metric.shape), metric.dtype),
-        in_specs=[pl.BlockSpec(memory_space=pltpu.HBM)],
-        out_specs=pl.BlockSpec(memory_space=pltpu.HBM),
-        scratch_shapes=[pltpu.SemaphoreType.DMA((rows,))],
-    )(metric)
+    hbm = pl.BlockSpec(memory_space=pltpu.HBM)
+    payload_shape = (1, UNIT, BLK)
+    copies, own = pl.pallas_call(
+        prepare_sends,
+        out_shape=(
+            jax.ShapeDtypeStruct((rows, *metric.shape), metric.dtype),
+            jax.ShapeDtypeStruct(payload_shape, slots.dtype),
+        ),
+        in_specs=[pl.BlockSpec(memory_space=pltpu.SMEM), hbm, hbm],
+        out_specs=(hbm, hbm),
+        scratch_shapes=[
+            pltpu.VMEM(metric.shape, metric.dtype),
+            pltpu.VMEM(payload_shape, slots.dtype),
+            pltpu.SemaphoreType.DMA((rows + 1 + KMAX,)),
+        ],
+        compiler_params=pltpu.CompilerParams(vmem_limit_bytes=60 << 20),
+    )(block_list, metric, slots)
     band = lax.all_to_all(copies, "row", split_axis=0, concat_axis=0, tiled=True)
     band = band.reshape(band_blocks, BLK, out_cols)
 
-    own = payload(slots, block_list, col_blocks)
     own_x = sent(own, X_PARTNER)
     near = jnp.concatenate([own, sent(own, CORE)])
     near_x = jnp.concatenate([own_x, sent(own_x, CORE)])
@@ -174,12 +200,12 @@
     b2 = sent(b1, RING)
     a3 = sent(a2, RING)
     a4 = sent(a3[:1], RING)
-    early = [a1, b1, a2, b2, a3]
-    late = [sent(a3, X_PARTNER), a4, sent(a4, X_PARTNER)]
-    early_other = sent(jnp.concatenate(early), CORE)
-    late_other = sent(jnp.concatenate(late), CORE)
-    early = [near, near_x, *early, early_other]
-    late = [*late, late_other]
+    b3 = sent(b2, RING)
+    b4 = sent(b3[:1], RING)
+    early_other = sent(jnp.concatenate([a1, b1, a2, b2, a3]), CORE)
+    late_other = sent(jnp.concatenate([b3, a4, b4]), CORE)
+    early = [near, near_x, a1, b1, a2, b2, a3, early_other]
+    late = [b3, a4, b4, late_other]
     total_shape = (PAIR_BLOCKS + 1, BLK, out_cols)
     total = kernel_call(
         early_products,

time: 163 us -> 99.6 us (0.61)
  Pallas kernels: 75.6 us -> 12.6 us
  waiting for transfers between devices: 24.6 us -> 19.9 us
  starting transfers between devices: 59 us -> 63.6 us
    pallas_call x1, Pallas kernels: 64.8 us -> 3.13 us  [on_device(): pl.pallas_call(prepare_sends, out_shape=(jax.ShapeDtypeStruct((rows, *met...]
    ppermute x13, waiting for transfers between devices: 24.6 us -> 19.9 us  [sent(): return lax.ppermute(value, axis, perm)]
    ppermute x13, starting transfers between devices: 45.4 us -> 50.1 us  [sent(): return lax.ppermute(value, axis, perm)]
  transfers between devices with their start and end apart: 14 -> 14, of which waited for: 7 -> 6; matrix products, arithmetic and copies ran while one was open for 1% -> 1% of each run, Pallas kernels for 4% -> 6%
where the time goes in v5:
time: 99.6 us; the launch traced here: 98.9 us
  starting transfers between devices  63.6 us (64%)
  waiting for transfers between devices  19.9 us (20%)
  Pallas kernels  12.6 us (13%)
  local copies, waits for them, and re-layouts  1.45 us (1%)
  other arithmetic  1.02 us (1%)
    ppermute x13, starting transfers between devices, sent(): return lax.ppermute(value, axis, perm)  50.1 us
    ppermute x13, waiting for transfers between devices, sent(): return lax.ppermute(value, axis, perm)  19.9 us
    all_to_all x1, starting transfers between devices, on_device(): lax.all_to_all(copies, 'row', split_axis=0, concat_axis=0, tiled=True)  13.6 us
    pallas_call x2, Pallas kernels, kernel_call(): pl.pallas_call(body, out_shape=out_shape, in_specs=[pl.BlockSpec(memory_s...  9.44 us
    pallas_call x1, Pallas kernels, on_device(): pl.pallas_call(prepare_sends, out_shape=(jax.ShapeDtypeStruct((rows, *met...  3.13 us
  transfers between devices with their start and end apart: 14, of which 6 were waited for; matrix products, arithmetic and copies ran while one was open for 1% of the time, Pallas kernels for 6%

profile of v5, /device:TPU:1, one launch (start us, length us, event | category | flops | bytes accessed | tf_op | source)
XLA Modules:
  0.0 98.9 jit_solution(7203531260957776762)
XLA Ops:
  0.0 3.1 %shard_map.37 = (bf16[16,512,128]{2,1,0:T(8,128)(2,1)}, bf16[1,784,128]{2,1,0:T(8,128)(2,1)}) custom-call(s32[6]{0:T(128)} %list_ref.1, bf16[512,128]{1,0:T(8,128)(2,1)} %metric_ref.1, bf16[6,128,128]{2,1,0:T(8,128)(2,1)} %slots_ref.1), custom_call_target="tpu_custom_call" | custom-call | tf_op jit(solution)/shard_map/pallas_call | solution.py:176
  3.1 0.0 copy-start.8
  3.1 13.6 %all-to-all-start = ((bf16[16,512,128]{2,1,0:T(8,128)(2,1)}), bf16[16,512,128]{2,1,0:T(8,128)(2,1)S(1)}, u32[]{:S(2)}, u32[]{:S(2)}) async-start(bf16[16,512,128]{2,1,0:T(8,128)(2,1)} %get-tuple-element.7), calls=%async_computation | async-start | bytes 4194304 | tf_op jit(solution)/shard_map/all_to_all | solution.py:191
  16.7 0.0 copy-done.8
  16.7 2.9 %collective-permute-start = (bf16[1,784,128]{2,1,0:T(8,128)(2,1)S(1)}, bf16[1,784,128]{2,1,0:T(8,128)(2,1)S(1)}, u32[]{:S(2)}, u32[]{:S(2)}) collective-permute-start(bf16[1,784,128]{2,1,0:T(8,128)(2,1)S(1)} %copy-done.8), channel_id=1, source_target_pairs={{0,1},{1,0},{2,3},{3,2},{4,5},{5,4},{6,7},{7,6},{8,9},{9,8},{10,11... | collective-permute-start | bytes 602120 | tf_op jit(solution)/shard_map/ppermute | solution.py:38
  19.6 2.2 %collective-permute-start.1 = (bf16[1,784,128]{2,1,0:T(8,128)(2,1)S(1)}, bf16[1,784,128]{2,1,0:T(8,128)(2,1)S(1)}, u32[]{:S(2)}, u32[]{:S(2)}) collective-permute-start(bf16[1,784,128]{2,1,0:T(8,128)(2,1)S(1)} %copy-done.8), channel_id=1, source_target_pairs={{0,16},{1,17},{2,18},{3,19},{4,20},{5,21},{6,22},{7,23},{8,24},{9,... | collective-permute-start | bytes 602120 | tf_op jit(solution)/shard_map/ppermute | solution.py:38
  21.9 0.0 collective-permute-done
  21.9 0.0 copy-start.7
  21.9 5.1 %collective-permute-start.3 = (bf16[2,784,128]{2,1,0:T(8,128)(2,1)S(1)}, bf16[2,784,128]{2,1,0:T(8,128)(2,1)S(1)}, u32[]{:S(2)}, u32[]{:S(2)}) collective-permute-start(bf16[2,784,128]{2,1,0:T(8,128)(2,1)S(1)} %constant_dynamic-update-slice_fusion.refs_0_), channel_id=1, source_target_pairs={{0,2},{1,15},{2,4},{3,1},{4,6},{5,3},{6,8},{7,5},{8,10},{9,7},{10,... | collective-permute-start | bytes 1204232 | tf_op jit(solution)/shard_map/ppermute | solution.py:38
  27.0 6.3 %collective-permute-done.1 = bf16[1,784,128]{2,1,0:T(8,128)(2,1)S(1)} collective-permute-done((bf16[1,784,128]{2,1,0:T(8,128)(2,1)S(1)}, bf16[1,784,128]{2,1,0:T(8,128)(2,1)S(1)}, u32[]{:S(2)}, u32[]{:S(2)}) %collective-permute-start.1) | collective-permute-done | bytes 200736 | tf_op jit(solution)/shard_map/ppermute | solution.py:38
  33.3 2.3 %collective-permute-start.2 = (bf16[1,784,128]{2,1,0:T(8,128)(2,1)S(1)}, bf16[1,784,128]{2,1,0:T(8,128)(2,1)S(1)}, u32[]{:S(2)}, u32[]{:S(2)}) collective-permute-start(bf16[1,784,128]{2,1,0:T(8,128)(2,1)S(1)} %collective-permute-done.1), channel_id=1, source_target_pairs={{0,1},{1,0},{2,3},{3,2},{4,5},{5,4},{6,7},{7,6},{8,9},{9,8},{10,11... | collective-permute-start | bytes 602120 | tf_op jit(solution)/shard_map/ppermute | solution.py:38
  35.7 1.0 %collective-permute-done.2 = bf16[1,784,128]{2,1,0:T(8,128)(2,1)S(1)} collective-permute-done((bf16[1,784,128]{2,1,0:T(8,128)(2,1)S(1)}, bf16[1,784,128]{2,1,0:T(8,128)(2,1)S(1)}, u32[]{:S(2)}, u32[]{:S(2)}) %collective-permute-start.2) | collective-permute-done | bytes 200736 | tf_op jit(solution)/shard_map/ppermute | solution.py:38
  36.8 0.0 copy-start.6
  36.8 5.1 %collective-permute-start.4 = (bf16[2,784,128]{2,1,0:T(8,128)(2,1)S(1)}, bf16[2,784,128]{2,1,0:T(8,128)(2,1)S(1)}, u32[]{:S(2)}, u32[]{:S(2)}) collective-permute-start(bf16[2,784,128]{2,1,0:T(8,128)(2,1)S(1)} %constant_dynamic-update-slice_fusion.2.refs_1_), channel_id=1, source_target_pairs={{0,2},{1,15},{2,4},{3,1},{4,6},{5,3},{6,8},{7,5},{8,10},{9,7},{10,... | collective-permute-start | bytes 1204232 | tf_op jit(solution)/shard_map/ppermute | solution.py:38
  41.9 0.0 collective-permute-done.3.refs_2_
  41.9 0.0 copy-start.2
  41.9 3.0 %collective-permute-start.5 = (bf16[2,784,128]{2,1,0:T(8,128)(2,1)S(1)}, bf16[2,784,128]{2,1,0:T(8,128)(2,1)S(1)}, u32[]{:S(2)}, u32[]{:S(2)}) collective-permute-start(bf16[2,784,128]{2,1,0:T(8,128)(2,1)S(1)} %collective-permute-done.3.refs_2_), channel_id=1, source_target_pairs={{0,2},{1,15},{2,4},{3,1},{4,6},{5,3},{6,8},{7,5},{8,10},{9,7},{10,... | collective-permute-start | bytes 1204232 | tf_op jit(solution)/shard_map/ppermute | solution.py:38
  44.9 1.8 %collective-permute-done.4.refs_3_ = bf16[2,784,128]{2,1,0:T(8,128)(2,1)S(1)} collective-permute-done((bf16[2,784,128]{2,1,0:T(8,128)(2,1)S(1)}, bf16[2,784,128]{2,1,0:T(8,128)(2,1)S(1)}, u32[]{:S(2)}, u32[]{:S(2)}) %collective-permute-start.4) | collective-permute-done | bytes 401440 | tf_op jit(solution)/shard_map/ppermute | solution.py:38
  46.7 5.0 %collective-permute-start.6 = (bf16[2,784,128]{2,1,0:T(8,128)(2,1)S(1)}, bf16[2,784,128]{2,1,0:T(8,128)(2,1)S(1)}, u32[]{:S(2)}, u32[]{:S(2)}) collective-permute-start(bf16[2,784,128]{2,1,0:T(8,128)(2,1)S(1)} %collective-permute-done.4.refs_3_), channel_id=1, source_target_pairs={{0,2},{1,15},{2,4},{3,1},{4,6},{5,3},{6,8},{7,5},{8,10},{9,7},{10,... | collective-permute-start | bytes 1204232 | tf_op jit(solution)/shard_map/ppermute | solution.py:38
  51.7 0.0 collective-permute-done.5.refs_4_
  51.7 0.0 copy-done.7
  51.7 0.0 copy-done.6
  51.7 0.0 copy-start.4
  51.7 4.6 %collective-permute-start.7 = (bf16[2,784,128]{2,1,0:T(8,128)(2,1)S(1)}, bf16[2,784,128]{2,1,0:T(8,128)(2,1)S(1)}, u32[]{:S(2)}, u32[]{:S(2)}) collective-permute-start(bf16[2,784,128]{2,1,0:T(8,128)(2,1)S(1)} %collective-permute-done.5.refs_4_), channel_id=1, source_target_pairs={{0,2},{1,15},{2,4},{3,1},{4,6},{5,3},{6,8},{7,5},{8,10},{9,7},{10,... | collective-permute-start | bytes 1204232 | tf_op jit(solution)/shard_map/ppermute | solution.py:38
  56.3 0.1 constant_dynamic-update-slice_fusion.7
  56.4 0.1 constant_dynamic-update-slice_fusion.6
  56.4 0.0 collective-permute-done.6.refs_5_
  56.5 0.1 constant_dynamic-update-slice_fusion.5
  56.5 4.5 %collective-permute-done.7.refs_6_ = bf16[2,784,128]{2,1,0:T(8,128)(2,1)S(1)} collective-permute-done((bf16[2,784,128]{2,1,0:T(8,128)(2,1)S(1)}, bf16[2,784,128]{2,1,0:T(8,128)(2,1)S(1)}, u32[]{:S(2)}, u32[]{:S(2)}) %collective-permute-start.7) | collective-permute-done | bytes 401440 | tf_op jit(solution)/shard_map/ppermute | solution.py:38
  61.1 0.1 constant_dynamic-update-slice_fusion.4
  61.1 0.0 copy-done.2
  61.1 0.0 copy-done.3
  61.2 0.0 copy-done.4
  61.2 4.5 %collective-permute-start.8 = (bf16[10,784,128]{2,1,0:T(8,128)(2,1)S(1)}, bf16[10,784,128]{2,1,0:T(8,128)(2,1)}, u32[]{:S(2)}, u32[]{:S(2)}) collective-permute-start(bf16[10,784,128]{2,1,0:T(8,128)(2,1)S(1)} %constant_dynamic-update-slice_fusion.4), channel_id=1, source_target_pairs={{0,1},{1,0},{2,3},{3,2},{4,5},{5,4},{6,7},{7,6},{8,9},{9,8},{10,11... | collective-permute-start | bytes 6021128 | tf_op jit(solution)/shard_map/ppermute | solution.py:38
  65.6 2.8 %collective-permute-start.9 = (bf16[2,784,128]{2,1,0:T(8,128)(2,1)S(1)}, bf16[2,784,128]{2,1,0:T(8,128)(2,1)S(1)}, u32[]{:S(2)}, u32[]{:S(2)}) collective-permute-start(bf16[2,784,128]{2,1,0:T(8,128)(2,1)S(1)} %collective-permute-done.6.refs_5_), channel_id=1, source_target_pairs={{0,2},{1,15},{2,4},{3,1},{4,6},{5,3},{6,8},{7,5},{8,10},{9,7},{10,... | collective-permute-start | bytes 1204232 | tf_op jit(solution)/shard_map/ppermute | solution.py:38
  68.4 2.6 %collective-permute-start.10 = (bf16[1,784,128]{2,1,0:T(8,128)(2,1)S(1)}, bf16[1,784,128]{2,1,0:T(8,128)(2,1)S(1)}, u32[]{:S(2)}, u32[]{:S(2)}) collective-permute-start(bf16[1,784,128]{2,1,0:T(8,128)(2,1)S(1)} %slice.8), channel_id=1, source_target_pairs={{0,2},{1,15},{2,4},{3,1},{4,6},{5,3},{6,8},{7,5},{8,10},{9,7},{10,... | collective-permute-start | bytes 602120 | tf_op jit(solution)/shard_map/ppermute | solution.py:38
  71.1 3.5 %collective-permute-done.9.refs_0_ = bf16[2,784,128]{2,1,0:T(8,128)(2,1)S(1)} collective-permute-done((bf16[2,784,128]{2,1,0:T(8,128)(2,1)S(1)}, bf16[2,784,128]{2,1,0:T(8,128)(2,1)S(1)}, u32[]{:S(2)}, u32[]{:S(2)}) %collective-permute-start.9) | collective-permute-done | bytes 401440 | tf_op jit(solution)/shard_map/ppermute | solution.py:38
  74.6 3.7 %collective-permute-start.11 = (bf16[1,784,128]{2,1,0:T(8,128)(2,1)S(1)}, bf16[1,784,128]{2,1,0:T(8,128)(2,1)S(1)}, u32[]{:S(2)}, u32[]{:S(2)}) collective-permute-start(bf16[1,784,128]{2,1,0:T(8,128)(2,1)S(1)} %slice.9), channel_id=1, source_target_pairs={{0,2},{1,15},{2,4},{3,1},{4,6},{5,3},{6,8},{7,5},{8,10},{9,7},{10,... | collective-permute-start | bytes 602120 | tf_op jit(solution)/shard_map/ppermute | solution.py:38
  78.3 0.0 collective-permute-done.10.refs_1_
  78.3 2.7 %collective-permute-done.11.refs_2_ = bf16[1,784,128]{2,1,0:T(8,128)(2,1)S(1)} collective-permute-done((bf16[1,784,128]{2,1,0:T(8,128)(2,1)S(1)}, bf16[1,784,128]{2,1,0:T(8,128)(2,1)S(1)}, u32[]{:S(2)}, u32[]{:S(2)}) %collective-permute-start.11) | collective-permute-done | bytes 200736 | tf_op jit(solution)/shard_map/ppermute | solution.py:38
  81.0 1.0 %pad_maximum_fusion = bf16[4,784,128]{2,1,0:T(8,128)(2,1)} fusion(bf16[1,784,128]{2,1,0:T(8,128)(2,1)S(1)} %collective-permute-done.11.refs_2_, bf16[1,784,128]{2,1,0:T(8,128)(2,1)S(1)} %collective-permute-done.10.refs_1_, bf16[2,784,128]{2,1,0:T(8,128)(2,1)S(1)} %collective-permute-done.9.refs_0_), kind=kLoop, calls=%fused_computation | loop fusion | flops 802816 | bytes 1605632 | tf_op jit(solution)/shard_map/concatenate | solution.py:206
  82.0 6.3 %collective-permute-start.12 = (bf16[4,784,128]{2,1,0:T(8,128)(2,1)}, bf16[4,784,128]{2,1,0:T(8,128)(2,1)}, u32[]{:S(2)}, u32[]{:S(2)}) collective-permute-start(bf16[4,784,128]{2,1,0:T(8,128)(2,1)} %pad_maximum_fusion), channel_id=1, source_target_pairs={{0,1},{1,0},{2,3},{3,2},{4,5},{5,4},{6,7},{7,6},{8,9},{9,8},{10,11... | collective-permute-start | bytes 2408456 | tf_op jit(solution)/shard_map/ppermute | solution.py:38
  88.4 0.0 collective-permute-done.8.refs_7_
  88.4 0.0 all-to-all-done
  88.4 6.0 %shard_map.38.early_ref = f32[9,128,128]{2,1,0:T(8,128)} custom-call(bf16[64,128,128]{2,1,0:T(8,128)(2,1)S(1)} %bitcast.2, bf16[2,784,128]{2,1,0:T(8,128)(2,1)} %copy-done.7, bf16[2,784,128]{2,1,0:T(8,128)(2,1)} %copy-done.6, bf16[2,784,128]{2,1,0:T(8,128)(2,1)} %copy-done.2, bf16[2,784,128]{2,1,0:T(8,128)(2,1)} %copy-done.3, ...), custom_call_target="tpu_custom_call" | custom-call | tf_op jit(solution)/shard_map/pallas_call | solution.py:114
  94.4 0.0 collective-permute-done.12.refs_3_
  94.4 1.1 %copy-done = f32[9,128,128]{2,1,0:T(8,128)S(1)} copy-done((f32[9,128,128]{2,1,0:T(8,128)S(1)}, f32[9,128,128]{2,1,0:T(8,128)}, u32[]{:S(2)}) %copy-start) | copy-done | bytes 589848
  95.4 3.5 %shard_map.39 = f32[8,128,128]{2,1,0:T(8,128)} custom-call(f32[9,128,128]{2,1,0:T(8,128)S(1)} %copy-done, bf16[64,128,128]{2,1,0:T(8,128)(2,1)S(1)} %bitcast.3, bf16[2,784,128]{2,1,0:T(8,128)(2,1)S(1)} %collective-permute-done.9.refs_0_, bf16[1,784,128]{2,1,0:T(8,128)(2,1)S(1)} %collective-permute-done.10.refs_1_, ...), custom_call_target="tpu_custom_call" | custom-call | tf_op jit(solution)/shard_map/pallas_call | solution.py:114
  (13 shorter events, 0.2 us)
Async XLA Ops:
  3.1 13.6 %copy-start.8 = (bf16[1,784,128]{2,1,0:T(8,128)(2,1)S(1)}, bf16[1,784,128]{2,1,0:T(8,128)(2,1)}, u32[]{:S(2)}) copy-start(bf16[1,784,128]{2,1,0:T(8,128)(2,1)} %get-tuple-element.8) | copy-start | bytes 602116
  3.1 85.2 %all-to-all-start = ((bf16[16,512,128]{2,1,0:T(8,128)(2,1)}), bf16[16,512,128]{2,1,0:T(8,128)(2,1)S(1)}, u32[]{:S(2)}, u32[]{:S(2)}) async-start(bf16[16,512,128]{2,1,0:T(8,128)(2,1)} %get-tuple-element.7), calls=%async_computation | async-start | bytes 4194304 | tf_op jit(solution)/shard_map/all_to_all | solution.py:191
  16.7 5.1 %collective-permute-start = (bf16[1,784,128]{2,1,0:T(8,128)(2,1)S(1)}, bf16[1,784,128]{2,1,0:T(8,128)(2,1)S(1)}, u32[]{:S(2)}, u32[]{:S(2)}) collective-permute-start(bf16[1,784,128]{2,1,0:T(8,128)(2,1)S(1)} %copy-done.8), channel_id=1, source_target_pairs={{0,1},{1,0},{2,3},{3,2},{4,5},{5,4},{6,7},{7,6},{8,9},{9,8},{10,11... | collective-permute-start | bytes 602120 | tf_op jit(solution)/shard_map/ppermute | solution.py:38
  19.6 13.7 %collective-permute-start.1 = (bf16[1,784,128]{2,1,0:T(8,128)(2,1)S(1)}, bf16[1,784,128]{2,1,0:T(8,128)(2,1)S(1)}, u32[]{:S(2)}, u32[]{:S(2)}) collective-permute-start(bf16[1,784,128]{2,1,0:T(8,128)(2,1)S(1)} %copy-done.8), channel_id=1, source_target_pairs={{0,16},{1,17},{2,18},{3,19},{4,20},{5,21},{6,22},{7,23},{8,24},{9,... | collective-permute-start | bytes 602120 | tf_op jit(solution)/shard_map/ppermute | solution.py:38
  21.9 29.8 %copy-start.7 = (bf16[2,784,128]{2,1,0:T(8,128)(2,1)}, bf16[2,784,128]{2,1,0:T(8,128)(2,1)S(1)}, u32[]{:S(2)}) copy-start(bf16[2,784,128]{2,1,0:T(8,128)(2,1)S(1)} %constant_dynamic-update-slice_fusion.refs_0_) | copy-start | bytes 1204228
  21.9 20.0 %collective-permute-start.3 = (bf16[2,784,128]{2,1,0:T(8,128)(2,1)S(1)}, bf16[2,784,128]{2,1,0:T(8,128)(2,1)S(1)}, u32[]{:S(2)}, u32[]{:S(2)}) collective-permute-start(bf16[2,784,128]{2,1,0:T(8,128)(2,1)S(1)} %constant_dynamic-update-slice_fusion.refs_0_), channel_id=1, source_target_pairs={{0,2},{1,15},{2,4},{3,1},{4,6},{5,3},{6,8},{7,5},{8,10},{9,7},{10,... | collective-permute-start | bytes 1204232 | tf_op jit(solution)/shard_map/ppermute | solution.py:38
  33.3 3.4 %collective-permute-start.2 = (bf16[1,784,128]{2,1,0:T(8,128)(2,1)S(1)}, bf16[1,784,128]{2,1,0:T(8,128)(2,1)S(1)}, u32[]{:S(2)}, u32[]{:S(2)}) collective-permute-start(bf16[1,784,128]{2,1,0:T(8,128)(2,1)S(1)} %collective-permute-done.1), channel_id=1, source_target_pairs={{0,1},{1,0},{2,3},{3,2},{4,5},{5,4},{6,7},{7,6},{8,9},{9,8},{10,11... | collective-permute-start | bytes 602120 | tf_op jit(solution)/shard_map/ppermute | solution.py:38
  36.8 14.9 %copy-start.6 = (bf16[2,784,128]{2,1,0:T(8,128)(2,1)}, bf16[2,784,128]{2,1,0:T(8,128)(2,1)S(1)}, u32[]{:S(2)}) copy-start(bf16[2,784,128]{2,1,0:T(8,128)(2,1)S(1)} %constant_dynamic-update-slice_fusion.2.refs_1_) | copy-start | bytes 1204228
  36.8 9.9 %collective-permute-start.4 = (bf16[2,784,128]{2,1,0:T(8,128)(2,1)S(1)}, bf16[2,784,128]{2,1,0:T(8,128)(2,1)S(1)}, u32[]{:S(2)}, u32[]{:S(2)}) collective-permute-start(bf16[2,784,128]{2,1,0:T(8,128)(2,1)S(1)} %constant_dynamic-update-slice_fusion.2.refs_1_), channel_id=1, source_target_pairs={{0,2},{1,15},{2,4},{3,1},{4,6},{5,3},{6,8},{7,5},{8,10},{9,7},{10,... | collective-permute-start | bytes 1204232 | tf_op jit(solution)/shard_map/ppermute | solution.py:38
  41.9 19.3 %copy-start.2 = (bf16[2,784,128]{2,1,0:T(8,128)(2,1)}, bf16[2,784,128]{2,1,0:T(8,128)(2,1)S(1)}, u32[]{:S(2)}) copy-start(bf16[2,784,128]{2,1,0:T(8,128)(2,1)S(1)} %collective-permute-done.3.refs_2_) | copy-start | bytes 1204228
  41.9 9.8 %collective-permute-start.5 = (bf16[2,784,128]{2,1,0:T(8,128)(2,1)S(1)}, bf16[2,784,128]{2,1,0:T(8,128)(2,1)S(1)}, u32[]{:S(2)}, u32[]{:S(2)}) collective-permute-start(bf16[2,784,128]{2,1,0:T(8,128)(2,1)S(1)} %collective-permute-done.3.refs_2_), channel_id=1, source_target_pairs={{0,2},{1,15},{2,4},{3,1},{4,6},{5,3},{6,8},{7,5},{8,10},{9,7},{10,... | collective-permute-start | bytes 1204232 | tf_op jit(solution)/shard_map/ppermute | solution.py:38
  46.7 14.5 %copy-start.3 = (bf16[2,784,128]{2,1,0:T(8,128)(2,1)}, bf16[2,784,128]{2,1,0:T(8,128)(2,1)S(1)}, u32[]{:S(2)}) copy-start(bf16[2,784,128]{2,1,0:T(8,128)(2,1)S(1)} %collective-permute-done.4.refs_3_) | copy-start | bytes 1204228
  46.7 9.8 %collective-permute-start.6 = (bf16[2,784,128]{2,1,0:T(8,128)(2,1)S(1)}, bf16[2,784,128]{2,1,0:T(8,128)(2,1)S(1)}, u32[]{:S(2)}, u32[]{:S(2)}) collective-permute-start(bf16[2,784,128]{2,1,0:T(8,128)(2,1)S(1)} %collective-permute-done.4.refs_3_), channel_id=1, source_target_pairs={{0,2},{1,15},{2,4},{3,1},{4,6},{5,3},{6,8},{7,5},{8,10},{9,7},{10,... | collective-permute-start | bytes 1204232 | tf_op jit(solution)/shard_map/ppermute | solution.py:38
  51.7 9.4 %copy-start.4 = (bf16[2,784,128]{2,1,0:T(8,128)(2,1)}, bf16[2,784,128]{2,1,0:T(8,128)(2,1)S(1)}, u32[]{:S(2)}) copy-start(bf16[2,784,128]{2,1,0:T(8,128)(2,1)S(1)} %collective-permute-done.5.refs_4_) | copy-start | bytes 1204228
  51.7 9.4 %collective-permute-start.7 = (bf16[2,784,128]{2,1,0:T(8,128)(2,1)S(1)}, bf16[2,784,128]{2,1,0:T(8,128)(2,1)S(1)}, u32[]{:S(2)}, u32[]{:S(2)}) collective-permute-start(bf16[2,784,128]{2,1,0:T(8,128)(2,1)S(1)} %collective-permute-done.5.refs_4_), channel_id=1, source_target_pairs={{0,2},{1,15},{2,4},{3,1},{4,6},{5,3},{6,8},{7,5},{8,10},{9,7},{10,... | collective-permute-start | bytes 1204232 | tf_op jit(solution)/shard_map/ppermute | solution.py:38
  56.5 21.8 %copy-start.5 = (bf16[2,784,128]{2,1,0:T(8,128)(2,1)}, bf16[2,784,128]{2,1,0:T(8,128)(2,1)S(1)}, u32[]{:S(2)}) copy-start(bf16[2,784,128]{2,1,0:T(8,128)(2,1)S(1)} %collective-permute-done.6.refs_5_) | copy-start | bytes 1204228
  61.1 27.3 %copy-start.1 = (bf16[2,784,128]{2,1,0:T(8,128)(2,1)}, bf16[2,784,128]{2,1,0:T(8,128)(2,1)S(1)}, u32[]{:S(2)}) copy-start(bf16[2,784,128]{2,1,0:T(8,128)(2,1)S(1)} %collective-permute-done.7.refs_6_) | copy-start | bytes 1204228
  61.2 27.2 %collective-permute-start.8 = (bf16[10,784,128]{2,1,0:T(8,128)(2,1)S(1)}, bf16[10,784,128]{2,1,0:T(8,128)(2,1)}, u32[]{:S(2)}, u32[]{:S(2)}) collective-permute-start(bf16[10,784,128]{2,1,0:T(8,128)(2,1)S(1)} %constant_dynamic-update-slice_fusion.4), channel_id=1, source_target_pairs={{0,1},{1,0},{2,3},{3,2},{4,5},{5,4},{6,7},{7,6},{8,9},{9,8},{10,11... | collective-permute-start | bytes 6021128 | tf_op jit(solution)/shard_map/ppermute | solution.py:38
  65.6 8.9 %collective-permute-start.9 = (bf16[2,784,128]{2,1,0:T(8,128)(2,1)S(1)}, bf16[2,784,128]{2,1,0:T(8,128)(2,1)S(1)}, u32[]{:S(2)}, u32[]{:S(2)}) collective-permute-start(bf16[2,784,128]{2,1,0:T(8,128)(2,1)S(1)} %collective-permute-done.6.refs_5_), channel_id=1, source_target_pairs={{0,2},{1,15},{2,4},{3,1},{4,6},{5,3},{6,8},{7,5},{8,10},{9,7},{10,... | collective-permute-start | bytes 1204232 | tf_op jit(solution)/shard_map/ppermute | solution.py:38
  68.4 9.8 %collective-permute-start.10 = (bf16[1,784,128]{2,1,0:T(8,128)(2,1)S(1)}, bf16[1,784,128]{2,1,0:T(8,128)(2,1)S(1)}, u32[]{:S(2)}, u32[]{:S(2)}) collective-permute-start(bf16[1,784,128]{2,1,0:T(8,128)(2,1)S(1)} %slice.8), channel_id=1, source_target_pairs={{0,2},{1,15},{2,4},{3,1},{4,6},{5,3},{6,8},{7,5},{8,10},{9,7},{10,... | collective-permute-start | bytes 602120 | tf_op jit(solution)/shard_map/ppermute | solution.py:38
  74.6 6.5 %collective-permute-start.11 = (bf16[1,784,128]{2,1,0:T(8,128)(2,1)S(1)}, bf16[1,784,128]{2,1,0:T(8,128)(2,1)S(1)}, u32[]{:S(2)}, u32[]{:S(2)}) collective-permute-start(bf16[1,784,128]{2,1,0:T(8,128)(2,1)S(1)} %slice.9), channel_id=1, source_target_pairs={{0,2},{1,15},{2,4},{3,1},{4,6},{5,3},{6,8},{7,5},{8,10},{9,7},{10,... | collective-permute-start | bytes 602120 | tf_op jit(solution)/shard_map/ppermute | solution.py:38
  82.0 12.3 %collective-permute-start.12 = (bf16[4,784,128]{2,1,0:T(8,128)(2,1)}, bf16[4,784,128]{2,1,0:T(8,128)(2,1)}, u32[]{:S(2)}, u32[]{:S(2)}) collective-permute-start(bf16[4,784,128]{2,1,0:T(8,128)(2,1)} %pad_maximum_fusion), channel_id=1, source_target_pairs={{0,1},{1,0},{2,3},{3,2},{4,5},{5,4},{6,7},{7,6},{8,9},{9,8},{10,11... | collective-permute-start | bytes 2408456 | tf_op jit(solution)/shard_map/ppermute | solution.py:38
  94.4 1.1 %copy-start = (f32[9,128,128]{2,1,0:T(8,128)S(1)}, f32[9,128,128]{2,1,0:T(8,128)}, u32[]{:S(2)}) copy-start(f32[9,128,128]{2,1,0:T(8,128)} %shard_map.38.early_ref) | copy-start | bytes 1769476

commit v6 on v4

--- a/solution.py
+++ b/solution.py
@@ -93,9 +93,15 @@
             total[pair_block] += prod
         return carry
 
-    for copy in piece_copies:
-        copy.wait()
-    lax.fori_loop(0, rows_v.shape[0], one_piece, 0, unroll=2)
+    start, end = 0, 0
+    for copy, ref in zip(piece_copies, piece_refs):
+        copy.wait()
+        end += ref.shape[0]
+        if (end - start) % 2 == 0:
+            length = end - start
+            step = max(n for n in (2, 3, 4) if length % n == 0)
+            lax.fori_loop(start, end, one_piece, 0, unroll=step)
+            start = end
 
 
 def early_products(metric_ref, *refs):
@@ -140,9 +146,12 @@
     )(*taken, metric, *pieces)
 
 
-def copy_to_each(source_ref, copies_ref, sems):
+def copy_to_each(source_ref, copies_ref, source_v, sems):
     count = copies_ref.shape[0]
-    copies = [pltpu.make_async_copy(source_ref, copies_ref.at[i], sems.at[i]) for i in range(count)]
+    taken = pltpu.make_async_copy(source_ref, source_v, sems.at[count])
+    taken.start()
+    taken.wait()
+    copies = [pltpu.make_async_copy(source_v, copies_ref.at[i], sems.at[i]) for i in range(count)]
     for copy in copies:
         copy.start()
     for copy in copies:
@@ -159,7 +168,7 @@
         out_shape=jax.ShapeDtypeStruct((rows, *metric.shape), metric.dtype),
         in_specs=[pl.BlockSpec(memory_space=pltpu.HBM)],
         out_specs=pl.BlockSpec(memory_space=pltpu.HBM),
-        scratch_shapes=[pltpu.SemaphoreType.DMA((rows,))],
+        scratch_shapes=[pltpu.VMEM(metric.shape, metric.dtype), pltpu.SemaphoreType.DMA((rows + 1,))],
     )(metric)
     band = lax.all_to_all(copies, "row", split_axis=0, concat_axis=0, tiled=True)
     band = band.reshape(band_blocks, BLK, out_cols)
@@ -174,12 +183,12 @@
     b2 = sent(b1, RING)
     a3 = sent(a2, RING)
     a4 = sent(a3[:1], RING)
-    early = [a1, b1, a2, b2, a3]
-    late = [sent(a3, X_PARTNER), a4, sent(a4, X_PARTNER)]
-    early_other = sent(jnp.concatenate(early), CORE)
-    late_other = sent(jnp.concatenate(late), CORE)
-    early = [near, near_x, *early, early_other]
-    late = [*late, late_other]
+    b3 = sent(b2, RING)
+    a4_x = sent(a4, X_PARTNER)
+    early_other = sent(jnp.concatenate([a1, b1, a2, a3]), CORE)
+    late_other = sent(jnp.concatenate([b2, b3, a4, a4_x]), CORE)
+    early = [near, near_x, a1, b1, a2, a3, early_other]
+    late = [b2, b3, a4, a4_x, late_other]
     total_shape = (PAIR_BLOCKS + 1, BLK, out_cols)
     total = kernel_call(
         early_products,

time: 163 us -> 93.2 us (0.57)
  Pallas kernels: 75.6 us -> 11.4 us
  waiting for transfers between devices: 24.6 us -> 13.2 us
  starting transfers between devices: 59 us -> 64.9 us
    pallas_call x1, Pallas kernels: 64.8 us -> 2.39 us  [on_device(): pl.pallas_call(copy_to_each, out_shape=jax.ShapeDtypeStruct((rows, *metri...]
    ppermute x13, waiting for transfers between devices: 24.6 us -> 13.2 us  [sent(): return lax.ppermute(value, axis, perm)]
    ppermute x13, starting transfers between devices: 45.4 us -> 51.3 us  [sent(): return lax.ppermute(value, axis, perm)]
    pallas_call x2, Pallas kernels: 10.8 us -> 9.04 us  [kernel_call(): pl.pallas_call(body, out_shape=out_shape, in_specs=[pl.BlockSpec(memory_s...]
  transfers between devices with their start and end apart: 14 -> 14, of which waited for: 7 -> 6; matrix products, arithmetic and copies ran while one was open for 1% -> 2% of each run, Pallas kernels for 4% -> 5%
where the time goes in v6:
time: 93.2 us; the launch traced here: 92.6 us
  starting transfers between devices  64.9 us (70%)
  waiting for transfers between devices  13.2 us (14%)
  Pallas kernels  11.4 us (12%)
  other arithmetic  1.57 us (2%)
  local copies, waits for them, and re-layouts  1.16 us (1%)
    ppermute x13, starting transfers between devices, sent(): return lax.ppermute(value, axis, perm)  51.3 us
    all_to_all x1, starting transfers between devices, on_device(): lax.all_to_all(copies, 'row', split_axis=0, concat_axis=0, tiled=True)  13.6 us
    ppermute x13, waiting for transfers between devices, sent(): return lax.ppermute(value, axis, perm)  13.2 us
    pallas_call x2, Pallas kernels, kernel_call(): pl.pallas_call(body, out_shape=out_shape, in_specs=[pl.BlockSpec(memory_s...  9.04 us
    pallas_call x1, Pallas kernels, on_device(): pl.pallas_call(copy_to_each, out_shape=jax.ShapeDtypeStruct((rows, *metri...  2.39 us
  transfers between devices with their start and end apart: 14, of which 6 were waited for; matrix products, arithmetic and copies ran while one was open for 2% of the time, Pallas kernels for 5%

profile of v6, /device:TPU:1, one launch (start us, length us, event | category | flops | bytes accessed | tf_op | source)
XLA Modules:
  0.0 92.6 jit_solution(1090664684908842790)
XLA Ops:
  0.0 2.4 %shard_map.37 = bf16[16,512,128]{2,1,0:T(8,128)(2,1)} custom-call(bf16[512,128]{1,0:T(8,128)(2,1)} %source_ref.1), custom_call_target="tpu_custom_call" | custom-call | tf_op jit(solution)/shard_map/pallas_call | solution.py:166
  2.4 0.0 copy-start.8
  2.4 0.0 copy-start.7
  2.4 13.6 %all-to-all-start = ((bf16[16,512,128]{2,1,0:T(8,128)(2,1)}), bf16[16,512,128]{2,1,0:T(8,128)(2,1)S(1)}, u32[]{:S(2)}, u32[]{:S(2)}) async-start(bf16[16,512,128]{2,1,0:T(8,128)(2,1)} %shard_map.37), calls=%async_computation | async-start | bytes 4194304 | tf_op jit(solution)/shard_map/all_to_all | solution.py:173
  16.0 0.0 copy-done.8
  16.0 0.1 fusion.3
  16.1 0.0 copy-done.7
  16.1 2.9 %collective-permute-start = (bf16[1,784,128]{2,1,0:T(8,128)(2,1)S(1)}, bf16[1,784,128]{2,1,0:T(8,128)(2,1)S(1)}, u32[]{:S(2)}, u32[]{:S(2)}) collective-permute-start(bf16[1,784,128]{2,1,0:T(8,128)(2,1)S(1)} %maximum_bitcast_fusion), channel_id=1, source_target_pairs={{0,1},{1,0},{2,3},{3,2},{4,5},{5,4},{6,7},{7,6},{8,9},{9,8},{10,11... | collective-permute-start | bytes 602120 | tf_op jit(solution)/shard_map/ppermute | solution.py:37
  19.0 2.2 %collective-permute-start.1 = (bf16[1,784,128]{2,1,0:T(8,128)(2,1)S(1)}, bf16[1,784,128]{2,1,0:T(8,128)(2,1)S(1)}, u32[]{:S(2)}, u32[]{:S(2)}) collective-permute-start(bf16[1,784,128]{2,1,0:T(8,128)(2,1)S(1)} %maximum_bitcast_fusion), channel_id=1, source_target_pairs={{0,16},{1,17},{2,18},{3,19},{4,20},{5,21},{6,22},{7,23},{8,24},{9,... | collective-permute-start | bytes 602120 | tf_op jit(solution)/shard_map/ppermute | solution.py:37
  21.2 0.0 collective-permute-done
  21.3 0.0 copy-start.5
  21.3 5.1 %collective-permute-start.3 = (bf16[2,784,128]{2,1,0:T(8,128)(2,1)S(1)}, bf16[2,784,128]{2,1,0:T(8,128)(2,1)S(1)}, u32[]{:S(2)}, u32[]{:S(2)}) collective-permute-start(bf16[2,784,128]{2,1,0:T(8,128)(2,1)S(1)} %pad_maximum_fusion.2.refs_0_), channel_id=1, source_target_pairs={{0,2},{1,15},{2,4},{3,1},{4,6},{5,3},{6,8},{7,5},{8,10},{9,7},{10,... | collective-permute-start | bytes 1204232 | tf_op jit(solution)/shard_map/ppermute | solution.py:37
  26.4 6.2 %collective-permute-done.1 = bf16[1,784,128]{2,1,0:T(8,128)(2,1)S(1)} collective-permute-done((bf16[1,784,128]{2,1,0:T(8,128)(2,1)S(1)}, bf16[1,784,128]{2,1,0:T(8,128)(2,1)S(1)}, u32[]{:S(2)}, u32[]{:S(2)}) %collective-permute-start.1) | collective-permute-done | bytes 200736 | tf_op jit(solution)/shard_map/ppermute | solution.py:37
  32.6 2.3 %collective-permute-start.2 = (bf16[1,784,128]{2,1,0:T(8,128)(2,1)S(1)}, bf16[1,784,128]{2,1,0:T(8,128)(2,1)S(1)}, u32[]{:S(2)}, u32[]{:S(2)}) collective-permute-start(bf16[1,784,128]{2,1,0:T(8,128)(2,1)S(1)} %collective-permute-done.1), channel_id=1, source_target_pairs={{0,1},{1,0},{2,3},{3,2},{4,5},{5,4},{6,7},{7,6},{8,9},{9,8},{10,11... | collective-permute-start | bytes 602120 | tf_op jit(solution)/shard_map/ppermute | solution.py:37
  35.0 1.0 %collective-permute-done.2 = bf16[1,784,128]{2,1,0:T(8,128)(2,1)S(1)} collective-permute-done((bf16[1,784,128]{2,1,0:T(8,128)(2,1)S(1)}, bf16[1,784,128]{2,1,0:T(8,128)(2,1)S(1)}, u32[]{:S(2)}, u32[]{:S(2)}) %collective-permute-start.2) | collective-permute-done | bytes 200736 | tf_op jit(solution)/shard_map/ppermute | solution.py:37
  36.0 0.0 copy-start.6
  36.0 5.1 %collective-permute-start.4 = (bf16[2,784,128]{2,1,0:T(8,128)(2,1)S(1)}, bf16[2,784,128]{2,1,0:T(8,128)(2,1)S(1)}, u32[]{:S(2)}, u32[]{:S(2)}) collective-permute-start(bf16[2,784,128]{2,1,0:T(8,128)(2,1)S(1)} %constant_dynamic-update-slice_fusion.refs_1_), channel_id=1, source_target_pairs={{0,2},{1,15},{2,4},{3,1},{4,6},{5,3},{6,8},{7,5},{8,10},{9,7},{10,... | collective-permute-start | bytes 1204232 | tf_op jit(solution)/shard_map/ppermute | solution.py:37
  41.1 0.0 collective-permute-done.3.refs_2_
  41.2 0.0 copy-start.2
  41.2 3.0 %collective-permute-start.5 = (bf16[2,784,128]{2,1,0:T(8,128)(2,1)S(1)}, bf16[2,784,128]{2,1,0:T(8,128)(2,1)S(1)}, u32[]{:S(2)}, u32[]{:S(2)}) collective-permute-start(bf16[2,784,128]{2,1,0:T(8,128)(2,1)S(1)} %collective-permute-done.3.refs_2_), channel_id=1, source_target_pairs={{0,2},{1,15},{2,4},{3,1},{4,6},{5,3},{6,8},{7,5},{8,10},{9,7},{10,... | collective-permute-start | bytes 1204232 | tf_op jit(solution)/shard_map/ppermute | solution.py:37
  44.1 1.8 %collective-permute-done.4.refs_3_ = bf16[2,784,128]{2,1,0:T(8,128)(2,1)S(1)} collective-permute-done((bf16[2,784,128]{2,1,0:T(8,128)(2,1)S(1)}, bf16[2,784,128]{2,1,0:T(8,128)(2,1)S(1)}, u32[]{:S(2)}, u32[]{:S(2)}) %collective-permute-start.4) | collective-permute-done | bytes 401440 | tf_op jit(solution)/shard_map/ppermute | solution.py:37
  45.9 5.0 %collective-permute-start.8 = (bf16[2,784,128]{2,1,0:T(8,128)(2,1)S(1)}, bf16[2,784,128]{2,1,0:T(8,128)(2,1)S(1)}, u32[]{:S(2)}, u32[]{:S(2)}) collective-permute-start(bf16[2,784,128]{2,1,0:T(8,128)(2,1)S(1)} %collective-permute-done.4.refs_3_), channel_id=1, source_target_pairs={{0,2},{1,15},{2,4},{3,1},{4,6},{5,3},{6,8},{7,5},{8,10},{9,7},{10,... | collective-permute-start | bytes 1204232 | tf_op jit(solution)/shard_map/ppermute | solution.py:37
  51.0 0.0 collective-permute-done.5.refs_4_
  51.0 0.0 copy-start.4
  51.0 4.6 %collective-permute-start.6 = (bf16[2,784,128]{2,1,0:T(8,128)(2,1)S(1)}, bf16[2,784,128]{2,1,0:T(8,128)(2,1)S(1)}, u32[]{:S(2)}, u32[]{:S(2)}) collective-permute-start(bf16[2,784,128]{2,1,0:T(8,128)(2,1)S(1)} %collective-permute-done.5.refs_4_), channel_id=1, source_target_pairs={{0,2},{1,15},{2,4},{3,1},{4,6},{5,3},{6,8},{7,5},{8,10},{9,7},{10,... | collective-permute-start | bytes 1204232 | tf_op jit(solution)/shard_map/ppermute | solution.py:37
  55.5 0.2 collective-permute-done.8.refs_0_
  55.7 5.3 %collective-permute-start.9 = (bf16[2,784,128]{2,1,0:T(8,128)(2,1)S(1)}, bf16[2,784,128]{2,1,0:T(8,128)(2,1)S(1)}, u32[]{:S(2)}, u32[]{:S(2)}) collective-permute-start(bf16[2,784,128]{2,1,0:T(8,128)(2,1)S(1)} %collective-permute-done.8.refs_0_), channel_id=1, source_target_pairs={{0,2},{1,15},{2,4},{3,1},{4,6},{5,3},{6,8},{7,5},{8,10},{9,7},{10,... | collective-permute-start | bytes 1204232 | tf_op jit(solution)/shard_map/ppermute | solution.py:37
  61.1 0.0 collective-permute-done.6.refs_5_
  61.1 0.0 copy-done.5
  61.1 4.6 %collective-permute-start.10 = (bf16[1,784,128]{2,1,0:T(8,128)(2,1)S(1)}, bf16[1,784,128]{2,1,0:T(8,128)(2,1)S(1)}, u32[]{:S(2)}, u32[]{:S(2)}) collective-permute-start(bf16[1,784,128]{2,1,0:T(8,128)(2,1)S(1)} %slice.4), channel_id=1, source_target_pairs={{0,2},{1,15},{2,4},{3,1},{4,6},{5,3},{6,8},{7,5},{8,10},{9,7},{10,... | collective-permute-start | bytes 602120 | tf_op jit(solution)/shard_map/ppermute | solution.py:37
  65.7 0.2 pad_maximum_fusion
  65.9 0.0 copy-done.2
  65.9 0.0 copy-done.3
  65.9 0.0 copy-done.4
  65.9 0.0 copy-done.1
  65.9 1.9 %collective-permute-start.7 = (bf16[8,784,128]{2,1,0:T(8,128)(2,1)S(1)}, bf16[8,784,128]{2,1,0:T(8,128)(2,1)}, u32[]{:S(2)}, u32[]{:S(2)}) collective-permute-start(bf16[8,784,128]{2,1,0:T(8,128)(2,1)S(1)} %pad_maximum_fusion), channel_id=1, source_target_pairs={{0,1},{1,0},{2,3},{3,2},{4,5},{5,4},{6,7},{7,6},{8,9},{9,8},{10,11... | collective-permute-start | bytes 4816904 | tf_op jit(solution)/shard_map/ppermute | solution.py:37
  67.9 0.5 collective-permute-done.10.refs_2_
  68.3 2.9 %collective-permute-start.11 = (bf16[1,784,128]{2,1,0:T(8,128)(2,1)S(1)}, bf16[1,784,128]{2,1,0:T(8,128)(2,1)S(1)}, u32[]{:S(2)}, u32[]{:S(2)}) collective-permute-start(bf16[1,784,128]{2,1,0:T(8,128)(2,1)S(1)} %collective-permute-done.10.refs_2_), channel_id=1, source_target_pairs={{0,16},{1,17},{2,18},{3,19},{4,20},{5,21},{6,22},{7,23},{8,24},{9,... | collective-permute-start | bytes 602120 | tf_op jit(solution)/shard_map/ppermute | solution.py:37
  71.2 0.0 collective-permute-done.9.refs_1_
  71.2 3.5 %collective-permute-done.11.refs_3_ = bf16[1,784,128]{2,1,0:T(8,128)(2,1)S(1)} collective-permute-done((bf16[1,784,128]{2,1,0:T(8,128)(2,1)S(1)}, bf16[1,784,128]{2,1,0:T(8,128)(2,1)S(1)}, u32[]{:S(2)}, u32[]{:S(2)}) %collective-permute-start.11) | collective-permute-done | bytes 200736 | tf_op jit(solution)/shard_map/ppermute | solution.py:37
  74.8 1.2 %pad_maximum_fusion.1 = bf16[6,784,128]{2,1,0:T(8,128)(2,1)} fusion(bf16[1,784,128]{2,1,0:T(8,128)(2,1)S(1)} %collective-permute-done.11.refs_3_, bf16[1,784,128]{2,1,0:T(8,128)(2,1)S(1)} %collective-permute-done.10.refs_2_, bf16[2,784,128]{2,1,0:T(8,128)(2,1)S(1)} %collective-permute-done.9.refs_1_, bf16[2,784,128]{2,1,0:T(8,128)(2,1)S(1)} %collective-permute-done.8.refs_0_), kind=kLoop, calls=%fused_computation.1 | loop fusion | flops 1806336 | bytes 2408448 | tf_op jit(solution)/shard_map/concatenate | solution.py:189
  76.0 6.5 %collective-permute-start.12 = (bf16[6,784,128]{2,1,0:T(8,128)(2,1)}, bf16[6,784,128]{2,1,0:T(8,128)(2,1)}, u32[]{:S(2)}, u32[]{:S(2)}) collective-permute-start(bf16[6,784,128]{2,1,0:T(8,128)(2,1)} %pad_maximum_fusion.1), channel_id=1, source_target_pairs={{0,1},{1,0},{2,3},{3,2},{4,5},{5,4},{6,7},{7,6},{8,9},{9,8},{10,11... | collective-permute-start | bytes 3612680 | tf_op jit(solution)/shard_map/ppermute | solution.py:37
  82.5 0.0 collective-permute-done.7.refs_6_
  82.5 0.0 all-to-all-done
  82.5 5.0 %shard_map.38.early_ref = f32[9,128,128]{2,1,0:T(8,128)} custom-call(bf16[64,128,128]{2,1,0:T(8,128)(2,1)S(1)} %bitcast.5, bf16[2,784,128]{2,1,0:T(8,128)(2,1)} %copy-done.5, bf16[2,784,128]{2,1,0:T(8,128)(2,1)} %copy-done.6, bf16[2,784,128]{2,1,0:T(8,128)(2,1)} %copy-done.2, bf16[2,784,128]{2,1,0:T(8,128)(2,1)} %copy-done.3, ...), custom_call_target="tpu_custom_call" | custom-call | tf_op jit(solution)/shard_map/pallas_call | solution.py:130
  87.5 0.0 collective-permute-done.12.refs_4_
  87.5 1.1 %copy-done = f32[9,128,128]{2,1,0:T(8,128)S(1)} copy-done((f32[9,128,128]{2,1,0:T(8,128)S(1)}, f32[9,128,128]{2,1,0:T(8,128)}, u32[]{:S(2)}) %copy-start) | copy-done | bytes 589848
  88.6 4.0 %shard_map.39 = f32[8,128,128]{2,1,0:T(8,128)} custom-call(f32[9,128,128]{2,1,0:T(8,128)S(1)} %copy-done, bf16[64,128,128]{2,1,0:T(8,128)(2,1)S(1)} %bitcast.6, bf16[2,784,128]{2,1,0:T(8,128)(2,1)S(1)} %collective-permute-done.8.refs_0_, bf16[2,784,128]{2,1,0:T(8,128)(2,1)S(1)} %collective-permute-done.9.refs_1_, ...), custom_call_target="tpu_custom_call" | custom-call | tf_op jit(solution)/shard_map/pallas_call | solution.py:130
  (11 shorter events, 0.1 us)
Async XLA Ops:
  2.4 13.6 %copy-start.8 = (s32[6]{0:T(128)S(1)}, s32[6]{0:T(128)}, u32[]{:S(2)}) copy-start(s32[6]{0:T(128)} %param.4) | copy-start | bytes 76
  2.4 13.7 %copy-start.7 = (bf16[6,128,128]{2,1,0:T(8,128)(2,1)S(1)}, bf16[6,128,128]{2,1,0:T(8,128)(2,1)}, u32[]{:S(2)}) copy-start(bf16[6,128,128]{2,1,0:T(8,128)(2,1)} %param.3) | copy-start | bytes 589828
  2.4 80.0 %all-to-all-start = ((bf16[16,512,128]{2,1,0:T(8,128)(2,1)}), bf16[16,512,128]{2,1,0:T(8,128)(2,1)S(1)}, u32[]{:S(2)}, u32[]{:S(2)}) async-start(bf16[16,512,128]{2,1,0:T(8,128)(2,1)} %shard_map.37), calls=%async_computation | async-start | bytes 4194304 | tf_op jit(solution)/shard_map/all_to_all | solution.py:173
  16.1 5.1 %collective-permute-start = (bf16[1,784,128]{2,1,0:T(8,128)(2,1)S(1)}, bf16[1,784,128]{2,1,0:T(8,128)(2,1)S(1)}, u32[]{:S(2)}, u32[]{:S(2)}) collective-permute-start(bf16[1,784,128]{2,1,0:T(8,128)(2,1)S(1)} %maximum_bitcast_fusion), channel_id=1, source_target_pairs={{0,1},{1,0},{2,3},{3,2},{4,5},{5,4},{6,7},{7,6},{8,9},{9,8},{10,11... | collective-permute-start | bytes 602120 | tf_op jit(solution)/shard_map/ppermute | solution.py:37
  19.0 13.6 %collective-permute-start.1 = (bf16[1,784,128]{2,1,0:T(8,128)(2,1)S(1)}, bf16[1,784,128]{2,1,0:T(8,128)(2,1)S(1)}, u32[]{:S(2)}, u32[]{:S(2)}) collective-permute-start(bf16[1,784,128]{2,1,0:T(8,128)(2,1)S(1)} %maximum_bitcast_fusion), channel_id=1, source_target_pairs={{0,16},{1,17},{2,18},{3,19},{4,20},{5,21},{6,22},{7,23},{8,24},{9,... | collective-permute-start | bytes 602120 | tf_op jit(solution)/shard_map/ppermute | solution.py:37
  21.3 39.8 %copy-start.5 = (bf16[2,784,128]{2,1,0:T(8,128)(2,1)}, bf16[2,784,128]{2,1,0:T(8,128)(2,1)S(1)}, u32[]{:S(2)}) copy-start(bf16[2,784,128]{2,1,0:T(8,128)(2,1)S(1)} %pad_maximum_fusion.2.refs_0_) | copy-start | bytes 1204228
  21.3 19.8 %collective-permute-start.3 = (bf16[2,784,128]{2,1,0:T(8,128)(2,1)S(1)}, bf16[2,784,128]{2,1,0:T(8,128)(2,1)S(1)}, u32[]{:S(2)}, u32[]{:S(2)}) collective-permute-start(bf16[2,784,128]{2,1,0:T(8,128)(2,1)S(1)} %pad_maximum_fusion.2.refs_0_), channel_id=1, source_target_pairs={{0,2},{1,15},{2,4},{3,1},{4,6},{5,3},{6,8},{7,5},{8,10},{9,7},{10,... | collective-permute-start | bytes 1204232 | tf_op jit(solution)/shard_map/ppermute | solution.py:37
  32.6 3.4 %collective-permute-start.2 = (bf16[1,784,128]{2,1,0:T(8,128)(2,1)S(1)}, bf16[1,784,128]{2,1,0:T(8,128)(2,1)S(1)}, u32[]{:S(2)}, u32[]{:S(2)}) collective-permute-start(bf16[1,784,128]{2,1,0:T(8,128)(2,1)S(1)} %collective-permute-done.1), channel_id=1, source_target_pairs={{0,1},{1,0},{2,3},{3,2},{4,5},{5,4},{6,7},{7,6},{8,9},{9,8},{10,11... | collective-permute-start | bytes 602120 | tf_op jit(solution)/shard_map/ppermute | solution.py:37
  36.0 25.1 %copy-start.6 = (bf16[2,784,128]{2,1,0:T(8,128)(2,1)}, bf16[2,784,128]{2,1,0:T(8,128)(2,1)S(1)}, u32[]{:S(2)}) copy-start(bf16[2,784,128]{2,1,0:T(8,128)(2,1)S(1)} %constant_dynamic-update-slice_fusion.refs_1_) | copy-start | bytes 1204228
  36.0 9.9 %collective-permute-start.4 = (bf16[2,784,128]{2,1,0:T(8,128)(2,1)S(1)}, bf16[2,784,128]{2,1,0:T(8,128)(2,1)S(1)}, u32[]{:S(2)}, u32[]{:S(2)}) collective-permute-start(bf16[2,784,128]{2,1,0:T(8,128)(2,1)S(1)} %constant_dynamic-update-slice_fusion.refs_1_), channel_id=1, source_target_pairs={{0,2},{1,15},{2,4},{3,1},{4,6},{5,3},{6,8},{7,5},{8,10},{9,7},{10,... | collective-permute-start | bytes 1204232 | tf_op jit(solution)/shard_map/ppermute | solution.py:37
  41.2 24.8 %copy-start.2 = (bf16[2,784,128]{2,1,0:T(8,128)(2,1)}, bf16[2,784,128]{2,1,0:T(8,128)(2,1)S(1)}, u32[]{:S(2)}) copy-start(bf16[2,784,128]{2,1,0:T(8,128)(2,1)S(1)} %collective-permute-done.3.refs_2_) | copy-start | bytes 1204228
  41.2 9.8 %collective-permute-start.5 = (bf16[2,784,128]{2,1,0:T(8,128)(2,1)S(1)}, bf16[2,784,128]{2,1,0:T(8,128)(2,1)S(1)}, u32[]{:S(2)}, u32[]{:S(2)}) collective-permute-start(bf16[2,784,128]{2,1,0:T(8,128)(2,1)S(1)} %collective-permute-done.3.refs_2_), channel_id=1, source_target_pairs={{0,2},{1,15},{2,4},{3,1},{4,6},{5,3},{6,8},{7,5},{8,10},{9,7},{10,... | collective-permute-start | bytes 1204232 | tf_op jit(solution)/shard_map/ppermute | solution.py:37
  45.9 20.0 %copy-start.3 = (bf16[2,784,128]{2,1,0:T(8,128)(2,1)}, bf16[2,784,128]{2,1,0:T(8,128)(2,1)S(1)}, u32[]{:S(2)}) copy-start(bf16[2,784,128]{2,1,0:T(8,128)(2,1)S(1)} %collective-permute-done.4.refs_3_) | copy-start | bytes 1204228
  45.9 9.8 %collective-permute-start.8 = (bf16[2,784,128]{2,1,0:T(8,128)(2,1)S(1)}, bf16[2,784,128]{2,1,0:T(8,128)(2,1)S(1)}, u32[]{:S(2)}, u32[]{:S(2)}) collective-permute-start(bf16[2,784,128]{2,1,0:T(8,128)(2,1)S(1)} %collective-permute-done.4.refs_3_), channel_id=1, source_target_pairs={{0,2},{1,15},{2,4},{3,1},{4,6},{5,3},{6,8},{7,5},{8,10},{9,7},{10,... | collective-permute-start | bytes 1204232 | tf_op jit(solution)/shard_map/ppermute | solution.py:37
  51.0 15.0 %copy-start.4 = (bf16[2,784,128]{2,1,0:T(8,128)(2,1)}, bf16[2,784,128]{2,1,0:T(8,128)(2,1)S(1)}, u32[]{:S(2)}) copy-start(bf16[2,784,128]{2,1,0:T(8,128)(2,1)S(1)} %collective-permute-done.5.refs_4_) | copy-start | bytes 1204228
  51.0 10.1 %collective-permute-start.6 = (bf16[2,784,128]{2,1,0:T(8,128)(2,1)S(1)}, bf16[2,784,128]{2,1,0:T(8,128)(2,1)S(1)}, u32[]{:S(2)}, u32[]{:S(2)}) collective-permute-start(bf16[2,784,128]{2,1,0:T(8,128)(2,1)S(1)} %collective-permute-done.5.refs_4_), channel_id=1, source_target_pairs={{0,2},{1,15},{2,4},{3,1},{4,6},{5,3},{6,8},{7,5},{8,10},{9,7},{10,... | collective-permute-start | bytes 1204232 | tf_op jit(solution)/shard_map/ppermute | solution.py:37
  55.7 15.5 %collective-permute-start.9 = (bf16[2,784,128]{2,1,0:T(8,128)(2,1)S(1)}, bf16[2,784,128]{2,1,0:T(8,128)(2,1)S(1)}, u32[]{:S(2)}, u32[]{:S(2)}) collective-permute-start(bf16[2,784,128]{2,1,0:T(8,128)(2,1)S(1)} %collective-permute-done.8.refs_0_), channel_id=1, source_target_pairs={{0,2},{1,15},{2,4},{3,1},{4,6},{5,3},{6,8},{7,5},{8,10},{9,7},{10,... | collective-permute-start | bytes 1204232 | tf_op jit(solution)/shard_map/ppermute | solution.py:37
  61.1 4.9 %copy-start.1 = (bf16[2,784,128]{2,1,0:T(8,128)(2,1)}, bf16[2,784,128]{2,1,0:T(8,128)(2,1)S(1)}, u32[]{:S(2)}) copy-start(bf16[2,784,128]{2,1,0:T(8,128)(2,1)S(1)} %collective-permute-done.6.refs_5_) | copy-start | bytes 1204228
  61.1 7.2 %collective-permute-start.10 = (bf16[1,784,128]{2,1,0:T(8,128)(2,1)S(1)}, bf16[1,784,128]{2,1,0:T(8,128)(2,1)S(1)}, u32[]{:S(2)}, u32[]{:S(2)}) collective-permute-start(bf16[1,784,128]{2,1,0:T(8,128)(2,1)S(1)} %slice.4), channel_id=1, source_target_pairs={{0,2},{1,15},{2,4},{3,1},{4,6},{5,3},{6,8},{7,5},{8,10},{9,7},{10,... | collective-permute-start | bytes 602120 | tf_op jit(solution)/shard_map/ppermute | solution.py:37
  65.9 16.5 %collective-permute-start.7 = (bf16[8,784,128]{2,1,0:T(8,128)(2,1)S(1)}, bf16[8,784,128]{2,1,0:T(8,128)(2,1)}, u32[]{:S(2)}, u32[]{:S(2)}) collective-permute-start(bf16[8,784,128]{2,1,0:T(8,128)(2,1)S(1)} %pad_maximum_fusion), channel_id=1, source_target_pairs={{0,1},{1,0},{2,3},{3,2},{4,5},{5,4},{6,7},{7,6},{8,9},{9,8},{10,11... | collective-permute-start | bytes 4816904 | tf_op jit(solution)/shard_map/ppermute | solution.py:37
  68.3 6.4 %collective-permute-start.11 = (bf16[1,784,128]{2,1,0:T(8,128)(2,1)S(1)}, bf16[1,784,128]{2,1,0:T(8,128)(2,1)S(1)}, u32[]{:S(2)}, u32[]{:S(2)}) collective-permute-start(bf16[1,784,128]{2,1,0:T(8,128)(2,1)S(1)} %collective-permute-done.10.refs_2_), channel_id=1, source_target_pairs={{0,16},{1,17},{2,18},{3,19},{4,20},{5,21},{6,22},{7,23},{8,24},{9,... | collective-permute-start | bytes 602120 | tf_op jit(solution)/shard_map/ppermute | solution.py:37
  76.0 11.5 %collective-permute-start.12 = (bf16[6,784,128]{2,1,0:T(8,128)(2,1)}, bf16[6,784,128]{2,1,0:T(8,128)(2,1)}, u32[]{:S(2)}, u32[]{:S(2)}) collective-permute-start(bf16[6,784,128]{2,1,0:T(8,128)(2,1)} %pad_maximum_fusion.1), channel_id=1, source_target_pairs={{0,1},{1,0},{2,3},{3,2},{4,5},{5,4},{6,7},{7,6},{8,9},{9,8},{10,11... | collective-permute-start | bytes 3612680 | tf_op jit(solution)/shard_map/ppermute | solution.py:37
  87.5 1.1 %copy-start = (f32[9,128,128]{2,1,0:T(8,128)S(1)}, f32[9,128,128]{2,1,0:T(8,128)}, u32[]{:S(2)}) copy-start(f32[9,128,128]{2,1,0:T(8,128)} %shard_map.38.early_ref) | copy-start | bytes 1769476
